TPU v7x, 512 devices: a whole 4x8x8 slice. The times are simulated.
512 devices in a mesh: dp: 32 (over y, x), tm: 16 (over z, core).
Axes of the slice: x: 4, y: 8, z: 8, core: 2. Of those that a mesh axis runs over, the one named last changes fastest.
Arguments:
- tokens: bfloat16 [32, 16, 256, 1024], P('dp', 'tm'), may hold values from -6 to 6
- gain: bfloat16 [1024], replicated, may hold values from 0.25 to 1.75
- w_qkv: bfloat16 [1024, 3072], P('dp'), may hold values from -0.1875 to 0.1875
- w_out: bfloat16 [1024, 1024], P('dp'), may hold values from -0.1875 to 0.1875
- w_pair: float32 [2, 1024, 32], replicated, may hold values from -3 to 3
- codebook: float32 [8, 32], replicated, may hold values from -5 to 5
- codes: int32 [32, 16, 1], P('dp', 'tm'), may hold values from 0 to 7
Outputs:
- grad_tokens: bfloat16 [32, 16, 256, 1024], P('dp', 'tm')
- grad_pair: float32 [2, 1024, 32], replicated
- codebook_step: float32 [8, 32], replicated
Inputs may be any that keep to these rules, and one draw needn't show every extreme that they name: Every one of the 8 codes is assigned to some clip frame.
All inputs are finite; a program needn't handle non-finite values.
Results may differ from a plain program's by a relative error of at most 0.014.
Values may be sent and summed in bfloat16 or wider, within the bound.
No kernel may reach another device: no remote copies, remote signals or barrier semaphores. Data moves between devices by JAX's collectives and lax.ppermute only.
A program may use at most 64 MiB of HBM per device.

v0:
```python
import jax
import jax.numpy as jnp
from jax import lax
from jax.sharding import Mesh
from jax.sharding import PartitionSpec as P

D = 1024
HEAD_DIM = 64
CODES = 8
PATCHES = 256
DP = ("dp_0", "dp_1")
TM = ("tm_0", "tm_1")


EPS = 1e-06
BETA = 0.25


def in_one_piece(arrays, axis, dim, along):
    both = jnp.concatenate(arrays, axis=along)
    result, at, outs = (lax.all_gather(both, axis, axis=dim, tiled=True), 0, [])
    for a in arrays:
        outs.append(lax.slice_in_dim(result, at, at + a.shape[along], axis=along))
        at += a.shape[along]
    return tuple(outs)


def in_blocks(value, dim, count):
    before, after = (value.shape[:dim], value.shape[dim + 1 :])
    return jnp.moveaxis(value.reshape(*before, count, -1, *after), dim, 0)


def sent_and_summed(value, axis, dim):
    count = lax.axis_size(axis)
    pieces = lax.all_to_all(in_blocks(value, dim, count), axis, 0, 0, tiled=True)
    return jnp.sum(pieces.astype(jnp.float32), axis=0)


def passed_along(value, axis, by):
    count = lax.axis_size(axis)
    pairs = [(i, i + by) for i in range(count) if 0 <= i + by < count]
    return lax.ppermute(value, axis, pairs)


def sent_and_summed_2(value, axis, dim):
    pieces = in_blocks(value, dim, lax.axis_size(axis))
    arrived = lax.all_to_all(pieces, axis, split_axis=0, concat_axis=0, tiled=True)
    return arrived.sum(axis=0)


def sum_in_two_steps(value, axes, dim):
    far, near = axes
    own = sent_and_summed_2(in_blocks(value, dim, lax.axis_size(far)), near, dim + 1)
    return jnp.sum(lax.all_to_all(own, far, 0, 0, tiled=True), axis=0)


def padded_to(lines, count):
    spare = -lines.shape[0] % count
    if not spare:
        return lines
    return jnp.concatenate([lines, jnp.zeros((spare, *lines.shape[1:]), lines.dtype)])


def from_everyone(value, axis):
    count = lax.axis_size(axis)
    return lax.all_to_all(
        jnp.broadcast_to(value[None], (count, *value.shape)), axis, 0, 0, tiled=True
    )


def joined_along(pieces, dim):
    dims = list(pieces.shape[1:])
    dims[dim] *= pieces.shape[0]
    return jnp.moveaxis(pieces, 0, dim).reshape(dims)


def gather_axes(value, axes, dim):
    far, near = axes
    first = from_everyone(value, far)
    pieces = jnp.swapaxes(from_everyone(first, near), 0, 1)
    return joined_along(pieces.reshape(-1, *value.shape), dim)


def total_of(value, axes):
    own = sum_in_two_steps(
        padded_to(value, lax.axis_size(axes[0]) * lax.axis_size(axes[1])), axes, 0
    )
    whole = gather_axes(own, axes, 0)
    return whole[: len(value)].reshape(value.shape)


def together(arrays, axis):
    ends = [0]
    for a in arrays:
        ends.append(ends[-1] + a.size)
    so_far = total_of(jnp.concatenate([a.ravel() for a in arrays]), axis)
    return tuple((so_far[b:e].reshape(a.shape) for a, b, e in zip(arrays, ends, ends[1:])))


def normalize(xf, gain):
    scale = lax.rsqrt(jnp.mean(xf * xf, axis=-1, keepdims=True) + EPS)
    return (xf * scale * gain.astype(jnp.float32)).astype(jnp.bfloat16)


def project(normed, weight):
    shape = normed.shape
    flat = jnp.dot(normed.reshape(-1, shape[-1]), weight, preferred_element_type=jnp.float32)
    return flat.astype(jnp.bfloat16).reshape(shape[:-1] + (3, shape[-1]))


def attend(qkv):
    clips, frames, patches, _, width = qkv.shape
    local_heads = width // HEAD_DIM
    parts = qkv.reshape(clips, frames, patches, 3, local_heads, HEAD_DIM)
    query = parts[:, :, :, 0].astype(jnp.float32)
    keys = parts[:, :, :, 1].astype(jnp.float32)
    values = parts[:, :, :, 2].astype(jnp.float32)
    scores = jnp.einsum("cfphd,cgphd->cphfg", query, keys) * HEAD_DIM ** (-0.5)
    causal = jnp.arange(frames)[:, None] >= jnp.arange(frames)[None, :]
    scores = jnp.where(causal, scores, -1e30)
    weights = jax.nn.softmax(scores, axis=-1).astype(jnp.bfloat16)
    mixed = jnp.einsum("cphfg,cgphd->cfphd", weights.astype(jnp.float32), values)
    return mixed.reshape(clips, frames, patches, width).astype(jnp.bfloat16)


def local(tokens, gain, w_qkv, w_out, w_pair, codebook, codes):
    xf = tokens.astype(jnp.float32)
    full_qkv, full_out = in_one_piece((w_qkv, w_out), DP, 0, 1)
    normed, norm_back = jax.vjp(lambda value: normalize(value, gain), xf)
    regrouped = lax.all_to_all(normed, TM, split_axis=2, concat_axis=1, tiled=True)
    qkv, qkv_back = jax.vjp(lambda value: project(value, full_qkv), regrouped)
    attended, attend_back = jax.vjp(attend, qkv)
    width = attended.shape[3]
    lead = attended.shape[:3]
    moved = jnp.dot(attended.reshape(-1, width), full_out, preferred_element_type=jnp.float32)
    partial_sum = jnp.sum(moved.reshape(lead + (D,)), axis=2)
    summed = sent_and_summed(partial_sum.astype(jnp.bfloat16), TM, 1)
    pooled = jnp.mean(xf, axis=2) + summed / PATCHES
    following = passed_along(pooled, TM, -1)
    flat_now = pooled.reshape(-1, D)
    flat_next = following.reshape(-1, D)
    highest = lax.Precision.HIGHEST
    action = jnp.dot(flat_now, w_pair[0], precision=highest) + jnp.dot(
        flat_next, w_pair[1], precision=highest
    )
    onehot = (codes.reshape(-1)[:, None] == jnp.arange(CODES)[None, :]).astype(jnp.float32)
    quantized = jnp.dot(onehot, codebook, precision=highest)
    diff = action - quantized
    d_action = 2.0 * BETA * diff
    d_quant = -2.0 * diff
    pair_part = jnp.stack(
        [
            jnp.dot(flat_now.T, d_action, precision=highest),
            jnp.dot(flat_next.T, d_action, precision=highest),
        ]
    )
    code_part = jnp.dot(onehot.T, d_quant, precision=highest)
    count_part = jnp.sum(onehot, axis=0)
    grad_pair, code_total, count = together(
        (pair_part, code_part, count_part), ("dp_0", ("dp_1", "tm_0", "tm_1"))
    )
    codebook_step = code_total / count[:, None]
    d_own = jnp.dot(d_action, w_pair[0].T, precision=highest).reshape(pooled.shape)
    d_next = jnp.dot(d_action, w_pair[1].T, precision=highest).reshape(pooled.shape)
    carried = passed_along(d_next, TM, 1)
    d_pooled = (d_own + carried) * PATCHES
    d_mean = d_pooled / PATCHES
    d_resid = jnp.broadcast_to(d_mean[:, :, None, :], xf.shape)
    every_mean = lax.all_gather(d_mean, TM, axis=1, tiled=True)
    d_rows = jnp.dot(every_mean.reshape(-1, D), full_out.astype(jnp.float32).T, precision=highest)
    d_rows = d_rows.astype(jnp.bfloat16).reshape(attended.shape[:2] + (1, width))
    d_attended = jnp.broadcast_to(d_rows, attended.shape)
    (d_qkv,) = attend_back(d_attended)
    (d_regrouped,) = qkv_back(d_qkv)
    d_normed = lax.all_to_all(d_regrouped, TM, split_axis=1, concat_axis=2, tiled=True)
    (d_through,) = norm_back(d_normed)
    grad_tokens = (d_resid + d_through).astype(jnp.bfloat16)
    return (grad_tokens, grad_pair, codebook_step)


def solution(mesh):
    torus = Mesh(mesh.devices.reshape(8, 4, 8, 2), ("dp_0", "dp_1", "tm_0", "tm_1"))
    return jax.shard_map(
        local,
        mesh=torus,
        in_specs=(P(DP, TM, None, None), P(), P(DP, None), P(DP, None), P(), P(), P(DP, TM, None)),
        out_specs=(P(DP, TM, None, None), P(), P()),
        check_vma=False,
    )
```

profile of v0, /device:TPU:1, one launch (start us, length us, event | category | flops | bytes accessed | tf_op | source)
XLA Modules:
  0.0 297.9 jit_solution(1898592563421478419)
XLA Ops:
  7.2 1.7 pad_maximum_fusion
  8.9 0.7 convert_element_type.127
  9.6 1.3 convert_reduce_fusion
  11.5 1.2 fusion.52
  12.7 0.8 copy.94
  14.1 3.9 %reduce.13 = bf16[256,1024]{1,0:T(8,128)(2,1)S(1)} reduce(bf16[256,1,1,1024]{3,2,1,0:T(2,128)(2,1)S(1)} %bitcast.157, bf16[]{:T(256)} %broadcast.201), dimensions={1,2}, to_apply=%bitcast.152.reduce_sub_computation | reduce | bytes 1048578
  18.0 1.2 reshape.405
  19.2 11.8 %all-to-all-start = ((bf16[16,2,8192]{2,1,0:T(2,128)(2,1)}), bf16[16,2,8192]{2,1,0:T(2,128)(2,1)S(1)}, u32[]{:S(2)}, u32[]{:S(2)}) async-start(bf16[16,2,8192]{2,1,0:T(2,128)(2,1)} %reshape.405), calls=%async_computation | async-start | bytes 1048576 | tf_op jit(solution)/shard_map/all_to_all | solution.py:130
  32.9 15.5 %all-to-all-done = bf16[16,2,8192]{2,1,0:T(2,128)(2,1)S(1)} async-done(((bf16[16,2,8192]{2,1,0:T(2,128)(2,1)}), bf16[16,2,8192]{2,1,0:T(2,128)(2,1)S(1)}, u32[]{:S(2)}, u32[]{:S(2)}) %all-to-all-start) | async-done | bytes 524320 | tf_op jit(solution)/shard_map/all_to_all | solution.py:130
  48.9 71.4 %all-gather.2.cloned.1.call-done = bf16[1024,4096]{1,0:T(8,128)(2,1)} async-done(((bf16[32,4096]{1,0:T(8,128)(2,1)}), bf16[1024,4096]{1,0:T(8,128)(2,1)}) %all-gather.2.cloned.1.call-update) | async-done | bytes 8388624 | tf_op jit(solution)/shard_map/all_gather | solution.py:21
  120.2 5.8 %fusion.5 = bf16[256,3072]{1,0:T(8,128)(2,1)} fusion(bf16[1024,4096]{1,0:T(8,128)(2,1)} %all-gather.2.cloned.1.call-done, bf16[1,1,256,1024]{3,1,0,2:T(2,128)(2,1)S(1)} %bitcast.160), kind=kOutput, calls=%fused_computation.5 | convolution fusion | flops 1611399168 | bytes 8388608 | tf_op jit(solution)/shard_map/jvp()/dot_general | solution.py:107
  126.0 3.6 %reshape.379 = bf16[1,16,16,3,16,64]{5,4,3,2,1,0:T(8,128)(2,1)S(1)} reshape(bf16[256,3072]{1,0:T(8,128)(2,1)} %fusion.5) | data formatting | bytes 3145728 | tf_op jit(solution)/shard_map/jvp()/reshape;jvp()/reshape | solution.py:114
  129.7 2.2 fusion.85
  131.9 3.6 %fusion.86 = (f32[16,16,16]{2,1,0:T(8,128)S(1)}, f32[16,16,16,16]{2,3,1,0:T(8,128)S(1)}) fusion(pred[16,16]{0,1:T(8,128)(4,1)S(1)} %iota_compare_fusion, bf16[1,16,16,1,16,64]{5,4,3,2,1,0:T(8,128)(2,1)} %get-tuple-element.15, bf16[1,16,16,1,16,64]{5,4,3,2,1,0:T(8,128)(2,1)} %get-tuple-element.16), kind=kOutput, calls=%fused_computation.111 | convolution fusion | flops 8650767 | bytes 1327360 | tf_op jit(solution)/shard_map/jvp()/sub | solution.py:121
  135.5 1.3 copy-done.3
  136.9 0.9 fusion.30
  138.1 0.7 convert_element_type.134
  138.8 2.4 fusion.39
  142.5 8.5 %all-to-all-start.1 = ((bf16[16,2,512]{2,1,0:T(2,128)(2,1)}), bf16[16,2,512]{2,1,0:T(2,128)(2,1)S(1)}, u32[]{:S(2)}, u32[]{:S(2)}) async-start(bf16[16,2,512]{2,1,0:T(2,128)(2,1)} %reshape.407), calls=%async_computation.1 | async-start | bytes 65536 | tf_op jit(solution)/shard_map/all_to_all | solution.py:35
  151.0 7.4 %all-to-all-done.1 = bf16[16,2,512]{2,1,0:T(2,128)(2,1)S(1)} async-done(((bf16[16,2,512]{2,1,0:T(2,128)(2,1)}), bf16[16,2,512]{2,1,0:T(2,128)(2,1)S(1)}, u32[]{:S(2)}, u32[]{:S(2)}) %all-to-all-start.1) | async-done | bytes 32800 | tf_op jit(solution)/shard_map/all_to_all | solution.py:35
  158.5 2.3 collective-permute-start
  161.0 2.4 collective-permute-done
  163.7 0.8 convolution_bitcast_fusion
  164.4 1.9 collective-permute-start.1
  168.1 1.1 copy.52
  169.2 6.0 %all-to-all-start.3 = ((f32[64,8,129]{2,1,0:T(8,128)}), f32[64,8,129]{2,1,0:T(8,128)}, u32[]{:S(2)}, u32[]{:S(2)}) async-start(f32[64,8,129]{2,1,0:T(8,128)} %copy.52), calls=%async_computation.3 | async-start | bytes 1048576 | tf_op jit(solution)/shard_map/all_to_all | solution.py:47
  175.2 0.9 fusion.45
  176.1 24.2 %all_gather.7 = f32[1,16,1024]{2,0,1:T(1,128)S(1)} all-gather(f32[1,1,1024]{2,0,1:T(1,128)S(1)} %fusion.45), channel_id=1, replica_groups=mesh['dp_0'=8,'dp_1'=4,'tm_0'=8,'tm_1'=2] {'tm_0','tm_1'}, dimensions={1}, use_global_device_ids=true | all-gather | bytes 69632 | tf_op jit(solution)/shard_map/all_gather | solution.py:169
  200.3 3.3 %fusion.42 = bf16[16,1024]{1,0:T(8,128)(2,1)S(1)} fusion(bf16[1024,4096]{1,0:T(8,128)(2,1)} %all-gather.2.cloned.1.call-done, f32[1,16,1024]{2,0,1:T(1,128)S(1)} %all_gather.7), kind=kOutput, calls=%fused_computation.45 | convolution fusion | flops 201342976 | bytes 2195456 | tf_op jit(solution)/shard_map/dot_general | solution.py:170
  203.7 2.7 fusion.33
  206.4 1.1 fusion.13
  207.7 2.1 fusion.32
  209.8 2.0 fusion.31
  211.8 1.1 reduce_sum.100
  213.5 4.2 %all-to-all-start.4 = ((f32[8,1,129]{2,1,0:T(1,128)}), f32[8,1,129]{2,1,0:T(1,128)S(1)}, u32[]{:S(2)}, u32[]{:S(2)}) async-start(f32[8,1,129]{2,1,0:T(1,128)} %all_to_all.37), calls=%async_computation.4 | async-start | bytes 16384 | tf_op jit(solution)/shard_map/all_to_all | solution.py:54
  217.7 2.4 pad_add_fusion
  220.1 0.8 copy.48
  220.9 3.3 %reshape.388 = bf16[256,3072]{1,0:T(8,128)(2,1)} reshape(bf16[1,16,16,3,16,64]{5,4,3,2,1,0:T(8,128)(2,1)S(1)} %copy.48) | data formatting | bytes 3145728 | tf_op jit(solution)/shard_map/transpose(jvp())/reshape;transpose(jvp())/reshape | solution.py:108
  224.9 6.5 %all-to-all-start.5 = ((f32[8,1,129]{2,1,0:T(1,128)}), f32[8,1,129]{2,1,0:T(1,128)S(1)}, u32[]{:S(2)}, u32[]{:S(2)}) async-start(f32[8,1,129]{2,1,0:T(1,128)} %broadcast_in_dim.88), calls=%async_computation.5 | async-start | bytes 16384 | tf_op jit(solution)/shard_map/all_to_all | solution.py:66
  231.4 5.9 %fusion.36 = bf16[256,1024]{1,0:T(8,128)(2,1)} fusion(bf16[256,3072]{1,0:T(8,128)(2,1)} %reshape.388, bf16[1024,4096]{1,0:T(8,128)(2,1)} %all-gather.2.cloned.1.call-done), kind=kOutput, calls=%fused_computation.43 | convolution fusion | flops 1610874880 | bytes 8388608 | tf_op jit(solution)/shard_map/transpose(jvp())/dot_general | solution.py:107
  237.3 0.7 all-to-all-done.5
  238.0 8.2 %all-to-all-start.2 = ((bf16[1,16,16,1024]{3,2,0,1:T(8,128)(2,1)}), bf16[1,16,16,1024]{3,2,0,1:T(8,128)(2,1)S(1)}, u32[]{:S(2)}, u32[]{:S(2)}) async-start(bf16[1,16,16,1024]{3,2,0,1:T(8,128)(2,1)} %bitcast.38), calls=%async_computation.2 | async-start | bytes 1048576 | tf_op jit(solution)/shard_map/all_to_all | solution.py:175
  246.3 17.3 %all-to-all-done.2 = bf16[1,16,16,1024]{3,2,0,1:T(8,128)(2,1)S(1)} async-done(((bf16[1,16,16,1024]{3,2,0,1:T(8,128)(2,1)}), bf16[1,16,16,1024]{3,2,0,1:T(8,128)(2,1)S(1)}, u32[]{:S(2)}, u32[]{:S(2)}) %all-to-all-start.2) | async-done | bytes 524320 | tf_op jit(solution)/shard_map/all_to_all | solution.py:175
  263.6 0.8 broadcast_in_dim.90
  264.4 6.1 %all-to-all-start.6 = ((f32[64,8,129]{2,1,0:T(8,128)}), f32[64,8,129]{2,1,0:T(8,128)S(1)}, u32[]{:S(2)}, u32[]{:S(2)}) async-start(f32[64,8,129]{2,1,0:T(8,128)} %broadcast_in_dim.90), calls=%async_computation.6 | async-start | bytes 1048576 | tf_op jit(solution)/shard_map/all_to_all | solution.py:66
  270.8 1.1 fusion.49
  271.9 15.9 %all-to-all-done.6 = f32[64,8,129]{2,1,0:T(8,128)S(1)} async-done(((f32[64,8,129]{2,1,0:T(8,128)}), f32[64,8,129]{2,1,0:T(8,128)S(1)}, u32[]{:S(2)}, u32[]{:S(2)}) %all-to-all-start.6) | async-done | bytes 264224 | tf_op jit(solution)/shard_map/all_to_all | solution.py:66
  289.3 1.0 copy.55
  (82 shorter events, 10.7 us)
Async XLA Ops:
  7.2 25.1 %copy-start = (f32[8,32]{1,0:T(8,128)S(1)}, f32[8,32]{1,0:T(8,128)}, u32[]{:S(2)}) copy-start(f32[8,32]{1,0:T(8,128)} %param.12) | copy-start | bytes 3076
  7.2 113.1 %all-gather.2.cloned.1.call-start = ((), (), s32[]{:S(2)}) async-start(), calls=%async_computation.7 | async-start | bytes 8650752 | tf_op jit(solution)/shard_map/all_gather | solution.py:21
  10.9 0.6 copy-start.12
  19.2 29.2 %all-to-all-start = ((bf16[16,2,8192]{2,1,0:T(2,128)(2,1)}), bf16[16,2,8192]{2,1,0:T(2,128)(2,1)S(1)}, u32[]{:S(2)}, u32[]{:S(2)}) async-start(bf16[16,2,8192]{2,1,0:T(2,128)(2,1)} %reshape.405), calls=%async_computation | async-start | bytes 1048576 | tf_op jit(solution)/shard_map/all_to_all | solution.py:130
  32.2 99.7 %copy-start.17 = (pred[16,16]{0,1:T(8,128)(4,1)}, pred[16,16]{0,1:T(8,128)(4,1)S(1)}, u32[]{:S(2)}) copy-start(pred[16,16]{0,1:T(8,128)(4,1)S(1)} %iota_compare_fusion) | copy-start | bytes 772
  131.9 5.0 %copy-start.2 = (bf16[1,16,16,1,16,64]{5,4,3,2,1,0:T(8,128)(2,1)S(1)}, bf16[1,16,16,1,16,64]{5,4,3,2,1,0:T(8,128)(2,1)}, u32[]{:S(2)}) copy-start(bf16[1,16,16,1,16,64]{5,4,3,2,1,0:T(8,128)(2,1)} %get-tuple-element.14) | copy-start | bytes 1572868
  135.5 1.4 copy-start.3
  135.5 2.2 copy-start.9
  138.8 12.2 %copy-start.10 = (f32[16,16,16]{2,1,0:T(8,128)S(1)}, f32[16,16,16]{2,1,0:T(8,128)}, u32[]{:S(2)}) copy-start(f32[16,16,16]{2,1,0:T(8,128)} %copy-done.9) | copy-start | bytes 49156
  138.8 22.0 %copy-start.5 = (f32[2,1024,32]{1,2,0:T(8,128)S(1)}, f32[2,1024,32]{1,2,0:T(8,128)}, u32[]{:S(2)}) copy-start(f32[2,1024,32]{1,2,0:T(8,128)} %param.11) | copy-start | bytes 786436
  138.8 24.6 %copy-start.16 = (f32[32]{0:T(128)S(1)}, f32[32]{0:T(128)}, u32[]{:S(2)}) copy-start(f32[32]{0:T(128)} %convolution_bitcast_fusion.2) | copy-start | bytes 388
  138.8 27.7 %copy-start.15 = (f32[8]{0:T(128)S(1)}, f32[8]{0:T(128)}, u32[]{:S(2)}) copy-start(f32[8]{0:T(128)} %compare_convert_fusion) | copy-start | bytes 100
  142.5 15.9 %all-to-all-start.1 = ((bf16[16,2,512]{2,1,0:T(2,128)(2,1)}), bf16[16,2,512]{2,1,0:T(2,128)(2,1)S(1)}, u32[]{:S(2)}, u32[]{:S(2)}) async-start(bf16[16,2,512]{2,1,0:T(2,128)(2,1)} %reshape.407), calls=%async_computation.1 | async-start | bytes 65536 | tf_op jit(solution)/shard_map/all_to_all | solution.py:35
  158.5 4.9 %collective-permute-start = (f32[1,1,1024]{2,1,0:T(1,128)S(1)}, f32[1,1,1024]{2,1,0:T(1,128)S(1)}, u32[]{:S(2)}, u32[]{:S(2)}) collective-permute-start(f32[1,1,1024]{2,1,0:T(1,128)S(1)} %bitcast.162), channel_id=1, source_target_pairs={{1,0},{2,1},{3,2},{4,3},{5,4},{6,5},{7,6},{8,7},{9,8},{10,9},{11,1... | collective-permute-start | bytes 12296 | tf_op jit(solution)/shard_map/ppermute | solution.py:42
  163.6 4.4 %copy-start.14 = (f32[32]{0:T(128)}, f32[32]{0:T(128)S(1)}, u32[]{:S(2)}) copy-start(f32[32]{0:T(128)S(1)} %get-tuple-element.25) | copy-start | bytes 388
  164.4 10.8 %collective-permute-start.1 = (f32[1,1,1024]{2,0,1:T(1,128)}, f32[1,1,1024]{2,0,1:T(1,128)}, u32[]{:S(2)}, u32[]{:S(2)}) collective-permute-start(f32[1,1,1024]{2,0,1:T(1,128)} %convolution_bitcast_fusion), channel_id=1, source_target_pairs={{0,1},{1,2},{2,3},{3,4},{4,5},{5,6},{6,7},{7,8},{8,9},{9,10},{10,1... | collective-permute-start | bytes 12296 | tf_op jit(solution)/shard_map/ppermute | solution.py:42
  169.2 34.5 %copy-start.4 = (f32[16,16,16,16]{2,3,1,0:T(8,128)S(1)}, f32[16,16,16,16]{2,3,1,0:T(8,128)}, u32[]{:S(2)}) copy-start(f32[16,16,16,16]{2,3,1,0:T(8,128)} %copy-done.3) | copy-start | bytes 786436
  169.2 42.6 %all-to-all-start.3 = ((f32[64,8,129]{2,1,0:T(8,128)}), f32[64,8,129]{2,1,0:T(8,128)}, u32[]{:S(2)}, u32[]{:S(2)}) async-start(f32[64,8,129]{2,1,0:T(8,128)} %copy.52), calls=%async_computation.3 | async-start | bytes 1048576 | tf_op jit(solution)/shard_map/all_to_all | solution.py:47
  206.4 1.2 copy-start.7
  206.4 1.2 copy-start.11
  206.4 1.2 copy-start.18
  207.7 2.1 copy-start.6
  209.8 8.0 %copy-start.8 = (bf16[1,16,16,1,16,64]{5,1,4,2,3,0:T(8,128)(2,1)S(1)}, bf16[1,16,16,1,16,64]{5,1,4,2,3,0:T(8,128)(2,1)}, u32[]{:S(2)}) copy-start(bf16[1,16,16,1,16,64]{5,1,4,2,3,0:T(8,128)(2,1)} %fusion.33) | copy-start | bytes 1572868
  213.5 10.8 %all-to-all-start.4 = ((f32[8,1,129]{2,1,0:T(1,128)}), f32[8,1,129]{2,1,0:T(1,128)S(1)}, u32[]{:S(2)}, u32[]{:S(2)}) async-start(f32[8,1,129]{2,1,0:T(1,128)} %all_to_all.37), calls=%async_computation.4 | async-start | bytes 16384 | tf_op jit(solution)/shard_map/all_to_all | solution.py:54
  224.9 13.1 %all-to-all-start.5 = ((f32[8,1,129]{2,1,0:T(1,128)}), f32[8,1,129]{2,1,0:T(1,128)S(1)}, u32[]{:S(2)}, u32[]{:S(2)}) async-start(f32[8,1,129]{2,1,0:T(1,128)} %broadcast_in_dim.88), calls=%async_computation.5 | async-start | bytes 16384 | tf_op jit(solution)/shard_map/all_to_all | solution.py:66
  237.3 33.2 %copy-start.1 = (bf16[1,1,256,1024]{3,2,1,0:T(8,128)(2,1)S(1)}, bf16[1,1,256,1024]{3,2,1,0:T(8,128)(2,1)}, u32[]{:S(2)}) copy-start(bf16[1,1,256,1024]{3,2,1,0:T(8,128)(2,1)} %param.7) | copy-start | bytes 1572868
  237.3 33.4 %copy-start.13 = (f32[256]{0:T(256)S(1)}, f32[256]{0:T(256)}, u32[]{:S(2)}) copy-start(f32[256]{0:T(256)} %copy-done.12) | copy-start | bytes 3076
  238.0 25.6 %all-to-all-start.2 = ((bf16[1,16,16,1024]{3,2,0,1:T(8,128)(2,1)}), bf16[1,16,16,1024]{3,2,0,1:T(8,128)(2,1)S(1)}, u32[]{:S(2)}, u32[]{:S(2)}) async-start(bf16[1,16,16,1024]{3,2,0,1:T(8,128)(2,1)} %bitcast.38), calls=%async_computation.2 | async-start | bytes 1048576 | tf_op jit(solution)/shard_map/all_to_all | solution.py:175
  264.4 23.4 %all-to-all-start.6 = ((f32[64,8,129]{2,1,0:T(8,128)}), f32[64,8,129]{2,1,0:T(8,128)S(1)}, u32[]{:S(2)}, u32[]{:S(2)}) async-start(f32[64,8,129]{2,1,0:T(8,128)} %broadcast_in_dim.90), calls=%async_computation.6 | async-start | bytes 1048576 | tf_op jit(solution)/shard_map/all_to_all | solution.py:66
Sparse Core Ops, SparseCore 0:
  11.8 108.4 all-gather.1
where the time goes:
time: 299 us; the launch traced here: 298 us
  waiting for transfers between devices  131 us (44%)
  starting transfers between devices  55.6 us (19%)
  matrix products  32.4 us (11%)
  blocking collectives  24.2 us (8%)
  local copies, waits for them, and re-layouts  24 us (8%)
  other arithmetic  15.9 us (5%)
  between operations  15.1 us (5%)
    all_gather x1, waiting for transfers between devices, in_one_piece(): result, at, outs = (lax.all_gather(both, axis, axis=dim, tiled=True), 0, [])  71.4 us
    all_gather x1, blocking collectives, local(): every_mean = lax.all_gather(d_mean, TM, axis=1, tiled=True)  24.2 us
    all_to_all x1, waiting for transfers between devices, local(): lax.all_to_all(d_regrouped, TM, split_axis=1, concat_axis=2, tiled=True)  17.3 us
    all_to_all x2, waiting for transfers between devices, from_everyone(): lax.all_to_all(jnp.broadcast_to(value[None], (count, *value.shape)), axis...  16.6 us
    all_to_all x1, waiting for transfers between devices, local(): lax.all_to_all(normed, TM, split_axis=2, concat_axis=1, tiled=True)  15.5 us
    all_to_all x2, starting transfers between devices, from_everyone(): lax.all_to_all(jnp.broadcast_to(value[None], (count, *value.shape)), axis...  12.6 us
    all_to_all x1, starting transfers between devices, local(): lax.all_to_all(normed, TM, split_axis=2, concat_axis=1, tiled=True)  11.8 us
    dot_general x2, matrix products, project(): jnp.dot(normed.reshape(-1, shape[-1]), weight, preferred_element_type=jnp...  11.7 us
  transfers between devices with their start and end apart: 10, of which 8 were waited for; matrix products, arithmetic and copies ran while one was open for 13% of the time, Pallas kernels for 0%

commit v1 on v0

v1 whole, which is shorter than its diff:
```python
import jax
import jax.numpy as jnp
from jax import lax
from jax.experimental import pallas as pl
from jax.experimental.pallas import tpu as pltpu
from jax.sharding import Mesh
from jax.sharding import PartitionSpec as P

D = 1024
HEAD_DIM = 64
LATENT = 32
CODES = 8
PATCHES = 256
FRAMES = 16
EPS = 1e-06
BETA = 0.25
DP = ("dp_0", "dp_1")
TM = ("tm_0", "tm_1")
HALF = 512
EXTRA = 256
GRADS = 512
PIECES = 5
BF = jnp.bfloat16
F32 = jnp.float32
HIGHEST = lax.Precision.HIGHEST


def params(mebibytes):
    return pltpu.CompilerParams(vmem_limit_bytes=mebibytes * 1024 * 1024)


SMEM = pl.BlockSpec(memory_space=pltpu.SMEM)


def nn(a, b, precision=None):
    return lax.dot_general(
        a, b, (((1,), (0,)), ((), ())), precision=precision, preferred_element_type=F32
    )


def nt(a, b, precision=None):
    return lax.dot_general(
        a, b, (((1,), (1,)), ((), ())), precision=precision, preferred_element_type=F32
    )


def tn(a, b, precision=None):
    return lax.dot_general(
        a, b, (((0,), (0,)), ((), ())), precision=precision, preferred_element_type=F32
    )


def two_terms(value):
    high = value.astype(BF)
    return high, (value - high.astype(F32)).astype(BF)


def iota(shape, dim):
    return lax.broadcasted_iota(jnp.int32, shape, dim)


def turned(value, shift):
    width = value.shape[-1]
    tiles = [pltpu.roll(value[:, j : j + 128], shift, 1) for j in range(0, width, 128)]
    return jnp.concatenate(tiles, axis=1)


def norm_kernel(code_ref, turn_ref, tokens_ref, gain_ref, normed_ref, extra_ref):
    xf = tokens_ref[...].astype(F32)
    scale = lax.rsqrt(jnp.mean(xf * xf, axis=-1, keepdims=True) + EPS)
    normed = xf * scale * gain_ref[...].astype(F32)
    normed_ref[...] = turned(normed, (128 - turn_ref[0]) % 128).astype(BF)
    mean = jnp.mean(xf, axis=0, keepdims=True)
    rows = jnp.concatenate([mean[:, j * 128 : (j + 1) * 128] for j in range(8)], axis=0)
    high = rows.astype(BF).astype(F32)
    mid = (rows - high).astype(BF).astype(F32)
    low = rows - high - mid
    code = jnp.full((8, 128), code_ref[0], jnp.int32).astype(F32)
    extra_ref[:, :128] = jnp.concatenate([high, mid], axis=0).astype(BF)
    extra_ref[:, 128:] = jnp.concatenate([low, code], axis=0).astype(BF)


def gathered(refs):
    own, after, first, second, before = refs
    half = first.shape[0]
    rows = []
    for far in range(2 * half):
        across = first[far] if far < half else second[far - half]
        rows += [own[far], after[far], across, before[far]]
    return jnp.concatenate(rows, axis=0)


def grouped_rows(value):
    value = value.reshape(FRAMES, 2, 8, value.shape[-1])
    return jnp.concatenate([value[:, g].reshape(128, -1) for g in range(2)], axis=0)


def causal_same_patch():
    row, col = (iota((128, 128), 0), iota((128, 128), 1))
    return (row % 8 == col % 8) & (col // 8 <= row // 8)


def forward_heads(x_ref, weight_refs, qkv_ref, prob_ref):
    x = x_ref[...].reshape(256, D)
    for part in range(3):
        weight = gathered(weight_refs[part * PIECES : (part + 1) * PIECES])
        qkv_ref[part] = grouped_rows(nn(x, weight)).astype(BF)
    allowed = causal_same_patch()
    first = iota((128, 128), 1) < HEAD_DIM
    sums = []
    for pair in range(2):
        lanes = pl.ds(pair * 128, 128)
        total = jnp.zeros((FRAMES, 128), F32)
        for group in range(2):
            rows = pl.ds(group * 128, 128)
            q, k, v = (qkv_ref[part, rows, lanes] for part in range(3))
            mixed = []
            for j in range(2):
                own = jnp.where(first if j == 0 else ~first, q.astype(F32), 0.0).astype(BF)
                scores = jnp.where(allowed, nt(own, k) * HEAD_DIM ** (-0.5), -1e30)
                raised = jnp.exp(scores - jnp.max(scores, axis=1, keepdims=True))
                prob = raised * (1.0 / jnp.sum(raised, axis=1, keepdims=True))
                prob_ref[pair * 4 + group * 2 + j] = prob
                mixed.append(nn(prob.astype(BF), v))
            attended = jnp.where(first, mixed[0], mixed[1]).astype(BF).astype(F32)
            total = total + jnp.sum(attended.reshape(FRAMES, 8, 128), axis=1)
        sums.append(total)
    return jnp.concatenate(sums, axis=1)


def forward_own_kernel(x_ref, *refs):
    qkv_ref, prob_ref, sum_ref = refs[3 * PIECES :]
    sum_ref[...] = forward_heads(x_ref, refs[: 3 * PIECES], qkv_ref, prob_ref)


def forward_other_kernel(side_ref, x_ref, *refs):
    own_ref, extra_ref, qkv_ref, prob_ref, out_ref, sum_ref = refs[3 * PIECES :]
    step = pl.program_id(0)
    side = side_ref[0]

    @pl.when(step == 0)
    def _():
        sum_ref[:, pl.ds(pl.multiple_of(side * HALF, HALF), HALF)] = own_ref[...]

    at = pl.multiple_of((1 - side) * HALF + step * 256, 256)
    sum_ref[:, pl.ds(at, 256)] = forward_heads(x_ref, refs[: 3 * PIECES], qkv_ref, prob_ref)

    @pl.when(step == 1)
    def _():
        sums = sum_ref[...].astype(BF)
        for to in range(FRAMES):
            out_ref[to, :, :D] = sums
            out_ref[to, :, D:] = extra_ref[...]


def weight_specs(weight, at):
    return [
        pl.BlockSpec((*piece.shape[:2], 256), lambda i, part=part: (0, 0, part * 2 + at(i)))
        for part in range(3)
        for piece in weight
    ]


def whole(shape):
    return pl.BlockSpec(shape, lambda *_: (0,) * len(shape))


SAVED_SHAPES = (
    pltpu.HBM((3, 256, HALF), BF),
    pltpu.HBM((16, 128, 128), F32),
)


def saved_specs(at):
    return [
        pl.BlockSpec((3, 256, 256), lambda i: (0, 0, at(i))),
        pl.BlockSpec((8, 128, 128), lambda i: (at(i), 0, 0)),
    ]


def in_hbm(*values):
    return [pltpu.with_memory_space_constraint(v, pltpu.HBM) for v in values]


def forward_own(x, weight):
    return pl.pallas_call(
        forward_own_kernel,
        grid=(2,),
        in_specs=[whole((16, 16, D)), *weight_specs(weight, lambda i: i)],
        out_specs=[*saved_specs(lambda i: i), pl.BlockSpec((FRAMES, 256), lambda i: (0, i))],
        out_shape=(*SAVED_SHAPES, jax.ShapeDtypeStruct((FRAMES, HALF), F32)),
        compiler_params=params(16),
        name="forward_own",
    )(x, *weight * 3)


def forward_other(side, x, weight, own_sum, extra):
    return pl.pallas_call(
        forward_other_kernel,
        grid=(2,),
        in_specs=[
            SMEM,
            whole((16, 16, D)),
            *weight_specs(weight, lambda i: i),
            whole((FRAMES, HALF)),
            whole((16, EXTRA)),
        ],
        out_specs=[*saved_specs(lambda i: i), whole((16, 16, D + EXTRA))],
        out_shape=(*SAVED_SHAPES, pltpu.HBM((16, 16, D + EXTRA), BF)),
        scratch_shapes=[pltpu.VMEM((FRAMES, D), F32)],
        compiler_params=params(16),
        name="forward_other",
    )(side, x, *weight * 3, own_sum, extra)


def head_kernel(at_ref, got_ref, out_w_ref, pair_ref, book_ref, rows_ref, mean_ref, send_ref, pooled_ref):
    got = got_ref[...]
    sums = jnp.sum(got[:, :, :D].astype(F32), axis=0)
    first = got[:, :, D : D + 128].reshape(256, 128)
    second = got[:, :, D + 128 :].reshape(256, 128)
    row, col = (iota((128, 256), 0), iota((128, 256), 1))
    frame, piece = (row % 16, row // 16)
    same = col // 16 == frame
    pick_two = jnp.where(same & (col % 8 == piece), 1.0, 0.0).astype(BF)
    pick_one = jnp.where(same & (col % 16 == piece), 1.0, 0.0).astype(BF)
    means = nn(pick_two, first) + nn(pick_one, second)
    xmean = jnp.concatenate([means[j * 16 : (j + 1) * 16] for j in range(8)], axis=1)
    row, col = (iota((16, 256), 0), iota((16, 256), 1))
    pick_code = jnp.where(col == row * 16 + 8, 1.0, 0.0).astype(BF)
    code = nn(pick_code, second)
    out_w = out_w_ref[...]
    high, low = two_terms(sums)
    pooled = xmean + (nn(high, out_w) + nn(low, out_w)) / PATCHES
    now = nt(pooled, pair_ref[0], HIGHEST)
    later = nt(pooled, pair_ref[1], HIGHEST)
    zero = jnp.zeros((1, LATENT), F32)
    action = now + jnp.concatenate([later[1:], zero], axis=0)
    quantized = jnp.zeros((FRAMES, LATENT), F32)
    for k in range(CODES):
        quantized = quantized + jnp.where(code[:, :LATENT] == k, book_ref[k : k + 1, :], 0.0)
    d_action = 2.0 * BETA * (action - quantized)
    d_before = jnp.concatenate([zero, d_action[:-1]], axis=0)
    d_mean = nn(d_action, pair_ref[0], HIGHEST) + nn(d_before, pair_ref[1], HIGHEST)
    mean_ref[...] = d_mean
    high, low = two_terms(d_mean)
    rows_ref[...] = (nt(high, out_w) + nt(low, out_w)).astype(BF)
    pooled_ref[...] = pooled
    at = at_ref[0]
    block = pooled_ref[:, pl.ds(pl.multiple_of((at // 2) * 128, 128), 128)]
    own = jnp.where(at % 2 == 0, block, pltpu.roll(block, 64, 1))[:, :64]
    mine = jnp.concatenate([own, d_action, code[:, :LATENT]], axis=1)
    for to in range(send_ref.shape[0]):
        send_ref[to] = mine


def head(at, got, out_w, w_pair, codebook, clips):
    return pl.pallas_call(
        head_kernel,
        in_specs=[SMEM, *[pl.BlockSpec(memory_space=pltpu.VMEM)] * 4],
        out_shape=(
            pltpu.HBM((FRAMES, D), BF),
            pltpu.HBM((FRAMES, D), F32),
            pltpu.HBM((clips, FRAMES, 128), F32),
        ),
        scratch_shapes=[pltpu.VMEM((FRAMES, D), F32)],
        compiler_params=params(16),
        name="head",
    )(at, got, out_w, w_pair, codebook)


def backward_heads(rows_ref, at, qkv_ref, prob_ref, weight_refs, acc_ref):
    first = iota((128, 128), 1) < HEAD_DIM
    d_frames = rows_ref[:, pl.ds(at, 256)].astype(F32)
    d_all = jnp.broadcast_to(d_frames[:, None, :], (FRAMES, 8, 256)).reshape(128, 256)
    pieces = [[[None] * 2 for _ in range(2)] for _ in range(3)]
    for pair in range(2):
        lanes = pl.ds(pair * 128, 128)
        d_wide = d_all[:, pair * 128 : (pair + 1) * 128]
        d_out = d_wide.astype(BF)
        for group in range(2):
            rows = pl.ds(group * 128, 128)
            q, k, v = (qkv_ref[part, rows, lanes] for part in range(3))
            found = []
            for j in range(2):
                prob = prob_ref[pair * 4 + group * 2 + j]
                own = jnp.where(first if j == 0 else ~first, d_wide, 0.0).astype(BF)
                d_weights = nt(own, v).astype(BF).astype(F32)
                inner = jnp.sum(d_weights * prob, axis=1, keepdims=True)
                d_scores = (prob * (d_weights - inner) * HEAD_DIM ** (-0.5)).astype(BF)
                found.append((nn(d_scores, k), tn(d_scores, q), tn(prob.astype(BF), d_out)))
            for part in range(3):
                pieces[part][pair][group] = jnp.where(first, found[0][part], found[1][part]).astype(BF)
    total = None
    for part in range(3):
        d_part = jnp.concatenate(
            [jnp.concatenate(pieces[part][pair], axis=0) for pair in range(2)], axis=1
        )
        term = nt(d_part, gathered(weight_refs[part * PIECES : (part + 1) * PIECES]))
        total = term if total is None else total + term
    acc_ref[...] += total


def backward_kernel(side_ref, rows_ref, *refs):
    each = 2 + 3 * PIECES
    own, other = (refs[:each], refs[each : 2 * each])
    out_ref, acc_ref = refs[2 * each :]
    step = pl.program_id(0)
    side = side_ref[0]

    @pl.when(step == 0)
    def _():
        acc_ref[...] = jnp.zeros_like(acc_ref)

    @pl.when(step < 2)
    def _():
        at = pl.multiple_of(side * HALF + step * 256, 256)
        backward_heads(rows_ref, at, own[0], own[1], own[2:], acc_ref)

    @pl.when(step >= 2)
    def _():
        at = pl.multiple_of((1 - side) * HALF + (step - 2) * 256, 256)
        backward_heads(rows_ref, at, other[0], other[1], other[2:], acc_ref)

    @pl.when(step == 3)
    def _():
        acc = acc_ref[...].reshape(2, FRAMES, 8, D)
        both = jnp.concatenate([acc[0][:, None], acc[1][:, None]], axis=1)
        out_ref[...] = both.reshape(FRAMES, 16, D).astype(BF)


def backward(side, d_rows, own, other):
    def early(i):
        return jnp.minimum(i, 1)

    def late(i):
        return jnp.maximum(i - 2, 0)

    return pl.pallas_call(
        backward_kernel,
        grid=(4,),
        in_specs=[
            SMEM,
            whole((FRAMES, D)),
            *saved_specs(early),
            *weight_specs(own[2], early),
            *saved_specs(late),
            *weight_specs(other[2], late),
        ],
        out_specs=whole((16, 16, D)),
        out_shape=pltpu.HBM((16, 16, D + GRADS), BF),
        scratch_shapes=[pltpu.VMEM((256, D), F32)],
        compiler_params=params(24),
        name="backward",
    )(side, d_rows, *in_hbm(*own[:2]), *own[2] * 3, *in_hbm(*other[:2]), *other[2] * 3)


def grads_kernel(_, got_ref, out_ref, step_ref):
    count = got_ref.shape[0] * FRAMES
    got = got_ref[...].reshape(count, 128)
    frame = iota((count, 128), 0) % FRAMES
    before = jnp.where(frame == 0, 0.0, pltpu.roll(got, 1, 0))
    onehot = jnp.where(got[:, 96:97] == iota((count, 128), 1).astype(F32), 1.0, 0.0)
    onehot = jnp.where(iota((count, 128), 1) < CODES, onehot, 0.0)
    now = tn(got, got, HIGHEST)[64:96]
    later = tn(before, got, HIGHEST)[64:96]
    both = jnp.concatenate([now, later], axis=0)
    high = both.astype(BF).astype(F32)
    low = both - high
    packed = jnp.where(iota((64, 128), 1) < 64, high, pltpu.roll(low, 64, 1)).astype(BF)
    for to in range(FRAMES):
        for q in range(4):
            out_ref[to, :, q * 128 : (q + 1) * 128] = packed[q * 16 : (q + 1) * 16]
    by_code = tn(onehot, got, HIGHEST)[:CODES, 64:96] * (-1.0 / BETA)
    counted = tn(onehot, jnp.ones((count, 128), F32), HIGHEST)[:CODES, :LATENT]
    step_ref[...] = by_code / counted


def grads(partly, got):
    return pl.pallas_call(
        grads_kernel,
        grid=(1,),
        in_specs=[pl.BlockSpec(memory_space=pl.ANY), whole(got.shape)],
        out_specs=[
            pl.BlockSpec((16, 16, GRADS), lambda i: (0, 0, D // GRADS)),
            whole((CODES, LATENT)),
        ],
        out_shape=(
            pltpu.HBM(partly.shape, BF),
            jax.ShapeDtypeStruct((CODES, LATENT), F32),
        ),
        input_output_aliases={0: 0},
        compiler_params=params(8),
        name="grads",
    )(*in_hbm(partly), got)


def last_kernel(at_ref, turn_ref, got_ref, tokens_ref, gain_ref, mean_ref, out_ref, pair_ref):
    xf = tokens_ref[...].astype(F32)
    scale = lax.rsqrt(jnp.mean(xf * xf, axis=-1, keepdims=True) + EPS)
    d_normed = turned(got_ref[:, :, :D].reshape(xf.shape).astype(F32), turn_ref[0])
    d_scaled = d_normed * gain_ref[...].astype(F32)
    inner = jnp.sum(d_scaled * xf, axis=-1, keepdims=True) / D
    d_through = d_scaled * scale - xf * (scale * scale * scale * inner)
    d_resid = mean_ref[pl.ds(at_ref[0], 1), :]
    out_ref[...] = (d_resid + d_through).astype(BF)
    even = iota((16, 128), 1) < 64
    for t in range(0, 4, 2):
        for q in range(4):
            terms = [got_ref[t + n, :, D + q * 128 : D + (q + 1) * 128].astype(F32) for n in range(2)]
            value = [term + pltpu.roll(term, 64, 1) for term in terms]
            rows, lanes = (pl.ds(q % 2 * 16, 16), pl.ds(t * 64, 128))
            pair_ref[q // 2, rows, lanes] = jnp.where(even, value[0], value[1])


def last(at, turn, got, tokens, gain, d_mean):
    return pl.pallas_call(
        last_kernel,
        grid=(4,),
        in_specs=[
            SMEM,
            SMEM,
            pl.BlockSpec((4, 16, D + GRADS), lambda i: (i, 0, 0)),
            pl.BlockSpec((64, D), lambda i: (i, 0)),
            whole((1, D)),
            whole((FRAMES, D)),
        ],
        out_specs=[
            pl.BlockSpec((64, D), lambda i: (i, 0)),
            pl.BlockSpec((2, LATENT, 256), lambda i: (0, 0, i)),
        ],
        out_shape=(
            jax.ShapeDtypeStruct((PATCHES, D), BF),
            jax.ShapeDtypeStruct((2, LATENT, D), F32),
        ),
        compiler_params=params(8),
        name="last",
    )(at, turn, got, tokens, gain, d_mean)


def sent_to_all(value, axis):
    count = lax.axis_size(axis)
    return lax.all_to_all(
        jnp.broadcast_to(value[None], (count, *value.shape)), axis, 0, 0, tiled=True
    )


def shifted(value, axis, by):
    count = lax.axis_size(axis)
    return lax.ppermute(value, axis, [(i, (i + by) % count) for i in range(count)])


def local(tokens, gain, w_qkv, w_out, w_pair, codebook, codes):
    side = lax.axis_index("tm_1")
    at = lax.axis_index(TM).reshape(1)
    turn = (lax.axis_index("dp_1") * 32).reshape(1)
    rows = w_qkv.shape[0]
    tokens = tokens.reshape(PATCHES, D)
    gain = gain.reshape(1, D)
    full_out = lax.all_gather(w_out, DP, axis=0, tiled=True)
    by_side = [
        jnp.concatenate([w_qkv[:, p * D + s * HALF :][:, :HALF] for p in range(3)], axis=1)
        for s in range(2)
    ]
    near = sent_to_all(jnp.where(side == 0, *by_side), "dp_0")
    half = near.shape[0] // 2
    after = shifted(near, "dp_1", -1)
    before = shifted(near, "dp_1", 1)
    first = shifted(before[:half], "dp_1", 1)
    second = shifted(after[half:], "dp_1", -1)
    own_w = [near, after, first, second, before]
    other_w = [shifted(piece, "tm_1", 1) for piece in own_w]
    side = side.reshape(1)

    normed, extra = pl.pallas_call(
        norm_kernel,
        in_specs=[SMEM, SMEM, *[pl.BlockSpec(memory_space=pltpu.VMEM)] * 2],
        out_shape=(
            jax.ShapeDtypeStruct((PATCHES, D), BF),
            jax.ShapeDtypeStruct((16, EXTRA), BF),
        ),
        compiler_params=params(8),
        name="norm",
    )(codes.reshape(1), turn, tokens, gain)
    x = lax.all_to_all(normed.reshape(16, 16, D), TM, 0, 0, tiled=True)

    own_qkv, own_prob, own_sum = forward_own(x, own_w)
    other_qkv, other_prob, partial = forward_other(side, x, other_w, own_sum, extra)
    arrived = lax.all_to_all(partial, TM, 0, 0, tiled=True)
    clips = lax.axis_size(DP)
    pair = jnp.swapaxes(w_pair, 1, 2)
    d_rows, d_mean, mine = head(at, arrived, full_out, pair, codebook, clips)
    everyone = lax.all_to_all(mine, DP, 0, 0, tiled=True)
    partly = backward(
        side, d_rows, (own_qkv, own_prob, own_w), (other_qkv, other_prob, other_w)
    )
    outgoing, codebook_step = grads(partly, everyone)
    back = lax.all_to_all(outgoing, TM, 0, 0, tiled=True)
    grad_tokens, grad_pair = last(at, turn, back, tokens, gain, d_mean)
    return (
        grad_tokens.reshape(1, 1, PATCHES, D),
        jnp.swapaxes(grad_pair, 1, 2),
        codebook_step,
    )


def solution(mesh):
    torus = Mesh(mesh.devices.reshape(8, 4, 8, 2), ("dp_0", "dp_1", "tm_0", "tm_1"))
    return jax.shard_map(
        local,
        mesh=torus,
        in_specs=(P(DP, TM, None, None), P(), P(DP, None), P(DP, None), P(), P(), P(DP, TM, None)),
        out_specs=(P(DP, TM, None, None), P(), P()),
        check_vma=False,
    )
```

time: 299 us -> 198 us (0.66)
  waiting for transfers between devices: 131 us -> 41.2 us
  Pallas kernels: 0 us -> 42.2 us
  matrix products: 32.4 us -> 0 us
  local copies, waits for them, and re-layouts: 24 us -> 5.24 us
  other arithmetic: 15.9 us -> 0.03 us
  starting transfers between devices: 55.6 us -> 67.3 us
    all_gather x1, waiting for transfers between devices: 71.4 us -> 0.01 us  [local(): full_out = lax.all_gather(w_out, DP, axis=0, tiled=True)]
    pallas_call x0 -> x7, Pallas kernels: none -> 42.2 us  [the longest x1 15.4 us: backward(): pl.pallas_call(backward_kernel, grid=(4,), in_specs=[SMEM, whole((FRAMES,...]
    dot_general x14 -> x0, matrix products: 28.8 us -> none  [the longest x2 11.7 us: project(): jnp.dot(normed.reshape(-1, shape[-1]), weight, preferred_element_type=jnp...]
    all_to_all x0 -> x1, blocking collectives: none -> 26.2 us  [local(): back = lax.all_to_all(outgoing, TM, 0, 0, tiled=True)]
    ppermute x2 -> x9, starting transfers between devices: 4.24 us -> 29.3 us  [shifted(): lax.ppermute(value, axis, [(i, (i + by) % count) for i in range(count)])]
    all_gather x1 -> x0, blocking collectives: 24.2 us -> none  [local(): every_mean = lax.all_gather(d_mean, TM, axis=1, tiled=True)]
    all_to_all x7 -> x4, waiting for transfers between devices: 56.9 us -> 40.4 us  [the longest x1 20.3 us: sent_to_all(): lax.all_to_all(jnp.broadcast_to(value[None], (count, *value.shape)), axis...]
    all_to_all x7 -> x4, starting transfers between devices: 51.4 us -> 38 us  [the longest x1 13.1 us: local(): arrived = lax.all_to_all(partial, TM, 0, 0, tiled=True)]
  transfers between devices with their start and end apart: 10 -> 14, of which waited for: 8 -> 3; matrix products, arithmetic and copies ran while one was open for 13% -> 0% of each run, Pallas kernels for 0% -> 17%
where the time goes in v1:
time: 198 us; the launch traced here: 197 us
  starting transfers between devices  67.3 us (34%)
  Pallas kernels  42.2 us (21%)
  waiting for transfers between devices  41.2 us (21%)
  blocking collectives  26.2 us (13%)
  between operations  15 us (8%)
  local copies, waits for them, and re-layouts  5.24 us (3%)
    ppermute x9, starting transfers between devices, shifted(): lax.ppermute(value, axis, [(i, (i + by) % count) for i in range(count)])  29.3 us
    all_to_all x1, blocking collectives, local(): back = lax.all_to_all(outgoing, TM, 0, 0, tiled=True)  26.2 us
    all_to_all x1, waiting for transfers between devices, sent_to_all(): lax.all_to_all(jnp.broadcast_to(value[None], (count, *value.shape)), axis...  20.3 us
    all_to_all x1, waiting for transfers between devices, local(): arrived = lax.all_to_all(partial, TM, 0, 0, tiled=True)  20.1 us
    pallas_call x1, Pallas kernels, backward(): pl.pallas_call(backward_kernel, grid=(4,), in_specs=[SMEM, whole((FRAMES,...  15.4 us
    all_to_all x1, starting transfers between devices, local(): arrived = lax.all_to_all(partial, TM, 0, 0, tiled=True)  13.1 us
    all_to_all x1, starting transfers between devices, local(): x = lax.all_to_all(normed.reshape(16, 16, D), TM, 0, 0, tiled=True)  11.6 us
    pallas_call x1, Pallas kernels, forward_other(): pl.pallas_call(forward_other_kernel, grid=(2,), in_specs=[SMEM, whole((16...  8.73 us
  transfers between devices with their start and end apart: 14, of which 3 were waited for; matrix products, arithmetic and copies ran while one was open for 0% of the time, Pallas kernels for 17%

profile of v1, /device:TPU:1, one launch (start us, length us, event | category | flops | bytes accessed | tf_op | source)
XLA Modules:
  0.0 197.1 jit_solution(6530642078057650711)
XLA Ops:
  7.2 0.0 copy-start.7
  7.2 0.0 copy-start.1
  7.2 0.9 fusion
  8.1 0.9 broadcast_in_dim.2
  9.1 7.7 %all-to-all-start.1 = ((bf16[8,32,1536]{2,1,0:T(8,128)(2,1)}), bf16[8,32,1536]{2,1,0:T(8,128)(2,1)S(1)}, u32[]{:S(2)}, u32[]{:S(2)}) async-start(bf16[8,32,1536]{2,1,0:T(8,128)(2,1)} %broadcast_in_dim.2), calls=%async_computation.1 | async-start | bytes 1572864 | tf_op jit(solution)/shard_map/all_to_all | solution.py:442
  16.7 0.0 all-gather.2.cloned.1.call-start
  16.8 0.7 all-gather.2.cloned.1.call-update
  17.5 20.3 %all-to-all-done.1.refs_0_.refs_5_.refs_10_.refs_2_.refs_7_.refs_12_ = bf16[8,32,1536]{2,1,0:T(8,128)(2,1)S(1)} async-done(((bf16[8,32,1536]{2,1,0:T(8,128)(2,1)}), bf16[8,32,1536]{2,1,0:T(8,128)(2,1)S(1)}, u32[]{:S(2)}, u32[]{:S(2)}) %all-to-all-start.1) | async-done | bytes 786464 | tf_op jit(solution)/shard_map/all_to_all | solution.py:442
  37.8 5.7 %collective-permute-start.3 = (bf16[8,32,1536]{2,1,0:T(8,128)(2,1)S(1)}, bf16[8,32,1536]{2,1,0:T(8,128)(2,1)S(1)}, u32[]{:S(2)}, u32[]{:S(2)}) collective-permute-start(bf16[8,32,1536]{2,1,0:T(8,128)(2,1)S(1)} %all-to-all-done.1.refs_0_.refs_5_.refs_10_.refs_2_.refs_7_.refs_12_), channel_id=1, source_target_pairs={{0,16},{16,32},{32,48},{48,0},{1,17},{17,33},{33,49},{49,1},{2,18}... | collective-permute-start | bytes 2359304 | tf_op jit(solution)/shard_map/ppermute | solution.py:449
  43.4 3.2 %collective-permute-start.1 = (bf16[8,32,1536]{2,1,0:T(8,128)(2,1)S(1)}, bf16[8,32,1536]{2,1,0:T(8,128)(2,1)S(1)}, u32[]{:S(2)}, u32[]{:S(2)}) collective-permute-start(bf16[8,32,1536]{2,1,0:T(8,128)(2,1)S(1)} %all-to-all-done.1.refs_0_.refs_5_.refs_10_.refs_2_.refs_7_.refs_12_), channel_id=1, source_target_pairs={{0,48},{16,0},{32,16},{48,32},{1,49},{17,1},{33,17},{49,33},{2,50}... | collective-permute-start | bytes 2359304 | tf_op jit(solution)/shard_map/ppermute | solution.py:449
  46.6 0.0 copy-done.7
  47.3 1.2 norm.1
  48.5 11.6 %all-to-all-start = ((bf16[16,16,1024]{2,1,0:T(8,128)(2,1)}), bf16[16,16,1024]{2,1,0:T(8,128)(2,1)}, u32[]{:S(2)}, u32[]{:S(2)}) async-start(bf16[16,16,1024]{2,1,0:T(8,128)(2,1)} %bitcast.5), calls=%async_computation | async-start | bytes 1048576 | tf_op jit(solution)/shard_map/all_to_all | solution.py:484
  60.1 2.1 %collective-permute-start = (bf16[8,32,1536]{2,1,0:T(8,128)(2,1)S(1)}, bf16[8,32,1536]{2,1,0:T(8,128)(2,1)S(1)}, u32[]{:S(2)}, u32[]{:S(2)}) collective-permute-start(bf16[8,32,1536]{2,1,0:T(8,128)(2,1)S(1)} %all-to-all-done.1.refs_0_.refs_5_.refs_10_.refs_2_.refs_7_.refs_12_), channel_id=1, source_target_pairs={{0,1},{1,0},{2,3},{3,2},{4,5},{5,4},{6,7},{7,6},{8,9},{9,8},{10,11... | collective-permute-start | bytes 2359304 | tf_op jit(solution)/shard_map/ppermute | solution.py:449
  62.2 0.1 collective-permute-done.3.refs_4_.refs_9_.refs_14_.refs_6_.refs_11_.refs_16_
  62.4 2.4 %collective-permute-start.4 = (bf16[4,32,1536]{2,1,0:T(8,128)(2,1)S(1)}, bf16[4,32,1536]{2,1,0:T(8,128)(2,1)S(1)}, u32[]{:S(2)}, u32[]{:S(2)}) collective-permute-start(bf16[4,32,1536]{2,1,0:T(8,128)(2,1)S(1)} %slice.40), channel_id=1, source_target_pairs={{0,16},{16,32},{32,48},{48,0},{1,17},{17,33},{33,49},{49,1},{2,18}... | collective-permute-start | bytes 1179656 | tf_op jit(solution)/shard_map/ppermute | solution.py:449
  64.8 0.0 collective-permute-done.1.refs_1_.refs_6_.refs_11_.refs_3_.refs_8_.refs_13_
  64.8 4.1 %collective-permute-start.6 = (bf16[4,32,1536]{2,1,0:T(8,128)(2,1)S(1)}, bf16[4,32,1536]{2,1,0:T(8,128)(2,1)}, u32[]{:S(2)}, u32[]{:S(2)}) collective-permute-start(bf16[4,32,1536]{2,1,0:T(8,128)(2,1)S(1)} %slice.41), channel_id=1, source_target_pairs={{0,48},{16,0},{32,16},{48,32},{1,49},{17,1},{33,17},{49,33},{2,50}... | collective-permute-start | bytes 1179656 | tf_op jit(solution)/shard_map/ppermute | solution.py:449
  68.9 4.0 %collective-permute-start.2 = (bf16[8,32,1536]{2,1,0:T(8,128)(2,1)S(1)}, bf16[8,32,1536]{2,1,0:T(8,128)(2,1)}, u32[]{:S(2)}, u32[]{:S(2)}) collective-permute-start(bf16[8,32,1536]{2,1,0:T(8,128)(2,1)S(1)} %collective-permute-done.1.refs_1_.refs_6_.refs_11_.refs_3_.refs_8_.refs_13_), channel_id=1, source_target_pairs={{0,1},{1,0},{2,3},{3,2},{4,5},{5,4},{6,7},{7,6},{8,9},{9,8},{10,11... | collective-permute-start | bytes 2359304 | tf_op jit(solution)/shard_map/ppermute | solution.py:449
  72.9 1.9 collective-permute-start.8
  74.9 0.0 collective-permute-done.4.refs_2_.refs_7_.refs_12_.refs_4_.refs_9_.refs_14_
  74.9 4.0 %collective-permute-start.5 = (bf16[4,32,1536]{2,1,0:T(8,128)(2,1)S(1)}, bf16[4,32,1536]{2,1,0:T(8,128)(2,1)}, u32[]{:S(2)}, u32[]{:S(2)}) collective-permute-start(bf16[4,32,1536]{2,1,0:T(8,128)(2,1)S(1)} %collective-permute-done.4.refs_2_.refs_7_.refs_12_.refs_4_.refs_9_.refs_14_), channel_id=1, source_target_pairs={{0,1},{1,0},{2,3},{3,2},{4,5},{5,4},{6,7},{7,6},{8,9},{9,8},{10,11... | collective-permute-start | bytes 1179656 | tf_op jit(solution)/shard_map/ppermute | solution.py:449
  78.9 0.0 collective-permute-done.6.refs_3_.refs_8_.refs_13_.refs_5_.refs_10_.refs_15_
  78.9 1.9 collective-permute-start.7
  80.8 0.0 all-to-all-done.x_ref
  80.8 7.8 %forward_own.1 = (bf16[3,256,512]{2,1,0:T(8,128)(2,1)}, f32[16,128,128]{2,1,0:T(8,128)}, f32[16,512]{1,0:T(8,128)S(1)}) custom-call(bf16[16,16,1024]{2,1,0:T(8,128)(2,1)} %all-to-all-done.x_ref, bf16[8,32,1536]{2,1,0:T(8,128)(2,1)S(1)} %all-to-all-done.1.refs_0_.refs_5_.refs_10_.refs_2_.refs_7_.refs_12_, ...), custom_call_target="tpu_custom_call" | custom-call | tf_op jit(solution)/shard_map/forward_own/pallas_call | solution.py:186
  88.6 0.0 collective-permute-done.refs_0_.refs_5_.refs_10_.refs_19_.refs_24_.refs_29_
  88.6 0.0 collective-permute-done.5.refs_2_.refs_7_.refs_12_.refs_21_.refs_26_.refs_31_
  88.6 0.0 collective-permute-done.7.refs_3_.refs_8_.refs_13_.refs_22_.refs_27_.refs_32_
  88.6 0.0 collective-permute-done.2.refs_1_.refs_6_.refs_11_.refs_20_.refs_25_.refs_30_
  88.6 0.0 collective-permute-done.8.refs_4_.refs_9_.refs_14_.refs_23_.refs_28_.refs_33_
  88.7 0.0 copy-start.6
  88.7 8.7 %forward_other.1 = (bf16[3,256,512]{2,1,0:T(8,128)(2,1)}, f32[16,128,128]{2,1,0:T(8,128)}, bf16[16,16,1280]{2,1,0:T(8,128)(2,1)}) custom-call(s32[1]{0:T(128)} %bitcast.2.side_ref, bf16[16,16,1024]{2,1,0:T(8,128)(2,1)} %all-to-all-done.x_ref, bf16[8,32,1536]{2,1,0:T(8,128)(2,1)S(1)} %collective-permute-done.refs_0_.refs_5_.refs_10_.refs_19_.refs_24_.refs_29_, ...), custom_call_target="tpu_custom_call" | custom-call | tf_op jit(solution)/shard_map/forward_other/pallas_call | solution.py:198
  97.4 13.1 %all-to-all-start.2 = ((bf16[16,16,1280]{2,1,0:T(8,128)(2,1)}), bf16[16,16,1280]{2,1,0:T(8,128)(2,1)}, u32[]{:S(2)}, u32[]{:S(2)}) async-start(bf16[16,16,1280]{2,1,0:T(8,128)(2,1)} %get-tuple-element.21), calls=%async_computation.2 | async-start | bytes 1310720 | tf_op jit(solution)/shard_map/all_to_all | solution.py:488
  110.5 0.0 all-gather.2.cloned.1.call-done.out_w_ref
  110.5 20.1 %all-to-all-done.2.got_ref = bf16[16,16,1280]{2,1,0:T(8,128)(2,1)} async-done(((bf16[16,16,1280]{2,1,0:T(8,128)(2,1)}), bf16[16,16,1280]{2,1,0:T(8,128)(2,1)}, u32[]{:S(2)}, u32[]{:S(2)}) %all-to-all-start.2) | async-done | bytes 655392 | tf_op jit(solution)/shard_map/all_to_all | solution.py:488
  130.6 1.6 copy-done
  132.2 0.9 copy-done.3
  133.2 4.1 %head.1 = (bf16[16,1024]{1,0:T(8,128)(2,1)}, f32[16,1024]{1,0:T(8,128)}, f32[32,16,128]{2,1,0:T(8,128)}) custom-call(s32[1]{0:T(128)} %bitcast.at_ref, bf16[16,16,1280]{2,1,0:T(8,128)(2,1)} %all-to-all-done.2.got_ref, bf16[1024,1024]{1,0:T(8,128)(2,1)S(1)} %copy-done, f32[2,32,1024]{2,1,0:T(8,128)S(1)} %bitcast.12, f32[8,32]{1,0:T(8,128)S(1)} %copy-done.6), custom_call_target="tpu_custom_call" | custom-call | tf_op jit(solution)/shard_map/head/pallas_call | solution.py:257
  137.3 5.6 %all-to-all-start.3 = ((f32[32,16,128]{2,1,0:T(8,128)}), f32[32,16,128]{2,1,0:T(8,128)}, u32[]{:S(2)}, u32[]{:S(2)}) async-start(f32[32,16,128]{2,1,0:T(8,128)} %get-tuple-element.27), calls=%async_computation.3 | async-start | bytes 524288 | tf_op jit(solution)/shard_map/all_to_all | solution.py:492
  143.0 0.7 copy-done.5
  143.7 15.4 %backward.1._ = bf16[16,16,1536]{2,1,0:T(8,128)(2,1)} custom-call(s32[1]{0:T(128)} %bitcast.2.side_ref, bf16[16,1024]{1,0:T(8,128)(2,1)S(1)} %copy-done.5, bf16[3,256,512]{2,1,0:T(8,128)(2,1)} %get-tuple-element.23.refs_0_, f32[16,128,128]{2,1,0:T(8,128)} %get-tuple-element.24.refs_1_, ...), custom_call_target="tpu_custom_call" | custom-call | tf_op jit(solution)/shard_map/backward/pallas_call | solution.py:338
  159.1 0.0 copy-start.2
  159.1 0.0 copy-start.4
  159.1 0.0 all-to-all-done.3.got_ref
  159.1 2.8 %grads.1 = (bf16[16,16,1536]{2,1,0:T(8,128)(2,1)}, f32[8,32]{1,0:T(8,128)}) custom-call(bf16[16,16,1536]{2,1,0:T(8,128)(2,1)} %backward.1._, f32[32,16,128]{2,1,0:T(8,128)} %all-to-all-done.3.got_ref), custom_call_target="tpu_custom_call", output_to_operand_aliasing={{0}: (0, {})} | custom-call | tf_op jit(solution)/shard_map/grads/pallas_call | solution.py:379
  161.9 26.2 %all_to_all.25.got_ref = bf16[16,16,1536]{2,1,0:T(8,128)(2,1)S(1)} all-to-all(bf16[16,16,1536]{2,1,0:T(8,128)(2,1)} %get-tuple-element.28), channel_id=1, replica_groups=mesh['dp_0'=8,'dp_1'=4,'tm_0'=8,'tm_1'=2] {'tm_0','tm_1'}, dimensions={0} | all-to-all | bytes 1572864 | tf_op jit(solution)/shard_map/all_to_all | solution.py:497
  188.1 2.2 %last.1 = (bf16[256,1024]{1,0:T(8,128)(2,1)}, f32[2,32,1024]{2,1,0:T(8,128)}) custom-call(s32[1]{0:T(128)} %bitcast.at_ref, s32[1]{0:T(128)} %bitcast.1.turn_ref, bf16[16,16,1536]{2,1,0:T(8,128)(2,1)S(1)} %all_to_all.25.got_ref, bf16[256,1024]{1,0:T(8,128)(2,1)S(1)} %bitcast.11, bf16[1,1024]{1,0:T(2,128)(2,1)S(1)} %reshape.78.gain_ref, f32[16,1024]{1,0:T(8,128)S(1)} %copy-done.4), custom_call_target="tpu_custom_call" | custom-call | tf_op jit(solution)/shard_map/last/pallas_call | solution.py:416
  (11 shorter events, 0.1 us)
Async XLA Ops:
  7.2 39.5 %copy-start.7 = (bf16[1024]{0:T(1024)(128)(2,1)S(1)}, bf16[1024]{0:T(1024)(128)(2,1)}, u32[]{:S(2)}) copy-start(bf16[1024]{0:T(1024)(128)(2,1)} %param.8) | copy-start | bytes 6148
  7.2 40.1 %copy-start.1 = (bf16[1,1,256,1024]{3,2,1,0:T(8,128)(2,1)S(1)}, bf16[1,1,256,1024]{3,2,1,0:T(8,128)(2,1)}, u32[]{:S(2)}) copy-start(bf16[1,1,256,1024]{3,2,1,0:T(8,128)(2,1)} %param.7) | copy-start | bytes 1572868
  9.1 28.7 %all-to-all-start.1 = ((bf16[8,32,1536]{2,1,0:T(8,128)(2,1)}), bf16[8,32,1536]{2,1,0:T(8,128)(2,1)S(1)}, u32[]{:S(2)}, u32[]{:S(2)}) async-start(bf16[8,32,1536]{2,1,0:T(8,128)(2,1)} %broadcast_in_dim.2), calls=%async_computation.1 | async-start | bytes 1572864 | tf_op jit(solution)/shard_map/all_to_all | solution.py:442
  16.7 93.8 %all-gather.2.cloned.1.call-start = ((), (), s32[]{:S(2)}) async-start(), calls=%async_computation.5 | async-start | bytes 2162688 | tf_op jit(solution)/shard_map/all_gather | solution.py:459
  37.8 24.6 %collective-permute-start.3 = (bf16[8,32,1536]{2,1,0:T(8,128)(2,1)S(1)}, bf16[8,32,1536]{2,1,0:T(8,128)(2,1)S(1)}, u32[]{:S(2)}, u32[]{:S(2)}) collective-permute-start(bf16[8,32,1536]{2,1,0:T(8,128)(2,1)S(1)} %all-to-all-done.1.refs_0_.refs_5_.refs_10_.refs_2_.refs_7_.refs_12_), channel_id=1, source_target_pairs={{0,16},{16,32},{32,48},{48,0},{1,17},{17,33},{33,49},{49,1},{2,18}... | collective-permute-start | bytes 2359304 | tf_op jit(solution)/shard_map/ppermute | solution.py:449
  43.4 21.4 %collective-permute-start.1 = (bf16[8,32,1536]{2,1,0:T(8,128)(2,1)S(1)}, bf16[8,32,1536]{2,1,0:T(8,128)(2,1)S(1)}, u32[]{:S(2)}, u32[]{:S(2)}) collective-permute-start(bf16[8,32,1536]{2,1,0:T(8,128)(2,1)S(1)} %all-to-all-done.1.refs_0_.refs_5_.refs_10_.refs_2_.refs_7_.refs_12_), channel_id=1, source_target_pairs={{0,48},{16,0},{32,16},{48,32},{1,49},{17,1},{33,17},{49,33},{2,50}... | collective-permute-start | bytes 2359304 | tf_op jit(solution)/shard_map/ppermute | solution.py:449
  48.5 32.3 %all-to-all-start = ((bf16[16,16,1024]{2,1,0:T(8,128)(2,1)}), bf16[16,16,1024]{2,1,0:T(8,128)(2,1)}, u32[]{:S(2)}, u32[]{:S(2)}) async-start(bf16[16,16,1024]{2,1,0:T(8,128)(2,1)} %bitcast.5), calls=%async_computation | async-start | bytes 1048576 | tf_op jit(solution)/shard_map/all_to_all | solution.py:484
  60.1 28.5 %collective-permute-start = (bf16[8,32,1536]{2,1,0:T(8,128)(2,1)S(1)}, bf16[8,32,1536]{2,1,0:T(8,128)(2,1)S(1)}, u32[]{:S(2)}, u32[]{:S(2)}) collective-permute-start(bf16[8,32,1536]{2,1,0:T(8,128)(2,1)S(1)} %all-to-all-done.1.refs_0_.refs_5_.refs_10_.refs_2_.refs_7_.refs_12_), channel_id=1, source_target_pairs={{0,1},{1,0},{2,3},{3,2},{4,5},{5,4},{6,7},{7,6},{8,9},{9,8},{10,11... | collective-permute-start | bytes 2359304 | tf_op jit(solution)/shard_map/ppermute | solution.py:449
  62.4 12.5 %collective-permute-start.4 = (bf16[4,32,1536]{2,1,0:T(8,128)(2,1)S(1)}, bf16[4,32,1536]{2,1,0:T(8,128)(2,1)S(1)}, u32[]{:S(2)}, u32[]{:S(2)}) collective-permute-start(bf16[4,32,1536]{2,1,0:T(8,128)(2,1)S(1)} %slice.40), channel_id=1, source_target_pairs={{0,16},{16,32},{32,48},{48,0},{1,17},{17,33},{33,49},{49,1},{2,18}... | collective-permute-start | bytes 1179656 | tf_op jit(solution)/shard_map/ppermute | solution.py:449
  64.8 14.1 %collective-permute-start.6 = (bf16[4,32,1536]{2,1,0:T(8,128)(2,1)S(1)}, bf16[4,32,1536]{2,1,0:T(8,128)(2,1)}, u32[]{:S(2)}, u32[]{:S(2)}) collective-permute-start(bf16[4,32,1536]{2,1,0:T(8,128)(2,1)S(1)} %slice.41), channel_id=1, source_target_pairs={{0,48},{16,0},{32,16},{48,32},{1,49},{17,1},{33,17},{49,33},{2,50}... | collective-permute-start | bytes 1179656 | tf_op jit(solution)/shard_map/ppermute | solution.py:449
  68.9 19.7 %collective-permute-start.2 = (bf16[8,32,1536]{2,1,0:T(8,128)(2,1)S(1)}, bf16[8,32,1536]{2,1,0:T(8,128)(2,1)}, u32[]{:S(2)}, u32[]{:S(2)}) collective-permute-start(bf16[8,32,1536]{2,1,0:T(8,128)(2,1)S(1)} %collective-permute-done.1.refs_1_.refs_6_.refs_11_.refs_3_.refs_8_.refs_13_), channel_id=1, source_target_pairs={{0,1},{1,0},{2,3},{3,2},{4,5},{5,4},{6,7},{7,6},{8,9},{9,8},{10,11... | collective-permute-start | bytes 2359304 | tf_op jit(solution)/shard_map/ppermute | solution.py:449
  72.9 15.7 %collective-permute-start.8 = (bf16[8,32,1536]{2,1,0:T(8,128)(2,1)S(1)}, bf16[8,32,1536]{2,1,0:T(8,128)(2,1)}, u32[]{:S(2)}, u32[]{:S(2)}) collective-permute-start(bf16[8,32,1536]{2,1,0:T(8,128)(2,1)S(1)} %collective-permute-done.3.refs_4_.refs_9_.refs_14_.refs_6_.refs_11_.refs_16_), channel_id=1, source_target_pairs={{0,1},{1,0},{2,3},{3,2},{4,5},{5,4},{6,7},{7,6},{8,9},{9,8},{10,11... | collective-permute-start | bytes 2359304 | tf_op jit(solution)/shard_map/ppermute | solution.py:449
  74.9 13.7 %collective-permute-start.5 = (bf16[4,32,1536]{2,1,0:T(8,128)(2,1)S(1)}, bf16[4,32,1536]{2,1,0:T(8,128)(2,1)}, u32[]{:S(2)}, u32[]{:S(2)}) collective-permute-start(bf16[4,32,1536]{2,1,0:T(8,128)(2,1)S(1)} %collective-permute-done.4.refs_2_.refs_7_.refs_12_.refs_4_.refs_9_.refs_14_), channel_id=1, source_target_pairs={{0,1},{1,0},{2,3},{3,2},{4,5},{5,4},{6,7},{7,6},{8,9},{9,8},{10,11... | collective-permute-start | bytes 1179656 | tf_op jit(solution)/shard_map/ppermute | solution.py:449
  78.9 9.7 %collective-permute-start.7 = (bf16[4,32,1536]{2,1,0:T(8,128)(2,1)}, bf16[4,32,1536]{2,1,0:T(8,128)(2,1)}, u32[]{:S(2)}, u32[]{:S(2)}) collective-permute-start(bf16[4,32,1536]{2,1,0:T(8,128)(2,1)} %collective-permute-done.6.refs_3_.refs_8_.refs_13_.refs_5_.refs_10_.refs_15_), channel_id=1, source_target_pairs={{0,1},{1,0},{2,3},{3,2},{4,5},{5,4},{6,7},{7,6},{8,9},{9,8},{10,11... | collective-permute-start | bytes 1179656 | tf_op jit(solution)/shard_map/ppermute | solution.py:449
  88.7 42.0 %copy-start.6 = (f32[8,32]{1,0:T(8,128)S(1)}, f32[8,32]{1,0:T(8,128)}, u32[]{:S(2)}) copy-start(f32[8,32]{1,0:T(8,128)} %book_ref.1) | copy-start | bytes 3076
  97.4 33.2 %all-to-all-start.2 = ((bf16[16,16,1280]{2,1,0:T(8,128)(2,1)}), bf16[16,16,1280]{2,1,0:T(8,128)(2,1)}, u32[]{:S(2)}, u32[]{:S(2)}) async-start(bf16[16,16,1280]{2,1,0:T(8,128)(2,1)} %get-tuple-element.21), calls=%async_computation.2 | async-start | bytes 1310720 | tf_op jit(solution)/shard_map/all_to_all | solution.py:488
  130.6 1.6 copy-start
  132.2 0.9 copy-start.3
  137.3 21.8 %all-to-all-start.3 = ((f32[32,16,128]{2,1,0:T(8,128)}), f32[32,16,128]{2,1,0:T(8,128)}, u32[]{:S(2)}, u32[]{:S(2)}) async-start(f32[32,16,128]{2,1,0:T(8,128)} %get-tuple-element.27), calls=%async_computation.3 | async-start | bytes 524288 | tf_op jit(solution)/shard_map/all_to_all | solution.py:492
  142.9 0.8 copy-start.5
  159.1 29.0 %copy-start.2 = (bf16[1,1,256,1024]{3,2,1,0:T(8,128)(2,1)S(1)}, bf16[1,1,256,1024]{3,2,1,0:T(8,128)(2,1)}, u32[]{:S(2)}) copy-start(bf16[1,1,256,1024]{3,2,1,0:T(8,128)(2,1)} %param.7) | copy-start | bytes 1572868
  159.1 29.0 %copy-start.4 = (f32[16,1024]{1,0:T(8,128)S(1)}, f32[16,1024]{1,0:T(8,128)}, u32[]{:S(2)}) copy-start(f32[16,1024]{1,0:T(8,128)} %get-tuple-element.29.mean_ref) | copy-start | bytes 196612
Sparse Core Ops, SparseCore 0:
  20.7 85.0 all-gather.1

commit v2 on v1

v2 whole, which is shorter than its diff:
```python
import jax
import jax.numpy as jnp
from jax import lax
from jax.experimental import pallas as pl
from jax.experimental.pallas import tpu as pltpu
from jax.sharding import Mesh
from jax.sharding import PartitionSpec as P

D = 1024
HEAD_DIM = 64
LATENT = 32
CODES = 8
PATCHES = 256
FRAMES = 16
EPS = 1e-06
BETA = 0.25
DP = ("dp_0", "dp_1")
TM = ("tm_0", "tm_1")
HALF = 512
EXTRA = 256
GRADS = 256
PIECES = 5
GROUPS = 4
ROWS = 512
BF = jnp.bfloat16
F32 = jnp.float32
HIGHEST = lax.Precision.HIGHEST


def params(mebibytes):
    return pltpu.CompilerParams(vmem_limit_bytes=mebibytes * 1024 * 1024)


SMEM = pl.BlockSpec(memory_space=pltpu.SMEM)


def nn(a, b, precision=None):
    return lax.dot_general(
        a, b, (((1,), (0,)), ((), ())), precision=precision, preferred_element_type=F32
    )


def nt(a, b, precision=None):
    return lax.dot_general(
        a, b, (((1,), (1,)), ((), ())), precision=precision, preferred_element_type=F32
    )


def tn(a, b, precision=None):
    return lax.dot_general(
        a, b, (((0,), (0,)), ((), ())), precision=precision, preferred_element_type=F32
    )


def two_terms(value):
    high = value.astype(BF)
    return high, (value - high.astype(F32)).astype(BF)


def iota(shape, dim):
    return lax.broadcasted_iota(jnp.int32, shape, dim)


def turned(value, shift):
    width = value.shape[-1]
    tiles = [pltpu.roll(value[:, j : j + 128], shift, 1) for j in range(0, width, 128)]
    return jnp.concatenate(tiles, axis=1)


def share_kernel(side_ref, weight_ref, out_ref):
    for part in range(3):
        at = pl.multiple_of(part * D + side_ref[0] * HALF, HALF)
        value = weight_ref[:, pl.ds(at, HALF)]
        for to in range(out_ref.shape[0]):
            out_ref[to, :, part * HALF : (part + 1) * HALF] = value


def share(side, weight, count):
    return pl.pallas_call(
        share_kernel,
        in_specs=[SMEM, pl.BlockSpec(memory_space=pltpu.VMEM)],
        out_shape=jax.ShapeDtypeStruct((count, weight.shape[0], 3 * HALF), BF),
        compiler_params=params(8),
        name="share",
    )(side, weight)


def norm_kernel(code_ref, turn_ref, tokens_ref, gain_ref, _, normed_ref, extra_ref):
    xf = tokens_ref[...].astype(F32)
    scale = lax.rsqrt(jnp.mean(xf * xf, axis=-1, keepdims=True) + EPS)
    normed = xf * scale * gain_ref[...].astype(F32)
    normed_ref[...] = turned(normed, (128 - turn_ref[0]) % 128).astype(BF)
    mean = jnp.mean(xf, axis=0, keepdims=True)
    rows = jnp.concatenate([mean[:, j * 128 : (j + 1) * 128] for j in range(8)], axis=0)
    high = rows.astype(BF).astype(F32)
    mid = (rows - high).astype(BF).astype(F32)
    low = rows - high - mid
    code = jnp.full((8, 128), code_ref[0], jnp.int32).astype(F32)
    extra_ref[:, :128] = jnp.concatenate([high, mid], axis=0).astype(BF)
    extra_ref[:, 128:] = jnp.concatenate([low, code], axis=0).astype(BF)


def gathered(refs):
    own, after, first, second, before = refs
    half = first.shape[0]
    rows = []
    for far in range(2 * half):
        across = first[far] if far < half else second[far - half]
        rows += [own[far], after[far], across, before[far]]
    return jnp.concatenate(rows, axis=0)


def grouped_rows(value):
    value = value.reshape(FRAMES, GROUPS, 8, value.shape[-1])
    return jnp.concatenate([value[:, g].reshape(128, -1) for g in range(GROUPS)], axis=0)


def frame_of(row):
    return row % 8 * 2 + row // 8


def causal_same_patch():
    row, col = (iota((128, 128), 0), iota((128, 128), 1))
    return (row % 8 == col % 8) & (frame_of(col // 8) <= frame_of(row // 8))


def head_masks():
    lane = iota((1, 128), 1)
    return tuple(jnp.where(lane // HEAD_DIM == j, 1.0, 0.0).astype(BF) for j in range(2))


def by_head(value, masks):
    return jnp.concatenate([value * mask for mask in masks], axis=0)


def units():
    return [(pair, group, pair * GROUPS + group) for pair in range(2) for group in range(GROUPS)]


def forward_heads(x_ref, weight_refs, qkv_ref, prob_ref):
    x = x_ref[...].reshape(ROWS, D)
    for part in range(3):
        weight = gathered(weight_refs[part * PIECES : (part + 1) * PIECES])
        qkv_ref[part] = grouped_rows(nn(x, weight)).astype(BF)
    allowed = causal_same_patch()
    masks = head_masks()

    def taken(part, pair, group):
        return qkv_ref[part, pl.ds(group * 128, 128), pl.ds(pair * 128, 128)]

    for pair, group, unit in units():
        scores = nt(by_head(taken(0, pair, group), masks), taken(1, pair, group))
        for j in range(2):
            one = scores[j * 128 : (j + 1) * 128] * HEAD_DIM ** (-0.5)
            prob_ref[unit * 2 + j] = jnp.where(allowed, one, -1e30)
    for at in range(16):
        scores = prob_ref[at]
        raised = jnp.exp(scores - jnp.max(scores, axis=1, keepdims=True))
        prob_ref[at] = raised * (1.0 / jnp.sum(raised, axis=1, keepdims=True))
    totals = [jnp.zeros((FRAMES, 128), F32)] * 2
    for pair, group, unit in units():
        weights = jnp.concatenate([prob_ref[unit * 2 + j] for j in range(2)], axis=1).astype(BF)
        mixed = nn(weights, by_head(taken(2, pair, group), masks))
        attended = mixed.astype(BF).astype(F32)
        totals[pair] = totals[pair] + jnp.sum(attended.reshape(FRAMES, 8, 128), axis=1)
    return jnp.concatenate(totals, axis=1)


def forward_kernel(_, side_ref, same_ref, cross_ref, *refs):
    extra_ref, qkv_ref, prob_ref, out_ref, x_ref, sum_ref = refs[3 * PIECES :]
    step = pl.program_id(0)

    @pl.when(step == 0)
    def _():
        x_ref[side_ref[0]] = same_ref[...]
        x_ref[1 - side_ref[0]] = cross_ref[...]

    lanes = pl.ds(pl.multiple_of(step * 256, 256), 256)
    sum_ref[:, lanes] = forward_heads(x_ref, refs[: 3 * PIECES], qkv_ref, prob_ref)

    @pl.when(step == 1)
    def _():
        sums = sum_ref[...].astype(BF)
        for to in range(FRAMES):
            out_ref[to, :, :HALF] = sums
            out_ref[to, :, HALF:] = extra_ref[...]


def weight_specs(weight):
    return [
        pl.BlockSpec((*piece.shape[:2], 256), lambda i, part=part: (0, 0, part * 2 + i))
        for part in range(3)
        for piece in weight
    ]


def whole(shape):
    return pl.BlockSpec(shape, lambda *_: (0,) * len(shape))


SAVED_SHAPES = (
    pltpu.HBM((3, ROWS, HALF), BF),
    pltpu.HBM((32, 128, 128), F32),
)


def saved_specs():
    return [
        pl.BlockSpec((3, ROWS, 256), lambda i: (0, 0, i)),
        pl.BlockSpec((16, 128, 128), lambda i: (i, 0, 0)),
    ]


def in_hbm(*values):
    return [pltpu.with_memory_space_constraint(v, pltpu.HBM) for v in values]


def forward(ready, side, same, cross, weight, extra):
    return pl.pallas_call(
        forward_kernel,
        grid=(2,),
        in_specs=[
            pl.BlockSpec(memory_space=pl.ANY),
            SMEM,
            whole(same.shape),
            whole(cross.shape),
            *weight_specs(weight),
            whole((16, EXTRA)),
        ],
        out_specs=[*saved_specs(), whole((16, 16, HALF + EXTRA))],
        out_shape=(*SAVED_SHAPES, pltpu.HBM((16, 16, HALF + EXTRA), BF)),
        scratch_shapes=[pltpu.VMEM((2, 8, 32, D), BF), pltpu.VMEM((FRAMES, HALF), F32)],
        compiler_params=params(24),
        cost_estimate=cost(1_000),
        name="forward",
    )(ready, side, same, cross, *weight * 3, extra)


def head_kernel(
    at_ref, got_ref, out_w_hbm, pair_hbm, book_ref, rows_ref, mean_ref, send_ref, *scratch
):
    pooled_ref, out_w_ref, pair_ref, sem = scratch
    copies = [
        pltpu.make_async_copy(out_w_hbm, out_w_ref, sem.at[0]),
        pltpu.make_async_copy(pair_hbm, pair_ref, sem.at[1]),
    ]
    for copy in copies:
        copy.start()
    got = got_ref[...].reshape(8, 2, 16, HALF + EXTRA)
    sums = [jnp.sum(got[:, c, :, :HALF].astype(F32), axis=0) for c in range(2)]
    sums = jnp.concatenate(sums, axis=1)
    got = got.reshape(16, 16, HALF + EXTRA)
    first = got[:, :, HALF : HALF + 128].reshape(256, 128)
    second = got[:, :, HALF + 128 :].reshape(256, 128)
    row, col = (iota((128, 256), 0), iota((128, 256), 1))
    frame, piece = (frame_of(row % 16), row // 16)
    same = col // 16 == frame
    pick_two = jnp.where(same & (col % 8 == piece), 1.0, 0.0).astype(BF)
    pick_one = jnp.where(same & (col % 16 == piece), 1.0, 0.0).astype(BF)
    means = nn(pick_two, first) + nn(pick_one, second)
    xmean = jnp.concatenate([means[j * 16 : (j + 1) * 16] for j in range(8)], axis=1)
    row, col = (iota((16, 256), 0), iota((16, 256), 1))
    pick_code = jnp.where(col == frame_of(row) * 16 + 8, 1.0, 0.0).astype(BF)
    code = nn(pick_code, second)
    for copy in copies:
        copy.wait()
    sums = jnp.concatenate(two_terms(sums), axis=0)
    moved = nn(sums, out_w_ref[...])
    pooled = xmean + (moved[:FRAMES] + moved[FRAMES:]) / PATCHES
    now = nt(pooled, pair_ref[0], HIGHEST)
    later = nt(pooled, pair_ref[1], HIGHEST)
    zero = jnp.zeros((1, LATENT), F32)
    action = now + jnp.concatenate([later[8:], later[1:8], zero], axis=0)
    quantized = jnp.zeros((FRAMES, LATENT), F32)
    for k in range(CODES):
        quantized = quantized + jnp.where(code[:, :LATENT] == k, book_ref[k : k + 1, :], 0.0)
    d_action = 2.0 * BETA * (action - quantized)
    d_before = jnp.concatenate([zero, d_action[8:15], d_action[:8]], axis=0)
    d_mean = nn(d_action, pair_ref[0], HIGHEST) + nn(d_before, pair_ref[1], HIGHEST)
    mean_ref[...] = d_mean
    terms = jnp.concatenate(two_terms(d_mean), axis=0)
    both = nt(terms, out_w_ref[...])
    rows_ref[...] = (both[:FRAMES] + both[FRAMES:]).astype(BF)
    pooled_ref[...] = pooled
    mine = pooled_ref[:, pl.ds(pl.multiple_of(at_ref[0] * 128, 128), 128)]
    high, low = two_terms(d_action)
    others = [mine.astype(BF), high, low, code[:, : 2 * LATENT].astype(BF)]
    mine = jnp.concatenate(others, axis=1)
    for to in range(send_ref.shape[0]):
        send_ref[to] = mine


def head(at, got, out_w, w_pair, codebook, clips):
    return pl.pallas_call(
        head_kernel,
        in_specs=[
            SMEM,
            pl.BlockSpec(memory_space=pltpu.VMEM),
            *[pl.BlockSpec(memory_space=pl.ANY)] * 2,
            pl.BlockSpec(memory_space=pltpu.VMEM),
        ],
        out_shape=(
            pltpu.HBM((FRAMES, D), BF),
            pltpu.HBM((FRAMES, D), F32),
            pltpu.HBM((clips, FRAMES, 256), BF),
        ),
        scratch_shapes=[
            pltpu.VMEM((FRAMES, D), F32),
            pltpu.VMEM((D, D), BF),
            pltpu.VMEM((2, LATENT, D), F32),
            pltpu.SemaphoreType.DMA((2,)),
        ],
        compiler_params=params(16),
        cost_estimate=cost(1_000),
        name="head",
    )(at, got, *in_hbm(out_w, w_pair), codebook)


def backward_heads(rows_ref, at, qkv_ref, prob_ref, weight_refs, acc_ref, cot_ref, part_ref):
    masks = head_masks()
    d_frames = rows_ref[:, pl.ds(at, 256)].astype(F32)
    d_all = jnp.broadcast_to(d_frames[:, None, :], (FRAMES, 8, 256)).reshape(128, 256).astype(BF)
    d_heads = [by_head(d_all[:, pair * 128 : (pair + 1) * 128], masks) for pair in range(2)]

    def taken(part, pair, group):
        return qkv_ref[part, pl.ds(group * 128, 128), pl.ds(pair * 128, 128)]

    for pair, group, unit in units():
        d_weights = nt(d_heads[pair], taken(2, pair, group))
        for j in range(2):
            cot_ref[unit * 2 + j] = d_weights[j * 128 : (j + 1) * 128].astype(BF)
    for index in range(16):
        prob = prob_ref[index]
        d_weights = cot_ref[index].astype(F32)
        inner = jnp.sum(d_weights * prob, axis=1, keepdims=True)
        cot_ref[index] = (prob * (d_weights - inner) * HEAD_DIM ** (-0.5)).astype(BF)
    for pair, group, unit in units():
        d_scores = [cot_ref[unit * 2 + j] for j in range(2)]
        prob = jnp.concatenate([prob_ref[unit * 2 + j].astype(BF) for j in range(2)], axis=0)
        d_query = nn(jnp.concatenate(d_scores, axis=1), by_head(taken(1, pair, group), masks))
        d_keys = tn(jnp.concatenate(d_scores, axis=0), by_head(taken(0, pair, group), masks))
        d_values = tn(prob, d_heads[pair])
        for part, value in enumerate((d_query, d_keys, d_values)):
            part_ref[part, pl.ds(group * 128, 128), pl.ds(pair * 128, 128)] = value.astype(BF)
    total = None
    for part in range(3):
        term = nt(part_ref[part], gathered(weight_refs[part * PIECES : (part + 1) * PIECES]))
        total = term if total is None else total + term
    acc_ref[...] += total


def backward_kernel(side_ref, rows_ref, *refs):
    keep_ref, give_ref, acc_ref, parts_ref, *scratch = refs[2 + 3 * PIECES :]
    step = pl.program_id(0)
    side = side_ref[0]

    @pl.when(step == 0)
    def _():
        acc_ref[...] = jnp.zeros_like(acc_ref)

    at = pl.multiple_of(side * HALF + step * 256, 256)
    backward_heads(rows_ref, at, refs[0], refs[1], refs[2 : 2 + 3 * PIECES], acc_ref, *scratch)

    @pl.when(step == 1)
    def _():
        for group in range(GROUPS):
            rows = acc_ref[pl.ds(group * 128, 128), :].reshape(2, 8, 8, D)
            parts_ref[:, :, pl.ds(group * 8, 8), :] = rows
        keep_ref[...] = parts_ref[side]
        give_ref[...] = parts_ref[1 - side].astype(BF)


def backward(side, d_rows, qkv, prob, weight):
    return pl.pallas_call(
        backward_kernel,
        grid=(2,),
        in_specs=[SMEM, whole((FRAMES, D)), *saved_specs(), *weight_specs(weight)],
        out_specs=[whole((8, 32, D))] * 2,
        out_shape=(pltpu.HBM((8, 32, D), F32), jax.ShapeDtypeStruct((8, 32, D), BF)),
        scratch_shapes=[
            pltpu.VMEM((ROWS, D), F32),
            pltpu.VMEM((2, 8, 32, D), F32),
            pltpu.VMEM((16, 128, 128), BF),
            pltpu.VMEM((3, ROWS, 256), BF),
        ],
        compiler_params=params(32),
        cost_estimate=cost(1_000),
        name="backward",
    )(side, *in_hbm(d_rows, qkv, prob), *weight * 3)


def grads_kernel(_, keep_ref, cross_ref, got_ref, out_ref, step_ref):
    count = got_ref.shape[0] * FRAMES
    got = got_ref[...].reshape(count, 256)
    means, others = (got[:, :128], got[:, 128:])
    wide = others.astype(F32)
    place, lane = (iota((count, 128), 0) % FRAMES, iota((count, 128), 1))
    shift = jnp.where(place == 0, 0.0, pltpu.roll(wide, count - 7, 0))
    before = jnp.where(place >= 8, pltpu.roll(wide, 8, 0), shift).astype(BF)
    code = wide[:, 2 * LATENT : 2 * LATENT + 1]
    onehot = jnp.where((code == lane.astype(F32)) & (lane < CODES), 1.0, 0.0).astype(BF)
    for part, value in enumerate((others, before)):
        terms = tn(value, means)
        total = (terms[:LATENT] + terms[LATENT : 2 * LATENT]).astype(BF)
        for to in range(8):
            out_ref[to, :, D + part * 128 : D + (part + 1) * 128] = total
    counted = jnp.where(lane < 2 * LATENT, wide, 1.0).astype(BF)
    totals = tn(onehot, counted)[:CODES]
    by_code = (totals[:, :LATENT] + totals[:, LATENT : 2 * LATENT]) * (-1.0 / BETA)
    out_ref[:, :, :D] = (keep_ref[...] + cross_ref[...].astype(F32)).astype(BF)
    step_ref[...] = by_code / totals[:, 2 * LATENT : 2 * LATENT + 1]


def grads(ready, keep, cross, got):
    return pl.pallas_call(
        grads_kernel,
        in_specs=[pl.BlockSpec(memory_space=pl.ANY), *[pl.BlockSpec(memory_space=pltpu.VMEM)] * 3],
        out_shape=(
            pltpu.HBM((8, 32, D + GRADS), BF),
            jax.ShapeDtypeStruct((CODES, LATENT), F32),
        ),
        compiler_params=params(8),
        cost_estimate=cost(1_000),
        name="grads",
    )(ready, keep, cross, got)


def last_kernel(at_ref, turn_ref, got_ref, tokens_ref, gain_ref, mean_ref, out_ref, pair_ref):
    xf = tokens_ref[...].astype(F32)
    scale = lax.rsqrt(jnp.mean(xf * xf, axis=-1, keepdims=True) + EPS)
    d_normed = turned(got_ref[:, :, :D].reshape(xf.shape).astype(F32), turn_ref[0])
    d_scaled = d_normed * gain_ref[...].astype(F32)
    inner = jnp.sum(d_scaled * xf, axis=-1, keepdims=True) / D
    d_through = d_scaled * scale - xf * (scale * scale * scale * inner)
    d_resid = mean_ref[pl.ds(at_ref[0], 1), :]
    out_ref[...] = (d_resid + d_through).astype(BF)
    for t in range(2):
        for part in range(2):
            value = got_ref[t, :, pl.ds(D + part * 128, 128)]
            pair_ref[part, :, pl.ds(t * 128, 128)] = value.astype(F32)


def last(at, turn, got, tokens, gain, d_mean):
    return pl.pallas_call(
        last_kernel,
        grid=(4,),
        in_specs=[
            SMEM,
            SMEM,
            pl.BlockSpec((2, 32, D + GRADS), lambda i: (i, 0, 0)),
            pl.BlockSpec((64, D), lambda i: (i, 0)),
            whole((1, D)),
            whole((FRAMES, D)),
        ],
        out_specs=[
            pl.BlockSpec((64, D), lambda i: (i, 0)),
            pl.BlockSpec((2, LATENT, 256), lambda i: (0, 0, i)),
        ],
        out_shape=(
            jax.ShapeDtypeStruct((PATCHES, D), BF),
            jax.ShapeDtypeStruct((2, LATENT, D), F32),
        ),
        compiler_params=params(8),
        name="last",
    )(at, turn, got, tokens, gain, d_mean)


def cost(flops):
    return pl.CostEstimate(flops=flops, transcendentals=0, bytes_accessed=0)


def touch_kernel(*refs):
    refs[-1][...] = jnp.zeros_like(refs[-1])


def touched(flops, *values):
    return pl.pallas_call(
        touch_kernel,
        in_specs=[pl.BlockSpec(memory_space=pltpu.VMEM)] * len(values),
        out_shape=pltpu.HBM((8, 128), F32),
        compiler_params=params(4),
        cost_estimate=cost(flops),
        name="touch",
    )(*values)


def shifted(value, axis, by):
    count = lax.axis_size(axis)
    return lax.ppermute(value, axis, [(i, (i + by) % count) for i in range(count)])


def local(tokens, gain, w_qkv, w_out, w_pair, codebook, codes):
    side = lax.axis_index("tm_1")
    layer = lax.axis_index("tm_0")
    turn = (lax.axis_index("dp_1") * 32).reshape(1)
    rows = w_qkv.shape[0]
    tokens = tokens.reshape(PATCHES, D)
    gain = gain.reshape(1, D)
    full_out = lax.all_gather(w_out, DP, axis=0, tiled=True)
    far = lax.axis_size("dp_0")
    near = lax.all_to_all(share(side.reshape(1), w_qkv, far), "dp_0", 0, 0, tiled=True)
    half = near.shape[0] // 2
    after = shifted(near, "dp_1", -1)
    before = shifted(near, "dp_1", 1)
    first = shifted(before[:half], "dp_1", 1)
    second = shifted(after[half:], "dp_1", -1)
    own_w = [near, after, first, second, before]
    at = (side * 8 + layer).reshape(1)
    layer = layer.reshape(1)
    side = side.reshape(1)

    normed, extra = pl.pallas_call(
        norm_kernel,
        in_specs=[
            SMEM,
            SMEM,
            *[pl.BlockSpec(memory_space=pltpu.VMEM)] * 2,
            pl.BlockSpec(memory_space=pl.ANY),
        ],
        out_shape=(
            pltpu.HBM((PATCHES, D), BF),
            jax.ShapeDtypeStruct((16, EXTRA), BF),
        ),
        compiler_params=params(8),
        cost_estimate=cost(1_000),
        name="norm",
    )(codes.reshape(1), turn, tokens, gain, near)
    same = lax.all_to_all(normed.reshape(8, 32, D), "tm_0", 0, 0, tiled=True)
    cross = shifted(same, "tm_1", 1)
    qkv, prob, partial = forward(touched(10_000_000_000, first, second), side, same, cross, own_w, extra)
    arrived = lax.all_to_all(partial, TM, 0, 0, tiled=True)
    clips = lax.axis_size(DP)
    pair = jnp.swapaxes(w_pair, 1, 2)
    d_rows, d_mean, mine = head(layer, arrived, full_out, pair, codebook, clips)
    everyone = lax.all_to_all(mine, DP, 0, 0, tiled=True)
    keep, give = backward(side, d_rows, qkv, prob, own_w)
    ready = touched(1_000_000_000, everyone)
    outgoing, codebook_step = grads(ready, keep, shifted(give, "tm_1", 1), everyone)
    back = lax.all_to_all(outgoing, "tm_0", 0, 0, tiled=True)
    grad_tokens, grad_pair = last(at, turn, back, tokens, gain, d_mean)
    return (
        grad_tokens.reshape(1, 1, PATCHES, D),
        jnp.swapaxes(grad_pair, 1, 2),
        codebook_step,
    )


def solution(mesh):
    torus = Mesh(mesh.devices.reshape(8, 4, 8, 2), ("dp_0", "dp_1", "tm_0", "tm_1"))
    return jax.shard_map(
        local,
        mesh=torus,
        in_specs=(P(DP, TM, None, None), P(), P(DP, None), P(DP, None), P(), P(), P(DP, TM, None)),
        out_specs=(P(DP, TM, None, None), P(), P()),
        check_vma=False,
    )
```

time: 198 us -> 175 us (0.88)
  waiting for transfers between devices: 41.2 us -> 70.7 us
  blocking collectives: 26.2 us -> 0 us
  Pallas kernels: 42.2 us -> 24.1 us
  starting transfers between devices: 67.3 us -> 61.7 us
  local copies, waits for them, and re-layouts: 5.24 us -> 3.24 us
    all_to_all x2 -> x3, waiting for transfers between devices: 20.3 us -> 46.8 us  [the longest x1 20.7 us: local(): back = lax.all_to_all(outgoing, 'tm_0', 0, 0, tiled=True)]
    all_to_all x1 -> x0, blocking collectives: 26.2 us -> none  [local(): back = lax.all_to_all(outgoing, TM, 0, 0, tiled=True)]
    pallas_call x5 -> x7, Pallas kernels: 38.8 us -> 20.8 us  [the longest x1 6.91 us: backward(): pl.pallas_call(backward_kernel, grid=(2,), in_specs=[SMEM, whole((FRAMES,...]
    ppermute x9 -> x6, starting transfers between devices: 29.3 us -> 21.1 us  [shifted(): lax.ppermute(value, axis, [(i, (i + by) % count) for i in range(count)])]
    all_to_all x1, waiting for transfers between devices: 20.1 us -> 14.5 us  [local(): arrived = lax.all_to_all(partial, TM, 0, 0, tiled=True)]
    ppermute x9 -> x6, waiting for transfers between devices: 0.13 us -> 4.69 us  [shifted(): lax.ppermute(value, axis, [(i, (i + by) % count) for i in range(count)])]
    all_to_all x1, waiting for transfers between devices: 0.01 us -> 3.99 us  [local(): everyone = lax.all_to_all(mine, DP, 0, 0, tiled=True)]
    all_to_all x2 -> x3, starting transfers between devices: 19.3 us -> 21.4 us  [the longest x1 10.2 us: local(): same = lax.all_to_all(normed.reshape(8, 32, D), 'tm_0', 0, 0, tiled=True)]
  transfers between devices with their start and end apart: 14 -> 12, of which waited for: 3 -> 7; matrix products, arithmetic and copies ran while one was open for 0% -> 0% of each run, Pallas kernels for 17% -> 9%
where the time goes in v2:
time: 175 us
  waiting for transfers between devices  70.7 us (40%)
  starting transfers between devices  61.7 us (35%)
  Pallas kernels  24.1 us (14%)
  between operations  14.9 us (9%)
  local copies, waits for them, and re-layouts  3.24 us (2%)
    ppermute x6, starting transfers between devices, shifted(): lax.ppermute(value, axis, [(i, (i + by) % count) for i in range(count)])  21.1 us
    all_to_all x1, waiting for transfers between devices, local(): back = lax.all_to_all(outgoing, 'tm_0', 0, 0, tiled=True)  20.7 us
    all_to_all x1, waiting for transfers between devices, local(): lax.all_to_all(share(side.reshape(1), w_qkv, far), 'dp_0', 0, 0, tiled=True)  20.3 us
    all_to_all x1, waiting for transfers between devices, local(): arrived = lax.all_to_all(partial, TM, 0, 0, tiled=True)  14.5 us
    all_to_all x1, starting transfers between devices, local(): arrived = lax.all_to_all(partial, TM, 0, 0, tiled=True)  14.2 us
    all_to_all x1, starting transfers between devices, local(): same = lax.all_to_all(normed.reshape(8, 32, D), 'tm_0', 0, 0, tiled=True)  10.2 us
    all_to_all x1, starting transfers between devices, local(): lax.all_to_all(share(side.reshape(1), w_qkv, far), 'dp_0', 0, 0, tiled=True)  7.65 us
    pallas_call x1, Pallas kernels, backward(): pl.pallas_call(backward_kernel, grid=(2,), in_specs=[SMEM, whole((FRAMES,...  6.91 us
  transfers between devices with their start and end apart: 12, of which 7 were waited for; matrix products, arithmetic and copies ran while one was open for 0% of the time, Pallas kernels for 9%

profile of v2, /device:TPU:1, one launch (start us, length us, event | category | flops | bytes accessed | tf_op | source)
XLA Modules:
  0.0 174.7 jit_solution(17291351080370122202)
XLA Ops:
  7.2 0.0 copy-start
  7.2 0.0 copy-start.3
  7.2 1.0 copy-done.3
  8.2 0.0 copy-start.8
  8.2 0.9 share.1
  9.1 7.7 %all-to-all-start = ((bf16[8,32,1536]{2,1,0:T(8,128)(2,1)}), bf16[8,32,1536]{2,1,0:T(8,128)(2,1)S(1)}, u32[]{:S(2)}, u32[]{:S(2)}) async-start(bf16[8,32,1536]{2,1,0:T(8,128)(2,1)} %share.1), calls=%async_computation | async-start | bytes 1572864 | tf_op jit(solution)/shard_map/all_to_all | solution.py:501
  16.8 0.0 all-gather.2.cloned.1.call-start
  16.8 0.7 all-gather.2.cloned.1.call-update
  17.5 20.3 %all-to-all-done._.refs_0_.refs_5_.refs_10_.refs_2_.refs_7_.refs_12_ = bf16[8,32,1536]{2,1,0:T(8,128)(2,1)S(1)} async-done(((bf16[8,32,1536]{2,1,0:T(8,128)(2,1)}), bf16[8,32,1536]{2,1,0:T(8,128)(2,1)S(1)}, u32[]{:S(2)}, u32[]{:S(2)}) %all-to-all-start) | async-done | bytes 786464 | tf_op jit(solution)/shard_map/all_to_all | solution.py:501
  37.8 5.7 %collective-permute-start = (bf16[8,32,1536]{2,1,0:T(8,128)(2,1)S(1)}, bf16[8,32,1536]{2,1,0:T(8,128)(2,1)S(1)}, u32[]{:S(2)}, u32[]{:S(2)}) collective-permute-start(bf16[8,32,1536]{2,1,0:T(8,128)(2,1)S(1)} %all-to-all-done._.refs_0_.refs_5_.refs_10_.refs_2_.refs_7_.refs_12_), channel_id=1, source_target_pairs={{0,16},{16,32},{32,48},{48,0},{1,17},{17,33},{33,49},{49,1},{2,18}... | collective-permute-start | bytes 2359304 | tf_op jit(solution)/shard_map/ppermute | solution.py:489
  43.4 3.2 %collective-permute-start.2 = (bf16[8,32,1536]{2,1,0:T(8,128)(2,1)S(1)}, bf16[8,32,1536]{2,1,0:T(8,128)(2,1)S(1)}, u32[]{:S(2)}, u32[]{:S(2)}) collective-permute-start(bf16[8,32,1536]{2,1,0:T(8,128)(2,1)S(1)} %all-to-all-done._.refs_0_.refs_5_.refs_10_.refs_2_.refs_7_.refs_12_), channel_id=1, source_target_pairs={{0,48},{16,0},{32,16},{48,32},{1,49},{17,1},{33,17},{49,33},{2,50}... | collective-permute-start | bytes 2359304 | tf_op jit(solution)/shard_map/ppermute | solution.py:489
  46.6 0.0 copy-done.8
  47.3 0.0 copy-done
  47.3 1.2 norm.1
  48.5 10.2 %all-to-all-start.1 = ((bf16[8,32,1024]{2,1,0:T(8,128)(2,1)}), bf16[8,32,1024]{2,1,0:T(8,128)(2,1)}, u32[]{:S(2)}, u32[]{:S(2)}) async-start(bf16[8,32,1024]{2,1,0:T(8,128)(2,1)} %bitcast.13), calls=%async_computation.1 | async-start | bytes 1048576 | tf_op jit(solution)/shard_map/all_to_all | solution.py:528
  58.8 3.6 %collective-permute-done.refs_4_.refs_9_.refs_14_.refs_6_.refs_11_.refs_16_ = bf16[8,32,1536]{2,1,0:T(8,128)(2,1)S(1)} collective-permute-done((bf16[8,32,1536]{2,1,0:T(8,128)(2,1)S(1)}, bf16[8,32,1536]{2,1,0:T(8,128)(2,1)S(1)}, u32[]{:S(2)}, u32[]{:S(2)}) %collective-permute-start) | collective-permute-done | bytes 786464 | tf_op jit(solution)/shard_map/ppermute | solution.py:489
  62.4 2.4 %collective-permute-start.1 = (bf16[4,32,1536]{2,1,0:T(8,128)(2,1)S(1)}, bf16[4,32,1536]{2,1,0:T(8,128)(2,1)S(1)}, u32[]{:S(2)}, u32[]{:S(2)}) collective-permute-start(bf16[4,32,1536]{2,1,0:T(8,128)(2,1)S(1)} %slice.8), channel_id=1, source_target_pairs={{0,16},{16,32},{32,48},{48,0},{1,17},{17,33},{33,49},{49,1},{2,18}... | collective-permute-start | bytes 1179656 | tf_op jit(solution)/shard_map/ppermute | solution.py:489
  64.8 0.0 collective-permute-done.2.refs_1_.refs_6_.refs_11_.refs_3_.refs_8_.refs_13_
  64.8 0.8 slice.9
  65.6 4.1 %collective-permute-start.3 = (bf16[4,32,1536]{2,1,0:T(8,128)(2,1)}, bf16[4,32,1536]{2,1,0:T(8,128)(2,1)S(1)}, u32[]{:S(2)}, u32[]{:S(2)}) collective-permute-start(bf16[4,32,1536]{2,1,0:T(8,128)(2,1)} %slice.9), channel_id=1, source_target_pairs={{0,48},{16,0},{32,16},{48,32},{1,49},{17,1},{33,17},{49,33},{2,50}... | collective-permute-start | bytes 1179656 | tf_op jit(solution)/shard_map/ppermute | solution.py:489
  69.7 5.8 %all-to-all-done.1.same_ref = bf16[8,32,1024]{2,1,0:T(8,128)(2,1)} async-done(((bf16[8,32,1024]{2,1,0:T(8,128)(2,1)}), bf16[8,32,1024]{2,1,0:T(8,128)(2,1)}, u32[]{:S(2)}, u32[]{:S(2)}) %all-to-all-start.1) | async-done | bytes 524320 | tf_op jit(solution)/shard_map/all_to_all | solution.py:528
  75.5 3.7 %collective-permute-start.4 = (bf16[8,32,1024]{2,1,0:T(8,128)(2,1)}, bf16[8,32,1024]{2,1,0:T(8,128)(2,1)S(1)}, u32[]{:S(2)}, u32[]{:S(2)}) collective-permute-start(bf16[8,32,1024]{2,1,0:T(8,128)(2,1)} %all-to-all-done.1.same_ref), channel_id=1, source_target_pairs={{0,1},{1,0},{2,3},{3,2},{4,5},{5,4},{6,7},{7,6},{8,9},{9,8},{10,11... | collective-permute-start | bytes 1572872 | tf_op jit(solution)/shard_map/ppermute | solution.py:489
  79.2 0.0 collective-permute-done.1.refs_0_.refs_2_.refs_7_.refs_12_.refs_4_.refs_9_.refs_14_
  79.2 0.0 collective-permute-done.3.refs_1_.refs_3_.refs_8_.refs_13_.refs_5_.refs_10_.refs_15_
  79.2 0.6 touch.2._
  79.8 1.1 collective-permute-done.4.cross_ref
  81.0 0.0 copy-start.6
  81.0 0.7 copy-done.6
  81.6 6.2 %forward.1 = (bf16[3,512,512]{2,1,0:T(8,128)(2,1)}, f32[32,128,128]{2,1,0:T(8,128)}, bf16[16,16,768]{2,1,0:T(8,128)(2,1)}) custom-call(f32[8,128]{1,0:T(8,128)S(1)} %copy-done.6, s32[1]{0:T(128)} %bitcast.3.side_ref, bf16[8,32,1024]{2,1,0:T(8,128)(2,1)} %all-to-all-done.1.same_ref, bf16[8,32,1024]{2,1,0:T(8,128)(2,1)S(1)} %collective-permute-done.4.cross_ref, ...), custom_call_target="tpu_custom_call" | custom-call | flops 1000 | tf_op jit(solution)/shard_map/forward/pallas_call | solution.py:219
  87.8 14.2 %all-to-all-start.2 = ((bf16[16,16,768]{2,1,0:T(8,128)(2,1)}), bf16[16,16,768]{2,1,0:T(8,128)(2,1)S(1)}, u32[]{:S(2)}, u32[]{:S(2)}) async-start(bf16[16,16,768]{2,1,0:T(8,128)(2,1)} %get-tuple-element.19), calls=%async_computation.2 | async-start | bytes 786432 | tf_op jit(solution)/shard_map/all_to_all | solution.py:531
  102.0 14.5 %all-to-all-done.2.got_ref = bf16[16,16,768]{2,1,0:T(8,128)(2,1)S(1)} async-done(((bf16[16,16,768]{2,1,0:T(8,128)(2,1)}), bf16[16,16,768]{2,1,0:T(8,128)(2,1)S(1)}, u32[]{:S(2)}, u32[]{:S(2)}) %all-to-all-start.2) | async-done | bytes 393248 | tf_op jit(solution)/shard_map/all_to_all | solution.py:531
  116.5 0.0 copy-done.5
  116.5 4.2 %head.1 = (bf16[16,1024]{1,0:T(8,128)(2,1)}, f32[16,1024]{1,0:T(8,128)}, bf16[32,16,256]{2,1,0:T(8,128)(2,1)}) custom-call(s32[1]{0:T(128)} %bitcast.2.at_ref, bf16[16,16,768]{2,1,0:T(8,128)(2,1)S(1)} %all-to-all-done.2.got_ref, bf16[1024,1024]{1,0:T(8,128)(2,1)} %all-gather.2.cloned.1.call-done.out_w_hbm, f32[2,32,1024]{2,1,0:T(8,128)} %bitcast.14, ...), custom_call_target="tpu_custom_call" | custom-call | flops 1000 | tf_op jit(solution)/shard_map/head/pallas_call | solution.py:294
  120.7 5.0 %all-to-all-start.3 = ((bf16[32,16,256]{2,1,0:T(8,128)(2,1)}), bf16[32,16,256]{2,1,0:T(8,128)(2,1)S(1)}, u32[]{:S(2)}, u32[]{:S(2)}) async-start(bf16[32,16,256]{2,1,0:T(8,128)(2,1)} %get-tuple-element.20), calls=%async_computation.3 | async-start | bytes 524288 | tf_op jit(solution)/shard_map/all_to_all | solution.py:535
  125.7 6.9 %backward.1 = (f32[8,32,1024]{2,1,0:T(8,128)}, bf16[8,32,1024]{2,1,0:T(8,128)(2,1)}) custom-call(s32[1]{0:T(128)} %bitcast.3.side_ref, bf16[16,1024]{1,0:T(8,128)(2,1)} %get-tuple-element.21.rows_ref, bf16[3,512,512]{2,1,0:T(8,128)(2,1)} %get-tuple-element.22.refs_0_, f32[32,128,128]{2,1,0:T(8,128)} %get-tuple-element.23.refs_1_, ...), custom_call_target="tpu_custom_call" | custom-call | flops 1000 | tf_op jit(solution)/shard_map/backward/pallas_call | solution.py:374
  132.6 2.0 %collective-permute-start.5 = (bf16[8,32,1024]{2,1,0:T(8,128)(2,1)}, bf16[8,32,1024]{2,1,0:T(8,128)(2,1)S(1)}, u32[]{:S(2)}, u32[]{:S(2)}) collective-permute-start(bf16[8,32,1024]{2,1,0:T(8,128)(2,1)} %get-tuple-element.25), channel_id=1, source_target_pairs={{0,1},{1,0},{2,3},{3,2},{4,5},{5,4},{6,7},{7,6},{8,9},{9,8},{10,11... | collective-permute-start | bytes 1572872 | tf_op jit(solution)/shard_map/ppermute | solution.py:489
  134.7 4.0 %all-to-all-done.3.refs_0_.got_ref = bf16[32,16,256]{2,1,0:T(8,128)(2,1)S(1)} async-done(((bf16[32,16,256]{2,1,0:T(8,128)(2,1)}), bf16[32,16,256]{2,1,0:T(8,128)(2,1)S(1)}, u32[]{:S(2)}, u32[]{:S(2)}) %all-to-all-start.3) | async-done | bytes 262176 | tf_op jit(solution)/shard_map/all_to_all | solution.py:535
  138.7 0.6 touch.3._
  139.3 0.0 collective-permute-done.5.cross_ref
  139.3 0.0 copy-done.2
  139.3 0.0 copy-start.7
  139.3 0.7 copy-done.7
  140.0 1.4 grads.1
  141.4 3.5 %all-to-all-start.4 = ((bf16[8,32,1280]{2,1,0:T(8,128)(2,1)}), bf16[8,32,1280]{2,1,0:T(8,128)(2,1)S(1)}, u32[]{:S(2)}, u32[]{:S(2)}) async-start(bf16[8,32,1280]{2,1,0:T(8,128)(2,1)} %get-tuple-element.26), calls=%async_computation.4 | async-start | bytes 1310720 | tf_op jit(solution)/shard_map/all_to_all | solution.py:539
  145.0 20.7 %all-to-all-done.4.got_ref = bf16[8,32,1280]{2,1,0:T(8,128)(2,1)S(1)} async-done(((bf16[8,32,1280]{2,1,0:T(8,128)(2,1)}), bf16[8,32,1280]{2,1,0:T(8,128)(2,1)S(1)}, u32[]{:S(2)}, u32[]{:S(2)}) %all-to-all-start.4) | async-done | bytes 655392 | tf_op jit(solution)/shard_map/all_to_all | solution.py:539
  165.7 0.0 copy-done.1
  165.7 0.0 copy-done.4
  165.7 2.1 %last.1 = (bf16[256,1024]{1,0:T(8,128)(2,1)}, f32[2,32,1024]{2,1,0:T(8,128)}) custom-call(s32[1]{0:T(128)} %bitcast.at_ref, s32[1]{0:T(128)} %bitcast.1.turn_ref, bf16[8,32,1280]{2,1,0:T(8,128)(2,1)S(1)} %all-to-all-done.4.got_ref, bf16[256,1024]{1,0:T(8,128)(2,1)S(1)} %bitcast.12, bf16[1,1024]{1,0:T(2,128)(2,1)S(1)} %reshape.40.gain_ref, ...), custom_call_target="tpu_custom_call" | custom-call | tf_op jit(solution)/shard_map/last/pallas_call | solution.py:444
  (7 shorter events, 0.0 us)
Async XLA Ops:
  7.2 40.2 %copy-start = (bf16[1,1,256,1024]{3,2,1,0:T(8,128)(2,1)S(1)}, bf16[1,1,256,1024]{3,2,1,0:T(8,128)(2,1)}, u32[]{:S(2)}) copy-start(bf16[1,1,256,1024]{3,2,1,0:T(8,128)(2,1)} %param.7) | copy-start | bytes 1572868
  7.2 1.0 copy-start.3
  8.2 38.5 %copy-start.8 = (bf16[1024]{0:T(1024)(128)(2,1)S(1)}, bf16[1024]{0:T(1024)(128)(2,1)}, u32[]{:S(2)}) copy-start(bf16[1024]{0:T(1024)(128)(2,1)} %param.8) | copy-start | bytes 6148
  9.1 28.7 %all-to-all-start = ((bf16[8,32,1536]{2,1,0:T(8,128)(2,1)}), bf16[8,32,1536]{2,1,0:T(8,128)(2,1)S(1)}, u32[]{:S(2)}, u32[]{:S(2)}) async-start(bf16[8,32,1536]{2,1,0:T(8,128)(2,1)} %share.1), calls=%async_computation | async-start | bytes 1572864 | tf_op jit(solution)/shard_map/all_to_all | solution.py:501
  16.8 99.8 %all-gather.2.cloned.1.call-start = ((), (), s32[]{:S(2)}) async-start(), calls=%async_computation.5 | async-start | bytes 2162688 | tf_op jit(solution)/shard_map/all_gather | solution.py:499
  37.8 24.6 %collective-permute-start = (bf16[8,32,1536]{2,1,0:T(8,128)(2,1)S(1)}, bf16[8,32,1536]{2,1,0:T(8,128)(2,1)S(1)}, u32[]{:S(2)}, u32[]{:S(2)}) collective-permute-start(bf16[8,32,1536]{2,1,0:T(8,128)(2,1)S(1)} %all-to-all-done._.refs_0_.refs_5_.refs_10_.refs_2_.refs_7_.refs_12_), channel_id=1, source_target_pairs={{0,16},{16,32},{32,48},{48,0},{1,17},{17,33},{33,49},{49,1},{2,18}... | collective-permute-start | bytes 2359304 | tf_op jit(solution)/shard_map/ppermute | solution.py:489
  43.4 21.4 %collective-permute-start.2 = (bf16[8,32,1536]{2,1,0:T(8,128)(2,1)S(1)}, bf16[8,32,1536]{2,1,0:T(8,128)(2,1)S(1)}, u32[]{:S(2)}, u32[]{:S(2)}) collective-permute-start(bf16[8,32,1536]{2,1,0:T(8,128)(2,1)S(1)} %all-to-all-done._.refs_0_.refs_5_.refs_10_.refs_2_.refs_7_.refs_12_), channel_id=1, source_target_pairs={{0,48},{16,0},{32,16},{48,32},{1,49},{17,1},{33,17},{49,33},{2,50}... | collective-permute-start | bytes 2359304 | tf_op jit(solution)/shard_map/ppermute | solution.py:489
  48.5 26.9 %all-to-all-start.1 = ((bf16[8,32,1024]{2,1,0:T(8,128)(2,1)}), bf16[8,32,1024]{2,1,0:T(8,128)(2,1)}, u32[]{:S(2)}, u32[]{:S(2)}) async-start(bf16[8,32,1024]{2,1,0:T(8,128)(2,1)} %bitcast.13), calls=%async_computation.1 | async-start | bytes 1048576 | tf_op jit(solution)/shard_map/all_to_all | solution.py:528
  62.4 16.9 %collective-permute-start.1 = (bf16[4,32,1536]{2,1,0:T(8,128)(2,1)S(1)}, bf16[4,32,1536]{2,1,0:T(8,128)(2,1)S(1)}, u32[]{:S(2)}, u32[]{:S(2)}) collective-permute-start(bf16[4,32,1536]{2,1,0:T(8,128)(2,1)S(1)} %slice.8), channel_id=1, source_target_pairs={{0,16},{16,32},{32,48},{48,0},{1,17},{17,33},{33,49},{49,1},{2,18}... | collective-permute-start | bytes 1179656 | tf_op jit(solution)/shard_map/ppermute | solution.py:489
  65.6 13.7 %collective-permute-start.3 = (bf16[4,32,1536]{2,1,0:T(8,128)(2,1)}, bf16[4,32,1536]{2,1,0:T(8,128)(2,1)S(1)}, u32[]{:S(2)}, u32[]{:S(2)}) collective-permute-start(bf16[4,32,1536]{2,1,0:T(8,128)(2,1)} %slice.9), channel_id=1, source_target_pairs={{0,48},{16,0},{32,16},{48,32},{1,49},{17,1},{33,17},{49,33},{2,50}... | collective-permute-start | bytes 1179656 | tf_op jit(solution)/shard_map/ppermute | solution.py:489
  75.5 5.5 %collective-permute-start.4 = (bf16[8,32,1024]{2,1,0:T(8,128)(2,1)}, bf16[8,32,1024]{2,1,0:T(8,128)(2,1)S(1)}, u32[]{:S(2)}, u32[]{:S(2)}) collective-permute-start(bf16[8,32,1024]{2,1,0:T(8,128)(2,1)} %all-to-all-done.1.same_ref), channel_id=1, source_target_pairs={{0,1},{1,0},{2,3},{3,2},{4,5},{5,4},{6,7},{7,6},{8,9},{9,8},{10,11... | collective-permute-start | bytes 1572872 | tf_op jit(solution)/shard_map/ppermute | solution.py:489
  81.0 0.7 copy-start.6
  81.6 34.9 %copy-start.5 = (f32[8,32]{1,0:T(8,128)S(1)}, f32[8,32]{1,0:T(8,128)}, u32[]{:S(2)}) copy-start(f32[8,32]{1,0:T(8,128)} %book_ref.1) | copy-start | bytes 3076
  87.8 28.7 %all-to-all-start.2 = ((bf16[16,16,768]{2,1,0:T(8,128)(2,1)}), bf16[16,16,768]{2,1,0:T(8,128)(2,1)S(1)}, u32[]{:S(2)}, u32[]{:S(2)}) async-start(bf16[16,16,768]{2,1,0:T(8,128)(2,1)} %get-tuple-element.19), calls=%async_computation.2 | async-start | bytes 786432 | tf_op jit(solution)/shard_map/all_to_all | solution.py:531
  120.7 17.9 %all-to-all-start.3 = ((bf16[32,16,256]{2,1,0:T(8,128)(2,1)}), bf16[32,16,256]{2,1,0:T(8,128)(2,1)S(1)}, u32[]{:S(2)}, u32[]{:S(2)}) async-start(bf16[32,16,256]{2,1,0:T(8,128)(2,1)} %get-tuple-element.20), calls=%async_computation.3 | async-start | bytes 524288 | tf_op jit(solution)/shard_map/all_to_all | solution.py:535
  132.6 6.6 %copy-start.2 = (f32[8,32,1024]{2,1,0:T(8,128)S(1)}, f32[8,32,1024]{2,1,0:T(8,128)}, u32[]{:S(2)}) copy-start(f32[8,32,1024]{2,1,0:T(8,128)} %get-tuple-element.24.keep_ref) | copy-start | bytes 3145732
  132.6 6.6 %collective-permute-start.5 = (bf16[8,32,1024]{2,1,0:T(8,128)(2,1)}, bf16[8,32,1024]{2,1,0:T(8,128)(2,1)S(1)}, u32[]{:S(2)}, u32[]{:S(2)}) collective-permute-start(bf16[8,32,1024]{2,1,0:T(8,128)(2,1)} %get-tuple-element.25), channel_id=1, source_target_pairs={{0,1},{1,0},{2,3},{3,2},{4,5},{5,4},{6,7},{7,6},{8,9},{9,8},{10,11... | collective-permute-start | bytes 1572872 | tf_op jit(solution)/shard_map/ppermute | solution.py:489
  139.2 26.4 %copy-start.1 = (bf16[1,1,256,1024]{3,2,1,0:T(8,128)(2,1)S(1)}, bf16[1,1,256,1024]{3,2,1,0:T(8,128)(2,1)}, u32[]{:S(2)}) copy-start(bf16[1,1,256,1024]{3,2,1,0:T(8,128)(2,1)} %param.7) | copy-start | bytes 1572868
  139.2 26.4 %copy-start.4 = (f32[16,1024]{1,0:T(8,128)S(1)}, f32[16,1024]{1,0:T(8,128)}, u32[]{:S(2)}) copy-start(f32[16,1024]{1,0:T(8,128)} %get-tuple-element.27.mean_ref) | copy-start | bytes 196612
  139.3 0.8 copy-start.7
  141.4 24.2 %all-to-all-start.4 = ((bf16[8,32,1280]{2,1,0:T(8,128)(2,1)}), bf16[8,32,1280]{2,1,0:T(8,128)(2,1)S(1)}, u32[]{:S(2)}, u32[]{:S(2)}) async-start(bf16[8,32,1280]{2,1,0:T(8,128)(2,1)} %get-tuple-element.26), calls=%async_computation.4 | async-start | bytes 1310720 | tf_op jit(solution)/shard_map/all_to_all | solution.py:539
Sparse Core Ops, SparseCore 0:
  20.8 84.6 all-gather.1

commit v3 on v2

--- a/solution.py
+++ b/solution.py
@@ -19,7 +19,7 @@
 HALF = 512
 EXTRA = 256
 GRADS = 256
-PIECES = 5
+PIECES = 7
 GROUPS = 4
 ROWS = 512
 BF = jnp.bfloat16
@@ -101,12 +101,13 @@
 
 
 def gathered(refs):
-    own, after, first, second, before = refs
-    half = first.shape[0]
+    own, *rest = refs
+    half = rest[0].shape[0]
+    after, across, before = (rest[i : i + 2] for i in range(0, 6, 2))
     rows = []
     for far in range(2 * half):
-        across = first[far] if far < half else second[far - half]
-        rows += [own[far], after[far], across, before[far]]
+        part, at = (far // half, far % half)
+        rows += [own[far], after[part][at], across[part][at], before[part][at]]
     return jnp.concatenate(rows, axis=0)
 
 
@@ -166,7 +167,7 @@
     return jnp.concatenate(totals, axis=1)
 
 
-def forward_kernel(_, side_ref, same_ref, cross_ref, *refs):
+def forward_kernel(_, __, side_ref, same_ref, cross_ref, *refs):
     extra_ref, qkv_ref, prob_ref, out_ref, x_ref, sum_ref = refs[3 * PIECES :]
     step = pl.program_id(0)
 
@@ -215,12 +216,12 @@
     return [pltpu.with_memory_space_constraint(v, pltpu.HBM) for v in values]
 
 
-def forward(ready, side, same, cross, weight, extra):
+def forward(ready, ready_too, side, same, cross, weight, extra):
     return pl.pallas_call(
         forward_kernel,
         grid=(2,),
         in_specs=[
-            pl.BlockSpec(memory_space=pl.ANY),
+            *[pl.BlockSpec(memory_space=pl.ANY)] * 2,
             SMEM,
             whole(same.shape),
             whole(cross.shape),
@@ -233,7 +234,7 @@
         compiler_params=params(24),
         cost_estimate=cost(1_000),
         name="forward",
-    )(ready, side, same, cross, *weight * 3, extra)
+    )(ready, ready_too, side, same, cross, *weight * 3, extra)
 
 
 def head_kernel(
@@ -500,11 +501,14 @@
     far = lax.axis_size("dp_0")
     near = lax.all_to_all(share(side.reshape(1), w_qkv, far), "dp_0", 0, 0, tiled=True)
     half = near.shape[0] // 2
-    after = shifted(near, "dp_1", -1)
-    before = shifted(near, "dp_1", 1)
-    first = shifted(before[:half], "dp_1", 1)
-    second = shifted(after[half:], "dp_1", -1)
-    own_w = [near, after, first, second, before]
+    early, late = (near[:half], near[half:])
+    before_early = shifted(early, "dp_1", 1)
+    after_late = shifted(late, "dp_1", -1)
+    first = shifted(before_early, "dp_1", 1)
+    second = shifted(after_late, "dp_1", -1)
+    after = [shifted(early, "dp_1", -1), after_late]
+    before = [before_early, shifted(late, "dp_1", 1)]
+    own_w = [near, *after, first, second, *before]
     at = (side * 8 + layer).reshape(1)
     layer = layer.reshape(1)
     side = side.reshape(1)
@@ -527,7 +531,7 @@
     )(codes.reshape(1), turn, tokens, gain, near)
     same = lax.all_to_all(normed.reshape(8, 32, D), "tm_0", 0, 0, tiled=True)
     cross = shifted(same, "tm_1", 1)
-    qkv, prob, partial = forward(touched(10_000_000_000, first, second), side, same, cross, own_w, extra)
+    qkv, prob, partial = forward(touched(10_000_000_000, first, second), touched(10_000_000_000, after[0], before[1]), side, same, cross, own_w, extra)
     arrived = lax.all_to_all(partial, TM, 0, 0, tiled=True)
     clips = lax.axis_size(DP)
     pair = jnp.swapaxes(w_pair, 1, 2)

time: 175 us -> 170 us (0.971)
  starting transfers between devices: 61.7 us -> 56.6 us
  waiting for transfers between devices: 70.7 us -> 68.6 us
    all_to_all x1, starting transfers between devices: 14.2 us -> 3.72 us  [local(): arrived = lax.all_to_all(partial, TM, 0, 0, tiled=True)]
    ppermute x6 -> x8, starting transfers between devices: 21.1 us -> 27.2 us  [shifted(): lax.ppermute(value, axis, [(i, (i + by) % count) for i in range(count)])]
    ppermute x6 -> x8, waiting for transfers between devices: 4.69 us -> 1.13 us  [shifted(): lax.ppermute(value, axis, [(i, (i + by) % count) for i in range(count)])]
    all_to_all x1, waiting for transfers between devices: 5.83 us -> 8.72 us  [local(): same = lax.all_to_all(normed.reshape(8, 32, D), 'tm_0', 0, 0, tiled=True)]
  transfers between devices with their start and end apart: 12 -> 14, of which waited for: 7 -> 6; matrix products, arithmetic and copies ran while one was open for 0% -> 0% of each run, Pallas kernels for 9% -> 10%
where the time goes in v3:
time: 170 us; the launch traced here: 168 us
  waiting for transfers between devices  68.6 us (40%)
  starting transfers between devices  56.6 us (33%)
  Pallas kernels  24.8 us (15%)
  between operations  14.9 us (9%)
  local copies, waits for them, and re-layouts  3.2 us (2%)
    ppermute x8, starting transfers between devices, shifted(): lax.ppermute(value, axis, [(i, (i + by) % count) for i in range(count)])  27.2 us
    all_to_all x1, waiting for transfers between devices, local(): lax.all_to_all(share(side.reshape(1), w_qkv, far), 'dp_0', 0, 0, tiled=True)  20.3 us
    all_to_all x1, waiting for transfers between devices, local(): back = lax.all_to_all(outgoing, 'tm_0', 0, 0, tiled=True)  19.3 us
    all_to_all x1, waiting for transfers between devices, local(): arrived = lax.all_to_all(partial, TM, 0, 0, tiled=True)  14.6 us
    all_to_all x1, starting transfers between devices, local(): same = lax.all_to_all(normed.reshape(8, 32, D), 'tm_0', 0, 0, tiled=True)  10.2 us
    all_to_all x1, waiting for transfers between devices, local(): same = lax.all_to_all(normed.reshape(8, 32, D), 'tm_0', 0, 0, tiled=True)  8.72 us
    all_to_all x1, starting transfers between devices, local(): lax.all_to_all(share(side.reshape(1), w_qkv, far), 'dp_0', 0, 0, tiled=True)  7.65 us
    pallas_call x1, Pallas kernels, backward(): pl.pallas_call(backward_kernel, grid=(2,), in_specs=[SMEM, whole((FRAMES,...  6.92 us
  transfers between devices with their start and end apart: 14, of which 6 were waited for; matrix products, arithmetic and copies ran while one was open for 0% of the time, Pallas kernels for 10%

profile of v3, /device:TPU:1, one launch (start us, length us, event | category | flops | bytes accessed | tf_op | source)
XLA Modules:
  0.0 168.0 jit_solution(7655430472857308682)
XLA Ops:
  7.2 0.0 copy-start.3
  7.2 0.9 copy-done.3
  8.1 0.9 share.1
  9.0 7.7 %all-to-all-start = ((bf16[8,32,1536]{2,1,0:T(8,128)(2,1)}), bf16[8,32,1536]{2,1,0:T(8,128)(2,1)S(1)}, u32[]{:S(2)}, u32[]{:S(2)}) async-start(bf16[8,32,1536]{2,1,0:T(8,128)(2,1)} %share.1), calls=%async_computation | async-start | bytes 1572864 | tf_op jit(solution)/shard_map/all_to_all | solution.py:502
  16.7 0.0 all-gather.2.cloned.1.call-start
  16.7 0.7 all-gather.2.cloned.1.call-update
  17.4 20.3 %all-to-all-done._.refs_0_.refs_7_.refs_14_.refs_2_.refs_9_.refs_16_ = bf16[8,32,1536]{2,1,0:T(8,128)(2,1)S(1)} async-done(((bf16[8,32,1536]{2,1,0:T(8,128)(2,1)}), bf16[8,32,1536]{2,1,0:T(8,128)(2,1)S(1)}, u32[]{:S(2)}, u32[]{:S(2)}) %all-to-all-start) | async-done | bytes 786464 | tf_op jit(solution)/shard_map/all_to_all | solution.py:502
  37.7 0.8 fusion
  38.5 5.7 %collective-permute-start = (bf16[4,32,1536]{2,1,0:T(8,128)(2,1)}, bf16[4,32,1536]{2,1,0:T(8,128)(2,1)S(1)}, u32[]{:S(2)}, u32[]{:S(2)}) collective-permute-start(bf16[4,32,1536]{2,1,0:T(8,128)(2,1)} %get-tuple-element.32), channel_id=1, source_target_pairs={{0,16},{16,32},{32,48},{48,0},{1,17},{17,33},{33,49},{49,1},{2,18}... | collective-permute-start | bytes 1179656 | tf_op jit(solution)/shard_map/ppermute | solution.py:490
  44.2 3.2 %collective-permute-start.2 = (bf16[4,32,1536]{2,1,0:T(8,128)(2,1)S(1)}, bf16[4,32,1536]{2,1,0:T(8,128)(2,1)S(1)}, u32[]{:S(2)}, u32[]{:S(2)}) collective-permute-start(bf16[4,32,1536]{2,1,0:T(8,128)(2,1)S(1)} %get-tuple-element.31), channel_id=1, source_target_pairs={{0,48},{16,0},{32,16},{48,32},{1,49},{17,1},{33,17},{49,33},{2,50}... | collective-permute-start | bytes 1179656 | tf_op jit(solution)/shard_map/ppermute | solution.py:490
  47.4 3.4 %collective-permute-start.4 = (bf16[4,32,1536]{2,1,0:T(8,128)(2,1)}, bf16[4,32,1536]{2,1,0:T(8,128)(2,1)S(1)}, u32[]{:S(2)}, u32[]{:S(2)}) collective-permute-start(bf16[4,32,1536]{2,1,0:T(8,128)(2,1)} %get-tuple-element.32), channel_id=1, source_target_pairs={{0,48},{16,0},{32,16},{48,32},{1,49},{17,1},{33,17},{49,33},{2,50}... | collective-permute-start | bytes 1179656 | tf_op jit(solution)/shard_map/ppermute | solution.py:490
  50.8 1.9 %collective-permute-start.5 = (bf16[4,32,1536]{2,1,0:T(8,128)(2,1)S(1)}, bf16[4,32,1536]{2,1,0:T(8,128)(2,1)S(1)}, u32[]{:S(2)}, u32[]{:S(2)}) collective-permute-start(bf16[4,32,1536]{2,1,0:T(8,128)(2,1)S(1)} %get-tuple-element.31), channel_id=1, source_target_pairs={{0,16},{16,32},{32,48},{48,0},{1,17},{17,33},{33,49},{49,1},{2,18}... | collective-permute-start | bytes 1179656 | tf_op jit(solution)/shard_map/ppermute | solution.py:490
  52.7 0.0 copy-done.9
  53.4 0.0 copy-done
  53.4 1.2 norm.1
  54.6 10.2 %all-to-all-start.1 = ((bf16[8,32,1024]{2,1,0:T(8,128)(2,1)}), bf16[8,32,1024]{2,1,0:T(8,128)(2,1)}, u32[]{:S(2)}, u32[]{:S(2)}) async-start(bf16[8,32,1024]{2,1,0:T(8,128)(2,1)} %bitcast.13), calls=%async_computation.1 | async-start | bytes 1048576 | tf_op jit(solution)/shard_map/all_to_all | solution.py:532
  64.8 0.0 collective-permute-done.refs_5_.refs_12_.refs_19_.refs_7_.refs_14_.refs_21_
  64.8 1.9 %collective-permute-start.1 = (bf16[4,32,1536]{2,1,0:T(8,128)(2,1)S(1)}, bf16[4,32,1536]{2,1,0:T(8,128)(2,1)S(1)}, u32[]{:S(2)}, u32[]{:S(2)}) collective-permute-start(bf16[4,32,1536]{2,1,0:T(8,128)(2,1)S(1)} %collective-permute-done.refs_5_.refs_12_.refs_19_.refs_7_.refs_14_.refs_21_), channel_id=1, source_target_pairs={{0,16},{16,32},{32,48},{48,0},{1,17},{17,33},{33,49},{49,1},{2,18}... | collective-permute-start | bytes 1179656 | tf_op jit(solution)/shard_map/ppermute | solution.py:490
  66.7 0.0 collective-permute-done.2.refs_2_.refs_9_.refs_16_.refs_4_.refs_11_.refs_18_
  66.8 4.6 %collective-permute-start.3 = (bf16[4,32,1536]{2,1,0:T(8,128)(2,1)S(1)}, bf16[4,32,1536]{2,1,0:T(8,128)(2,1)S(1)}, u32[]{:S(2)}, u32[]{:S(2)}) collective-permute-start(bf16[4,32,1536]{2,1,0:T(8,128)(2,1)S(1)} %collective-permute-done.2.refs_2_.refs_9_.refs_16_.refs_4_.refs_11_.refs_18_), channel_id=1, source_target_pairs={{0,48},{16,0},{32,16},{48,32},{1,49},{17,1},{33,17},{49,33},{2,50}... | collective-permute-start | bytes 1179656 | tf_op jit(solution)/shard_map/ppermute | solution.py:490
  71.3 0.0 collective-permute-done.4.refs_0_.refs_1_.refs_8_.refs_15_.refs_3_.refs_10_.refs_17_
  71.3 0.0 collective-permute-done.5.refs_1_.refs_6_.refs_13_.refs_20_.refs_8_.refs_15_.refs_22_
  71.4 0.6 touch.4.__
  72.0 8.7 %all-to-all-done.1.same_ref = bf16[8,32,1024]{2,1,0:T(8,128)(2,1)} async-done(((bf16[8,32,1024]{2,1,0:T(8,128)(2,1)}), bf16[8,32,1024]{2,1,0:T(8,128)(2,1)}, u32[]{:S(2)}, u32[]{:S(2)}) %all-to-all-start.1) | async-done | bytes 524320 | tf_op jit(solution)/shard_map/all_to_all | solution.py:532
  80.7 4.6 %collective-permute-start.6 = (bf16[8,32,1024]{2,1,0:T(8,128)(2,1)}, bf16[8,32,1024]{2,1,0:T(8,128)(2,1)S(1)}, u32[]{:S(2)}, u32[]{:S(2)}) collective-permute-start(bf16[8,32,1024]{2,1,0:T(8,128)(2,1)} %all-to-all-done.1.same_ref), channel_id=1, source_target_pairs={{0,1},{1,0},{2,3},{3,2},{4,5},{5,4},{6,7},{7,6},{8,9},{9,8},{10,11... | collective-permute-start | bytes 1572872 | tf_op jit(solution)/shard_map/ppermute | solution.py:490
  85.3 0.0 collective-permute-done.1.refs_0_.refs_3_.refs_10_.refs_17_.refs_5_.refs_12_.refs_19_
  85.3 0.0 collective-permute-done.3.refs_1_.refs_4_.refs_11_.refs_18_.refs_6_.refs_13_.refs_20_
  85.3 0.6 touch.3._
  85.9 1.1 collective-permute-done.6.cross_ref
  87.0 0.0 copy-done.6
  87.0 0.7 copy-done.7
  87.7 6.2 %forward.1 = (bf16[3,512,512]{2,1,0:T(8,128)(2,1)}, f32[32,128,128]{2,1,0:T(8,128)}, bf16[16,16,768]{2,1,0:T(8,128)(2,1)}) custom-call(f32[8,128]{1,0:T(8,128)S(1)} %copy-done.7, f32[8,128]{1,0:T(8,128)S(1)} %copy-done.6, s32[1]{0:T(128)} %bitcast.3.side_ref, bf16[8,32,1024]{2,1,0:T(8,128)(2,1)} %all-to-all-done.1.same_ref, ...), custom_call_target="tpu_custom_call" | custom-call | flops 1000 | tf_op jit(solution)/shard_map/forward/pallas_call | solution.py:220
  93.8 3.7 %all-to-all-start.2 = ((bf16[16,16,768]{2,1,0:T(8,128)(2,1)}), bf16[16,16,768]{2,1,0:T(8,128)(2,1)S(1)}, u32[]{:S(2)}, u32[]{:S(2)}) async-start(bf16[16,16,768]{2,1,0:T(8,128)(2,1)} %get-tuple-element.19), calls=%async_computation.2 | async-start | bytes 786432 | tf_op jit(solution)/shard_map/all_to_all | solution.py:535
  97.6 14.6 %all-to-all-done.2.got_ref = bf16[16,16,768]{2,1,0:T(8,128)(2,1)S(1)} async-done(((bf16[16,16,768]{2,1,0:T(8,128)(2,1)}), bf16[16,16,768]{2,1,0:T(8,128)(2,1)S(1)}, u32[]{:S(2)}, u32[]{:S(2)}) %all-to-all-start.2) | async-done | bytes 393248 | tf_op jit(solution)/shard_map/all_to_all | solution.py:535
  112.1 4.2 %head.1 = (bf16[16,1024]{1,0:T(8,128)(2,1)}, f32[16,1024]{1,0:T(8,128)}, bf16[32,16,256]{2,1,0:T(8,128)(2,1)}) custom-call(s32[1]{0:T(128)} %bitcast.2.at_ref, bf16[16,16,768]{2,1,0:T(8,128)(2,1)S(1)} %all-to-all-done.2.got_ref, bf16[1024,1024]{1,0:T(8,128)(2,1)} %all-gather.2.cloned.1.call-done.out_w_hbm, f32[2,32,1024]{2,1,0:T(8,128)} %bitcast.14, ...), custom_call_target="tpu_custom_call" | custom-call | flops 1000 | tf_op jit(solution)/shard_map/head/pallas_call | solution.py:295
  116.3 4.2 %all-to-all-start.3 = ((bf16[32,16,256]{2,1,0:T(8,128)(2,1)}), bf16[32,16,256]{2,1,0:T(8,128)(2,1)S(1)}, u32[]{:S(2)}, u32[]{:S(2)}) async-start(bf16[32,16,256]{2,1,0:T(8,128)(2,1)} %get-tuple-element.20), calls=%async_computation.3 | async-start | bytes 524288 | tf_op jit(solution)/shard_map/all_to_all | solution.py:539
  120.5 6.9 %backward.1 = (f32[8,32,1024]{2,1,0:T(8,128)}, bf16[8,32,1024]{2,1,0:T(8,128)(2,1)}) custom-call(s32[1]{0:T(128)} %bitcast.3.side_ref, bf16[16,1024]{1,0:T(8,128)(2,1)} %get-tuple-element.21.rows_ref, bf16[3,512,512]{2,1,0:T(8,128)(2,1)} %get-tuple-element.22.refs_0_, f32[32,128,128]{2,1,0:T(8,128)} %get-tuple-element.23.refs_1_, ...), custom_call_target="tpu_custom_call" | custom-call | flops 1000 | tf_op jit(solution)/shard_map/backward/pallas_call | solution.py:375
  127.4 2.0 %collective-permute-start.7 = (bf16[8,32,1024]{2,1,0:T(8,128)(2,1)}, bf16[8,32,1024]{2,1,0:T(8,128)(2,1)S(1)}, u32[]{:S(2)}, u32[]{:S(2)}) collective-permute-start(bf16[8,32,1024]{2,1,0:T(8,128)(2,1)} %get-tuple-element.25), channel_id=1, source_target_pairs={{0,1},{1,0},{2,3},{3,2},{4,5},{5,4},{6,7},{7,6},{8,9},{9,8},{10,11... | collective-permute-start | bytes 1572872 | tf_op jit(solution)/shard_map/ppermute | solution.py:490
  129.4 4.0 %all-to-all-done.3.refs_0_.got_ref = bf16[32,16,256]{2,1,0:T(8,128)(2,1)S(1)} async-done(((bf16[32,16,256]{2,1,0:T(8,128)(2,1)}), bf16[32,16,256]{2,1,0:T(8,128)(2,1)S(1)}, u32[]{:S(2)}, u32[]{:S(2)}) %all-to-all-start.3) | async-done | bytes 262176 | tf_op jit(solution)/shard_map/all_to_all | solution.py:539
  133.4 0.6 touch.5._
  134.0 0.0 collective-permute-done.7.cross_ref
  134.0 0.0 copy-start.8
  134.0 0.7 copy-done.8
  134.8 1.4 grads.1
  136.2 3.5 %all-to-all-start.4 = ((bf16[8,32,1280]{2,1,0:T(8,128)(2,1)}), bf16[8,32,1280]{2,1,0:T(8,128)(2,1)S(1)}, u32[]{:S(2)}, u32[]{:S(2)}) async-start(bf16[8,32,1280]{2,1,0:T(8,128)(2,1)} %get-tuple-element.26), calls=%async_computation.4 | async-start | bytes 1310720 | tf_op jit(solution)/shard_map/all_to_all | solution.py:543
  139.8 19.3 %all-to-all-done.4.got_ref = bf16[8,32,1280]{2,1,0:T(8,128)(2,1)S(1)} async-done(((bf16[8,32,1280]{2,1,0:T(8,128)(2,1)}), bf16[8,32,1280]{2,1,0:T(8,128)(2,1)S(1)}, u32[]{:S(2)}, u32[]{:S(2)}) %all-to-all-start.4) | async-done | bytes 655392 | tf_op jit(solution)/shard_map/all_to_all | solution.py:543
  159.1 0.0 copy-done.1
  159.1 2.1 %last.1 = (bf16[256,1024]{1,0:T(8,128)(2,1)}, f32[2,32,1024]{2,1,0:T(8,128)}) custom-call(s32[1]{0:T(128)} %bitcast.at_ref, s32[1]{0:T(128)} %bitcast.1.turn_ref, bf16[8,32,1280]{2,1,0:T(8,128)(2,1)S(1)} %all-to-all-done.4.got_ref, bf16[256,1024]{1,0:T(8,128)(2,1)S(1)} %bitcast.12, bf16[1,1024]{1,0:T(2,128)(2,1)S(1)} %reshape.40.gain_ref, ...), custom_call_target="tpu_custom_call" | custom-call | tf_op jit(solution)/shard_map/last/pallas_call | solution.py:445
  (13 shorter events, 0.0 us)
Async XLA Ops:
  7.2 0.9 copy-start.3
  8.1 44.6 %copy-start.9 = (bf16[1024]{0:T(1024)(128)(2,1)S(1)}, bf16[1024]{0:T(1024)(128)(2,1)}, u32[]{:S(2)}) copy-start(bf16[1024]{0:T(1024)(128)(2,1)} %param.8) | copy-start | bytes 6148
  8.1 45.3 %copy-start = (bf16[1,1,256,1024]{3,2,1,0:T(8,128)(2,1)S(1)}, bf16[1,1,256,1024]{3,2,1,0:T(8,128)(2,1)}, u32[]{:S(2)}) copy-start(bf16[1,1,256,1024]{3,2,1,0:T(8,128)(2,1)} %param.7) | copy-start | bytes 1572868
  9.0 28.7 %all-to-all-start = ((bf16[8,32,1536]{2,1,0:T(8,128)(2,1)}), bf16[8,32,1536]{2,1,0:T(8,128)(2,1)S(1)}, u32[]{:S(2)}, u32[]{:S(2)}) async-start(bf16[8,32,1536]{2,1,0:T(8,128)(2,1)} %share.1), calls=%async_computation | async-start | bytes 1572864 | tf_op jit(solution)/shard_map/all_to_all | solution.py:502
  16.7 95.4 %all-gather.2.cloned.1.call-start = ((), (), s32[]{:S(2)}) async-start(), calls=%async_computation.5 | async-start | bytes 2162688 | tf_op jit(solution)/shard_map/all_gather | solution.py:500
  38.5 26.3 %collective-permute-start = (bf16[4,32,1536]{2,1,0:T(8,128)(2,1)}, bf16[4,32,1536]{2,1,0:T(8,128)(2,1)S(1)}, u32[]{:S(2)}, u32[]{:S(2)}) collective-permute-start(bf16[4,32,1536]{2,1,0:T(8,128)(2,1)} %get-tuple-element.32), channel_id=1, source_target_pairs={{0,16},{16,32},{32,48},{48,0},{1,17},{17,33},{33,49},{49,1},{2,18}... | collective-permute-start | bytes 1179656 | tf_op jit(solution)/shard_map/ppermute | solution.py:490
  44.2 22.6 %collective-permute-start.2 = (bf16[4,32,1536]{2,1,0:T(8,128)(2,1)S(1)}, bf16[4,32,1536]{2,1,0:T(8,128)(2,1)S(1)}, u32[]{:S(2)}, u32[]{:S(2)}) collective-permute-start(bf16[4,32,1536]{2,1,0:T(8,128)(2,1)S(1)} %get-tuple-element.31), channel_id=1, source_target_pairs={{0,48},{16,0},{32,16},{48,32},{1,49},{17,1},{33,17},{49,33},{2,50}... | collective-permute-start | bytes 1179656 | tf_op jit(solution)/shard_map/ppermute | solution.py:490
  47.4 23.9 %collective-permute-start.4 = (bf16[4,32,1536]{2,1,0:T(8,128)(2,1)}, bf16[4,32,1536]{2,1,0:T(8,128)(2,1)S(1)}, u32[]{:S(2)}, u32[]{:S(2)}) collective-permute-start(bf16[4,32,1536]{2,1,0:T(8,128)(2,1)} %get-tuple-element.32), channel_id=1, source_target_pairs={{0,48},{16,0},{32,16},{48,32},{1,49},{17,1},{33,17},{49,33},{2,50}... | collective-permute-start | bytes 1179656 | tf_op jit(solution)/shard_map/ppermute | solution.py:490
  50.8 20.6 %collective-permute-start.5 = (bf16[4,32,1536]{2,1,0:T(8,128)(2,1)S(1)}, bf16[4,32,1536]{2,1,0:T(8,128)(2,1)S(1)}, u32[]{:S(2)}, u32[]{:S(2)}) collective-permute-start(bf16[4,32,1536]{2,1,0:T(8,128)(2,1)S(1)} %get-tuple-element.31), channel_id=1, source_target_pairs={{0,16},{16,32},{32,48},{48,0},{1,17},{17,33},{33,49},{49,1},{2,18}... | collective-permute-start | bytes 1179656 | tf_op jit(solution)/shard_map/ppermute | solution.py:490
  54.6 26.1 %all-to-all-start.1 = ((bf16[8,32,1024]{2,1,0:T(8,128)(2,1)}), bf16[8,32,1024]{2,1,0:T(8,128)(2,1)}, u32[]{:S(2)}, u32[]{:S(2)}) async-start(bf16[8,32,1024]{2,1,0:T(8,128)(2,1)} %bitcast.13), calls=%async_computation.1 | async-start | bytes 1048576 | tf_op jit(solution)/shard_map/all_to_all | solution.py:532
  64.8 20.5 %collective-permute-start.1 = (bf16[4,32,1536]{2,1,0:T(8,128)(2,1)S(1)}, bf16[4,32,1536]{2,1,0:T(8,128)(2,1)S(1)}, u32[]{:S(2)}, u32[]{:S(2)}) collective-permute-start(bf16[4,32,1536]{2,1,0:T(8,128)(2,1)S(1)} %collective-permute-done.refs_5_.refs_12_.refs_19_.refs_7_.refs_14_.refs_21_), channel_id=1, source_target_pairs={{0,16},{16,32},{32,48},{48,0},{1,17},{17,33},{33,49},{49,1},{2,18}... | collective-permute-start | bytes 1179656 | tf_op jit(solution)/shard_map/ppermute | solution.py:490
  66.8 18.5 %collective-permute-start.3 = (bf16[4,32,1536]{2,1,0:T(8,128)(2,1)S(1)}, bf16[4,32,1536]{2,1,0:T(8,128)(2,1)S(1)}, u32[]{:S(2)}, u32[]{:S(2)}) collective-permute-start(bf16[4,32,1536]{2,1,0:T(8,128)(2,1)S(1)} %collective-permute-done.2.refs_2_.refs_9_.refs_16_.refs_4_.refs_11_.refs_18_), channel_id=1, source_target_pairs={{0,48},{16,0},{32,16},{48,32},{1,49},{17,1},{33,17},{49,33},{2,50}... | collective-permute-start | bytes 1179656 | tf_op jit(solution)/shard_map/ppermute | solution.py:490
  72.0 15.0 %copy-start.6 = (f32[8,128]{1,0:T(8,128)S(1)}, f32[8,128]{1,0:T(8,128)}, u32[]{:S(2)}) copy-start(f32[8,128]{1,0:T(8,128)} %touch.4.__) | copy-start | bytes 12292
  80.7 6.3 %collective-permute-start.6 = (bf16[8,32,1024]{2,1,0:T(8,128)(2,1)}, bf16[8,32,1024]{2,1,0:T(8,128)(2,1)S(1)}, u32[]{:S(2)}, u32[]{:S(2)}) collective-permute-start(bf16[8,32,1024]{2,1,0:T(8,128)(2,1)} %all-to-all-done.1.same_ref), channel_id=1, source_target_pairs={{0,1},{1,0},{2,3},{3,2},{4,5},{5,4},{6,7},{7,6},{8,9},{9,8},{10,11... | collective-permute-start | bytes 1572872 | tf_op jit(solution)/shard_map/ppermute | solution.py:490
  87.0 0.7 copy-start.7
  87.7 24.4 %copy-start.5 = (f32[8,32]{1,0:T(8,128)S(1)}, f32[8,32]{1,0:T(8,128)}, u32[]{:S(2)}) copy-start(f32[8,32]{1,0:T(8,128)} %book_ref.1) | copy-start | bytes 3076
  93.8 18.3 %all-to-all-start.2 = ((bf16[16,16,768]{2,1,0:T(8,128)(2,1)}), bf16[16,16,768]{2,1,0:T(8,128)(2,1)S(1)}, u32[]{:S(2)}, u32[]{:S(2)}) async-start(bf16[16,16,768]{2,1,0:T(8,128)(2,1)} %get-tuple-element.19), calls=%async_computation.2 | async-start | bytes 786432 | tf_op jit(solution)/shard_map/all_to_all | solution.py:535
  116.3 17.1 %all-to-all-start.3 = ((bf16[32,16,256]{2,1,0:T(8,128)(2,1)}), bf16[32,16,256]{2,1,0:T(8,128)(2,1)S(1)}, u32[]{:S(2)}, u32[]{:S(2)}) async-start(bf16[32,16,256]{2,1,0:T(8,128)(2,1)} %get-tuple-element.20), calls=%async_computation.3 | async-start | bytes 524288 | tf_op jit(solution)/shard_map/all_to_all | solution.py:539
  127.4 6.6 %copy-start.2 = (f32[8,32,1024]{2,1,0:T(8,128)S(1)}, f32[8,32,1024]{2,1,0:T(8,128)}, u32[]{:S(2)}) copy-start(f32[8,32,1024]{2,1,0:T(8,128)} %get-tuple-element.24.keep_ref) | copy-start | bytes 3145732
  127.4 6.6 %collective-permute-start.7 = (bf16[8,32,1024]{2,1,0:T(8,128)(2,1)}, bf16[8,32,1024]{2,1,0:T(8,128)(2,1)S(1)}, u32[]{:S(2)}, u32[]{:S(2)}) collective-permute-start(bf16[8,32,1024]{2,1,0:T(8,128)(2,1)} %get-tuple-element.25), channel_id=1, source_target_pairs={{0,1},{1,0},{2,3},{3,2},{4,5},{5,4},{6,7},{7,6},{8,9},{9,8},{10,11... | collective-permute-start | bytes 1572872 | tf_op jit(solution)/shard_map/ppermute | solution.py:490
  134.0 25.1 %copy-start.1 = (bf16[1,1,256,1024]{3,2,1,0:T(8,128)(2,1)S(1)}, bf16[1,1,256,1024]{3,2,1,0:T(8,128)(2,1)}, u32[]{:S(2)}) copy-start(bf16[1,1,256,1024]{3,2,1,0:T(8,128)(2,1)} %param.7) | copy-start | bytes 1572868
  134.0 25.1 %copy-start.4 = (f32[16,1024]{1,0:T(8,128)S(1)}, f32[16,1024]{1,0:T(8,128)}, u32[]{:S(2)}) copy-start(f32[16,1024]{1,0:T(8,128)} %get-tuple-element.27.mean_ref) | copy-start | bytes 196612
  134.0 0.8 copy-start.8
  136.2 22.9 %all-to-all-start.4 = ((bf16[8,32,1280]{2,1,0:T(8,128)(2,1)}), bf16[8,32,1280]{2,1,0:T(8,128)(2,1)S(1)}, u32[]{:S(2)}, u32[]{:S(2)}) async-start(bf16[8,32,1280]{2,1,0:T(8,128)(2,1)} %get-tuple-element.26), calls=%async_computation.4 | async-start | bytes 1310720 | tf_op jit(solution)/shard_map/all_to_all | solution.py:543
Sparse Core Ops, SparseCore 0:
  20.7 84.5 all-gather.1

commit v4 on v3

--- a/solution.py
+++ b/solution.py
@@ -67,22 +67,41 @@
     return jnp.concatenate(tiles, axis=1)
 
 
-def share_kernel(side_ref, weight_ref, out_ref):
+def share_kernel(side_ref, weight_ref, out_ref, own_ref, sem):
+    copies = []
     for part in range(3):
         at = pl.multiple_of(part * D + side_ref[0] * HALF, HALF)
-        value = weight_ref[:, pl.ds(at, HALF)]
-        for to in range(out_ref.shape[0]):
-            out_ref[to, :, part * HALF : (part + 1) * HALF] = value
+        lanes = pl.ds(part * HALF, HALF)
+        piece = weight_ref.at[:, pl.ds(at, HALF)]
+        copies.append(pltpu.make_async_copy(piece, own_ref.at[:, lanes], sem.at[part]))
+    for copy in copies:
+        copy.start()
+    for copy in copies:
+        copy.wait()
+    sends = [
+        pltpu.make_async_copy(own_ref, out_ref.at[to], sem.at[3 + to])
+        for to in range(out_ref.shape[0])
+    ]
+    for send in sends:
+        send.start()
+    for send in sends:
+        send.wait()
 
 
 def share(side, weight, count):
+    rows = weight.shape[0]
     return pl.pallas_call(
         share_kernel,
-        in_specs=[SMEM, pl.BlockSpec(memory_space=pltpu.VMEM)],
-        out_shape=jax.ShapeDtypeStruct((count, weight.shape[0], 3 * HALF), BF),
+        in_specs=[SMEM, pl.BlockSpec(memory_space=pl.ANY)],
+        out_specs=pl.BlockSpec(memory_space=pl.ANY),
+        out_shape=pltpu.HBM((count, rows, 3 * HALF), BF),
+        scratch_shapes=[
+            pltpu.VMEM((rows, 3 * HALF), BF),
+            pltpu.SemaphoreType.DMA((3 + count,)),
+        ],
         compiler_params=params(8),
         name="share",
-    )(side, weight)
+    )(side, *in_hbm(weight))
 
 
 def norm_kernel(code_ref, turn_ref, tokens_ref, gain_ref, _, normed_ref, extra_ref):
@@ -234,7 +253,7 @@
         compiler_params=params(24),
         cost_estimate=cost(1_000),
         name="forward",
-    )(ready, ready_too, side, same, cross, *weight * 3, extra)
+    )(*in_hbm(ready, ready_too), side, same, cross, *weight * 3, extra)
 
 
 def head_kernel(
@@ -423,7 +442,7 @@
         compiler_params=params(8),
         cost_estimate=cost(1_000),
         name="grads",
-    )(ready, keep, cross, got)
+    )(*in_hbm(ready), keep, cross, got)
 
 
 def last_kernel(at_ref, turn_ref, got_ref, tokens_ref, gain_ref, mean_ref, out_ref, pair_ref):

time: 170 us -> 169 us (level)
  local copies, waits for them, and re-layouts: 3.2 us -> 0.83 us
    unnamed x20 -> x12, local copies, waits for them, and re-layouts: 2.38 us -> 0.03 us
where the time goes in v4:
time: 169 us; the launch traced here: 167 us
  waiting for transfers between devices  68.4 us (40%)
  starting transfers between devices  57.7 us (34%)
  Pallas kernels  25.7 us (15%)
  between operations  14.9 us (9%)
    ppermute x8, starting transfers between devices, shifted(): lax.ppermute(value, axis, [(i, (i + by) % count) for i in range(count)])  27.2 us
    all_to_all x1, waiting for transfers between devices, local(): lax.all_to_all(share(side.reshape(1), w_qkv, far), 'dp_0', 0, 0, tiled=True)  20.3 us
    all_to_all x1, waiting for transfers between devices, local(): back = lax.all_to_all(outgoing, 'tm_0', 0, 0, tiled=True)  19.6 us
    all_to_all x1, waiting for transfers between devices, local(): arrived = lax.all_to_all(partial, TM, 0, 0, tiled=True)  14.6 us
    all_to_all x1, starting transfers between devices, local(): same = lax.all_to_all(normed.reshape(8, 32, D), 'tm_0', 0, 0, tiled=True)  10.2 us
    all_to_all x1, waiting for transfers between devices, local(): same = lax.all_to_all(normed.reshape(8, 32, D), 'tm_0', 0, 0, tiled=True)  8.73 us
    all_to_all x1, starting transfers between devices, local(): lax.all_to_all(share(side.reshape(1), w_qkv, far), 'dp_0', 0, 0, tiled=True)  7.66 us
    pallas_call x1, Pallas kernels, backward(): pl.pallas_call(backward_kernel, grid=(2,), in_specs=[SMEM, whole((FRAMES,...  6.93 us
  transfers between devices with their start and end apart: 14, of which 6 were waited for; matrix products, arithmetic and copies ran while one was open for 0% of the time, Pallas kernels for 10%

profile of v4, /device:TPU:1, one launch (start us, length us, event | category | flops | bytes accessed | tf_op | source)
XLA Modules:
  0.0 167.5 jit_solution(5274759784656928505)
XLA Ops:
  7.2 0.0 copy-start.5
  7.2 0.0 copy-start
  7.2 1.8 %share.1 = bf16[8,32,1536]{2,1,0:T(8,128)(2,1)} custom-call(s32[1]{0:T(128)} %bitcast.3.side_ref, bf16[32,3072]{1,0:T(8,128)(2,1)} %weight_ref.1), custom_call_target="tpu_custom_call" | custom-call | tf_op jit(solution)/shard_map/share/pallas_call | solution.py:93
  9.0 7.7 %all-to-all-start = ((bf16[8,32,1536]{2,1,0:T(8,128)(2,1)}), bf16[8,32,1536]{2,1,0:T(8,128)(2,1)S(1)}, u32[]{:S(2)}, u32[]{:S(2)}) async-start(bf16[8,32,1536]{2,1,0:T(8,128)(2,1)} %share.1), calls=%async_computation | async-start | bytes 1572864 | tf_op jit(solution)/shard_map/all_to_all | solution.py:521
  16.7 0.0 all-gather.2.cloned.1.call-start
  16.7 0.7 all-gather.2.cloned.1.call-update
  17.4 20.3 %all-to-all-done._.refs_0_.refs_7_.refs_14_.refs_2_.refs_9_.refs_16_ = bf16[8,32,1536]{2,1,0:T(8,128)(2,1)S(1)} async-done(((bf16[8,32,1536]{2,1,0:T(8,128)(2,1)}), bf16[8,32,1536]{2,1,0:T(8,128)(2,1)S(1)}, u32[]{:S(2)}, u32[]{:S(2)}) %all-to-all-start) | async-done | bytes 786464 | tf_op jit(solution)/shard_map/all_to_all | solution.py:521
  37.7 0.8 fusion
  38.5 5.7 %collective-permute-start = (bf16[4,32,1536]{2,1,0:T(8,128)(2,1)}, bf16[4,32,1536]{2,1,0:T(8,128)(2,1)S(1)}, u32[]{:S(2)}, u32[]{:S(2)}) collective-permute-start(bf16[4,32,1536]{2,1,0:T(8,128)(2,1)} %get-tuple-element.32), channel_id=1, source_target_pairs={{0,16},{16,32},{32,48},{48,0},{1,17},{17,33},{33,49},{49,1},{2,18}... | collective-permute-start | bytes 1179656 | tf_op jit(solution)/shard_map/ppermute | solution.py:509
  44.2 3.2 %collective-permute-start.2 = (bf16[4,32,1536]{2,1,0:T(8,128)(2,1)S(1)}, bf16[4,32,1536]{2,1,0:T(8,128)(2,1)S(1)}, u32[]{:S(2)}, u32[]{:S(2)}) collective-permute-start(bf16[4,32,1536]{2,1,0:T(8,128)(2,1)S(1)} %get-tuple-element.31), channel_id=1, source_target_pairs={{0,48},{16,0},{32,16},{48,32},{1,49},{17,1},{33,17},{49,33},{2,50}... | collective-permute-start | bytes 1179656 | tf_op jit(solution)/shard_map/ppermute | solution.py:509
  47.4 3.4 %collective-permute-start.4 = (bf16[4,32,1536]{2,1,0:T(8,128)(2,1)}, bf16[4,32,1536]{2,1,0:T(8,128)(2,1)S(1)}, u32[]{:S(2)}, u32[]{:S(2)}) collective-permute-start(bf16[4,32,1536]{2,1,0:T(8,128)(2,1)} %get-tuple-element.32), channel_id=1, source_target_pairs={{0,48},{16,0},{32,16},{48,32},{1,49},{17,1},{33,17},{49,33},{2,50}... | collective-permute-start | bytes 1179656 | tf_op jit(solution)/shard_map/ppermute | solution.py:509
  50.7 1.9 %collective-permute-start.5 = (bf16[4,32,1536]{2,1,0:T(8,128)(2,1)S(1)}, bf16[4,32,1536]{2,1,0:T(8,128)(2,1)S(1)}, u32[]{:S(2)}, u32[]{:S(2)}) collective-permute-start(bf16[4,32,1536]{2,1,0:T(8,128)(2,1)S(1)} %get-tuple-element.31), channel_id=1, source_target_pairs={{0,16},{16,32},{32,48},{48,0},{1,17},{17,33},{33,49},{49,1},{2,18}... | collective-permute-start | bytes 1179656 | tf_op jit(solution)/shard_map/ppermute | solution.py:509
  52.7 0.0 copy-done.5
  53.4 0.0 copy-done
  53.4 1.2 norm.1
  54.6 10.2 %all-to-all-start.1 = ((bf16[8,32,1024]{2,1,0:T(8,128)(2,1)}), bf16[8,32,1024]{2,1,0:T(8,128)(2,1)}, u32[]{:S(2)}, u32[]{:S(2)}) async-start(bf16[8,32,1024]{2,1,0:T(8,128)(2,1)} %bitcast.13), calls=%async_computation.1 | async-start | bytes 1048576 | tf_op jit(solution)/shard_map/all_to_all | solution.py:551
  64.8 0.0 collective-permute-done.refs_5_.refs_12_.refs_19_.refs_7_.refs_14_.refs_21_
  64.8 1.9 %collective-permute-start.1 = (bf16[4,32,1536]{2,1,0:T(8,128)(2,1)S(1)}, bf16[4,32,1536]{2,1,0:T(8,128)(2,1)S(1)}, u32[]{:S(2)}, u32[]{:S(2)}) collective-permute-start(bf16[4,32,1536]{2,1,0:T(8,128)(2,1)S(1)} %collective-permute-done.refs_5_.refs_12_.refs_19_.refs_7_.refs_14_.refs_21_), channel_id=1, source_target_pairs={{0,16},{16,32},{32,48},{48,0},{1,17},{17,33},{33,49},{49,1},{2,18}... | collective-permute-start | bytes 1179656 | tf_op jit(solution)/shard_map/ppermute | solution.py:509
  66.7 0.0 collective-permute-done.2.refs_2_.refs_9_.refs_16_.refs_4_.refs_11_.refs_18_
  66.7 4.6 %collective-permute-start.3 = (bf16[4,32,1536]{2,1,0:T(8,128)(2,1)S(1)}, bf16[4,32,1536]{2,1,0:T(8,128)(2,1)S(1)}, u32[]{:S(2)}, u32[]{:S(2)}) collective-permute-start(bf16[4,32,1536]{2,1,0:T(8,128)(2,1)S(1)} %collective-permute-done.2.refs_2_.refs_9_.refs_16_.refs_4_.refs_11_.refs_18_), channel_id=1, source_target_pairs={{0,48},{16,0},{32,16},{48,32},{1,49},{17,1},{33,17},{49,33},{2,50}... | collective-permute-start | bytes 1179656 | tf_op jit(solution)/shard_map/ppermute | solution.py:509
  71.3 0.0 collective-permute-done.4.refs_0_.refs_1_.refs_8_.refs_15_.refs_3_.refs_10_.refs_17_
  71.3 0.0 collective-permute-done.5.refs_1_.refs_6_.refs_13_.refs_20_.refs_8_.refs_15_.refs_22_
  71.3 0.6 touch.4.__
  71.9 8.7 %all-to-all-done.1.same_ref = bf16[8,32,1024]{2,1,0:T(8,128)(2,1)} async-done(((bf16[8,32,1024]{2,1,0:T(8,128)(2,1)}), bf16[8,32,1024]{2,1,0:T(8,128)(2,1)}, u32[]{:S(2)}, u32[]{:S(2)}) %all-to-all-start.1) | async-done | bytes 524320 | tf_op jit(solution)/shard_map/all_to_all | solution.py:551
  80.7 4.6 %collective-permute-start.6 = (bf16[8,32,1024]{2,1,0:T(8,128)(2,1)}, bf16[8,32,1024]{2,1,0:T(8,128)(2,1)S(1)}, u32[]{:S(2)}, u32[]{:S(2)}) collective-permute-start(bf16[8,32,1024]{2,1,0:T(8,128)(2,1)} %all-to-all-done.1.same_ref), channel_id=1, source_target_pairs={{0,1},{1,0},{2,3},{3,2},{4,5},{5,4},{6,7},{7,6},{8,9},{9,8},{10,11... | collective-permute-start | bytes 1572872 | tf_op jit(solution)/shard_map/ppermute | solution.py:509
  85.3 0.0 collective-permute-done.1.refs_0_.refs_3_.refs_10_.refs_17_.refs_5_.refs_12_.refs_19_
  85.3 0.0 collective-permute-done.3.refs_1_.refs_4_.refs_11_.refs_18_.refs_6_.refs_13_.refs_20_
  85.3 0.6 touch.3._
  85.9 1.1 collective-permute-done.6.cross_ref
  87.0 0.0 copy-start.4
  87.0 6.2 %forward.1 = (bf16[3,512,512]{2,1,0:T(8,128)(2,1)}, f32[32,128,128]{2,1,0:T(8,128)}, bf16[16,16,768]{2,1,0:T(8,128)(2,1)}) custom-call(f32[8,128]{1,0:T(8,128)} %touch.3._, f32[8,128]{1,0:T(8,128)} %touch.4.__, s32[1]{0:T(128)} %bitcast.3.side_ref, bf16[8,32,1024]{2,1,0:T(8,128)(2,1)} %all-to-all-done.1.same_ref, ...), custom_call_target="tpu_custom_call" | custom-call | flops 1000 | tf_op jit(solution)/shard_map/forward/pallas_call | solution.py:239
  93.1 3.7 %all-to-all-start.2 = ((bf16[16,16,768]{2,1,0:T(8,128)(2,1)}), bf16[16,16,768]{2,1,0:T(8,128)(2,1)S(1)}, u32[]{:S(2)}, u32[]{:S(2)}) async-start(bf16[16,16,768]{2,1,0:T(8,128)(2,1)} %get-tuple-element.19), calls=%async_computation.2 | async-start | bytes 786432 | tf_op jit(solution)/shard_map/all_to_all | solution.py:554
  96.9 14.6 %all-to-all-done.2.got_ref = bf16[16,16,768]{2,1,0:T(8,128)(2,1)S(1)} async-done(((bf16[16,16,768]{2,1,0:T(8,128)(2,1)}), bf16[16,16,768]{2,1,0:T(8,128)(2,1)S(1)}, u32[]{:S(2)}, u32[]{:S(2)}) %all-to-all-start.2) | async-done | bytes 393248 | tf_op jit(solution)/shard_map/all_to_all | solution.py:554
  111.4 0.0 copy-done.4
  111.4 4.2 %head.1 = (bf16[16,1024]{1,0:T(8,128)(2,1)}, f32[16,1024]{1,0:T(8,128)}, bf16[32,16,256]{2,1,0:T(8,128)(2,1)}) custom-call(s32[1]{0:T(128)} %bitcast.2.at_ref, bf16[16,16,768]{2,1,0:T(8,128)(2,1)S(1)} %all-to-all-done.2.got_ref, bf16[1024,1024]{1,0:T(8,128)(2,1)} %all-gather.2.cloned.1.call-done.out_w_hbm, f32[2,32,1024]{2,1,0:T(8,128)} %bitcast.14, ...), custom_call_target="tpu_custom_call" | custom-call | flops 1000 | tf_op jit(solution)/shard_map/head/pallas_call | solution.py:314
  115.6 4.1 %all-to-all-start.3 = ((bf16[32,16,256]{2,1,0:T(8,128)(2,1)}), bf16[32,16,256]{2,1,0:T(8,128)(2,1)S(1)}, u32[]{:S(2)}, u32[]{:S(2)}) async-start(bf16[32,16,256]{2,1,0:T(8,128)(2,1)} %get-tuple-element.20), calls=%async_computation.3 | async-start | bytes 524288 | tf_op jit(solution)/shard_map/all_to_all | solution.py:558
  119.8 6.9 %backward.1 = (f32[8,32,1024]{2,1,0:T(8,128)}, bf16[8,32,1024]{2,1,0:T(8,128)(2,1)}) custom-call(s32[1]{0:T(128)} %bitcast.3.side_ref, bf16[16,1024]{1,0:T(8,128)(2,1)} %get-tuple-element.21.rows_ref, bf16[3,512,512]{2,1,0:T(8,128)(2,1)} %get-tuple-element.22.refs_0_, f32[32,128,128]{2,1,0:T(8,128)} %get-tuple-element.23.refs_1_, ...), custom_call_target="tpu_custom_call" | custom-call | flops 1000 | tf_op jit(solution)/shard_map/backward/pallas_call | solution.py:394
  126.7 2.0 %collective-permute-start.7 = (bf16[8,32,1024]{2,1,0:T(8,128)(2,1)}, bf16[8,32,1024]{2,1,0:T(8,128)(2,1)S(1)}, u32[]{:S(2)}, u32[]{:S(2)}) collective-permute-start(bf16[8,32,1024]{2,1,0:T(8,128)(2,1)} %get-tuple-element.25), channel_id=1, source_target_pairs={{0,1},{1,0},{2,3},{3,2},{4,5},{5,4},{6,7},{7,6},{8,9},{9,8},{10,11... | collective-permute-start | bytes 1572872 | tf_op jit(solution)/shard_map/ppermute | solution.py:509
  128.8 3.5 %all-to-all-done.3.refs_0_.got_ref = bf16[32,16,256]{2,1,0:T(8,128)(2,1)S(1)} async-done(((bf16[32,16,256]{2,1,0:T(8,128)(2,1)}), bf16[32,16,256]{2,1,0:T(8,128)(2,1)S(1)}, u32[]{:S(2)}, u32[]{:S(2)}) %all-to-all-start.3) | async-done | bytes 262176 | tf_op jit(solution)/shard_map/all_to_all | solution.py:558
  132.3 0.6 touch.5._
  132.9 0.0 collective-permute-done.7.cross_ref
  132.9 0.0 copy-done.2
  132.9 1.4 grads.1
  134.3 4.6 %all-to-all-start.4 = ((bf16[8,32,1280]{2,1,0:T(8,128)(2,1)}), bf16[8,32,1280]{2,1,0:T(8,128)(2,1)S(1)}, u32[]{:S(2)}, u32[]{:S(2)}) async-start(bf16[8,32,1280]{2,1,0:T(8,128)(2,1)} %get-tuple-element.26), calls=%async_computation.4 | async-start | bytes 1310720 | tf_op jit(solution)/shard_map/all_to_all | solution.py:562
  138.9 19.6 %all-to-all-done.4.got_ref = bf16[8,32,1280]{2,1,0:T(8,128)(2,1)S(1)} async-done(((bf16[8,32,1280]{2,1,0:T(8,128)(2,1)}), bf16[8,32,1280]{2,1,0:T(8,128)(2,1)S(1)}, u32[]{:S(2)}, u32[]{:S(2)}) %all-to-all-start.4) | async-done | bytes 655392 | tf_op jit(solution)/shard_map/all_to_all | solution.py:562
  158.5 0.0 copy-done.1
  158.5 0.0 copy-done.3
  158.5 2.1 %last.1 = (bf16[256,1024]{1,0:T(8,128)(2,1)}, f32[2,32,1024]{2,1,0:T(8,128)}) custom-call(s32[1]{0:T(128)} %bitcast.at_ref, s32[1]{0:T(128)} %bitcast.1.turn_ref, bf16[8,32,1280]{2,1,0:T(8,128)(2,1)S(1)} %all-to-all-done.4.got_ref, bf16[256,1024]{1,0:T(8,128)(2,1)S(1)} %bitcast.12, bf16[1,1024]{1,0:T(2,128)(2,1)S(1)} %reshape.40.gain_ref, ...), custom_call_target="tpu_custom_call" | custom-call | tf_op jit(solution)/shard_map/last/pallas_call | solution.py:464
  (5 shorter events, 0.0 us)
Async XLA Ops:
  7.2 45.5 %copy-start.5 = (bf16[1024]{0:T(1024)(128)(2,1)S(1)}, bf16[1024]{0:T(1024)(128)(2,1)}, u32[]{:S(2)}) copy-start(bf16[1024]{0:T(1024)(128)(2,1)} %param.8) | copy-start | bytes 6148
  7.2 46.2 %copy-start = (bf16[1,1,256,1024]{3,2,1,0:T(8,128)(2,1)S(1)}, bf16[1,1,256,1024]{3,2,1,0:T(8,128)(2,1)}, u32[]{:S(2)}) copy-start(bf16[1,1,256,1024]{3,2,1,0:T(8,128)(2,1)} %param.7) | copy-start | bytes 1572868
  9.0 28.7 %all-to-all-start = ((bf16[8,32,1536]{2,1,0:T(8,128)(2,1)}), bf16[8,32,1536]{2,1,0:T(8,128)(2,1)S(1)}, u32[]{:S(2)}, u32[]{:S(2)}) async-start(bf16[8,32,1536]{2,1,0:T(8,128)(2,1)} %share.1), calls=%async_computation | async-start | bytes 1572864 | tf_op jit(solution)/shard_map/all_to_all | solution.py:521
  16.7 94.7 %all-gather.2.cloned.1.call-start = ((), (), s32[]{:S(2)}) async-start(), calls=%async_computation.5 | async-start | bytes 2162688 | tf_op jit(solution)/shard_map/all_gather | solution.py:519
  38.5 26.3 %collective-permute-start = (bf16[4,32,1536]{2,1,0:T(8,128)(2,1)}, bf16[4,32,1536]{2,1,0:T(8,128)(2,1)S(1)}, u32[]{:S(2)}, u32[]{:S(2)}) collective-permute-start(bf16[4,32,1536]{2,1,0:T(8,128)(2,1)} %get-tuple-element.32), channel_id=1, source_target_pairs={{0,16},{16,32},{32,48},{48,0},{1,17},{17,33},{33,49},{49,1},{2,18}... | collective-permute-start | bytes 1179656 | tf_op jit(solution)/shard_map/ppermute | solution.py:509
  44.2 22.6 %collective-permute-start.2 = (bf16[4,32,1536]{2,1,0:T(8,128)(2,1)S(1)}, bf16[4,32,1536]{2,1,0:T(8,128)(2,1)S(1)}, u32[]{:S(2)}, u32[]{:S(2)}) collective-permute-start(bf16[4,32,1536]{2,1,0:T(8,128)(2,1)S(1)} %get-tuple-element.31), channel_id=1, source_target_pairs={{0,48},{16,0},{32,16},{48,32},{1,49},{17,1},{33,17},{49,33},{2,50}... | collective-permute-start | bytes 1179656 | tf_op jit(solution)/shard_map/ppermute | solution.py:509
  47.4 23.9 %collective-permute-start.4 = (bf16[4,32,1536]{2,1,0:T(8,128)(2,1)}, bf16[4,32,1536]{2,1,0:T(8,128)(2,1)S(1)}, u32[]{:S(2)}, u32[]{:S(2)}) collective-permute-start(bf16[4,32,1536]{2,1,0:T(8,128)(2,1)} %get-tuple-element.32), channel_id=1, source_target_pairs={{0,48},{16,0},{32,16},{48,32},{1,49},{17,1},{33,17},{49,33},{2,50}... | collective-permute-start | bytes 1179656 | tf_op jit(solution)/shard_map/ppermute | solution.py:509
  50.7 20.6 %collective-permute-start.5 = (bf16[4,32,1536]{2,1,0:T(8,128)(2,1)S(1)}, bf16[4,32,1536]{2,1,0:T(8,128)(2,1)S(1)}, u32[]{:S(2)}, u32[]{:S(2)}) collective-permute-start(bf16[4,32,1536]{2,1,0:T(8,128)(2,1)S(1)} %get-tuple-element.31), channel_id=1, source_target_pairs={{0,16},{16,32},{32,48},{48,0},{1,17},{17,33},{33,49},{49,1},{2,18}... | collective-permute-start | bytes 1179656 | tf_op jit(solution)/shard_map/ppermute | solution.py:509
  54.6 26.1 %all-to-all-start.1 = ((bf16[8,32,1024]{2,1,0:T(8,128)(2,1)}), bf16[8,32,1024]{2,1,0:T(8,128)(2,1)}, u32[]{:S(2)}, u32[]{:S(2)}) async-start(bf16[8,32,1024]{2,1,0:T(8,128)(2,1)} %bitcast.13), calls=%async_computation.1 | async-start | bytes 1048576 | tf_op jit(solution)/shard_map/all_to_all | solution.py:551
  64.8 20.5 %collective-permute-start.1 = (bf16[4,32,1536]{2,1,0:T(8,128)(2,1)S(1)}, bf16[4,32,1536]{2,1,0:T(8,128)(2,1)S(1)}, u32[]{:S(2)}, u32[]{:S(2)}) collective-permute-start(bf16[4,32,1536]{2,1,0:T(8,128)(2,1)S(1)} %collective-permute-done.refs_5_.refs_12_.refs_19_.refs_7_.refs_14_.refs_21_), channel_id=1, source_target_pairs={{0,16},{16,32},{32,48},{48,0},{1,17},{17,33},{33,49},{49,1},{2,18}... | collective-permute-start | bytes 1179656 | tf_op jit(solution)/shard_map/ppermute | solution.py:509
  66.7 18.5 %collective-permute-start.3 = (bf16[4,32,1536]{2,1,0:T(8,128)(2,1)S(1)}, bf16[4,32,1536]{2,1,0:T(8,128)(2,1)S(1)}, u32[]{:S(2)}, u32[]{:S(2)}) collective-permute-start(bf16[4,32,1536]{2,1,0:T(8,128)(2,1)S(1)} %collective-permute-done.2.refs_2_.refs_9_.refs_16_.refs_4_.refs_11_.refs_18_), channel_id=1, source_target_pairs={{0,48},{16,0},{32,16},{48,32},{1,49},{17,1},{33,17},{49,33},{2,50}... | collective-permute-start | bytes 1179656 | tf_op jit(solution)/shard_map/ppermute | solution.py:509
  80.7 6.3 %collective-permute-start.6 = (bf16[8,32,1024]{2,1,0:T(8,128)(2,1)}, bf16[8,32,1024]{2,1,0:T(8,128)(2,1)S(1)}, u32[]{:S(2)}, u32[]{:S(2)}) collective-permute-start(bf16[8,32,1024]{2,1,0:T(8,128)(2,1)} %all-to-all-done.1.same_ref), channel_id=1, source_target_pairs={{0,1},{1,0},{2,3},{3,2},{4,5},{5,4},{6,7},{7,6},{8,9},{9,8},{10,11... | collective-permute-start | bytes 1572872 | tf_op jit(solution)/shard_map/ppermute | solution.py:509
  87.0 24.4 %copy-start.4 = (f32[8,32]{1,0:T(8,128)S(1)}, f32[8,32]{1,0:T(8,128)}, u32[]{:S(2)}) copy-start(f32[8,32]{1,0:T(8,128)} %book_ref.1) | copy-start | bytes 3076
  93.1 18.3 %all-to-all-start.2 = ((bf16[16,16,768]{2,1,0:T(8,128)(2,1)}), bf16[16,16,768]{2,1,0:T(8,128)(2,1)S(1)}, u32[]{:S(2)}, u32[]{:S(2)}) async-start(bf16[16,16,768]{2,1,0:T(8,128)(2,1)} %get-tuple-element.19), calls=%async_computation.2 | async-start | bytes 786432 | tf_op jit(solution)/shard_map/all_to_all | solution.py:554
  115.6 16.6 %all-to-all-start.3 = ((bf16[32,16,256]{2,1,0:T(8,128)(2,1)}), bf16[32,16,256]{2,1,0:T(8,128)(2,1)S(1)}, u32[]{:S(2)}, u32[]{:S(2)}) async-start(bf16[32,16,256]{2,1,0:T(8,128)(2,1)} %get-tuple-element.20), calls=%async_computation.3 | async-start | bytes 524288 | tf_op jit(solution)/shard_map/all_to_all | solution.py:558
  126.7 6.2 %copy-start.2 = (f32[8,32,1024]{2,1,0:T(8,128)S(1)}, f32[8,32,1024]{2,1,0:T(8,128)}, u32[]{:S(2)}) copy-start(f32[8,32,1024]{2,1,0:T(8,128)} %get-tuple-element.24.keep_ref) | copy-start | bytes 3145732
  126.7 6.1 %collective-permute-start.7 = (bf16[8,32,1024]{2,1,0:T(8,128)(2,1)}, bf16[8,32,1024]{2,1,0:T(8,128)(2,1)S(1)}, u32[]{:S(2)}, u32[]{:S(2)}) collective-permute-start(bf16[8,32,1024]{2,1,0:T(8,128)(2,1)} %get-tuple-element.25), channel_id=1, source_target_pairs={{0,1},{1,0},{2,3},{3,2},{4,5},{5,4},{6,7},{7,6},{8,9},{9,8},{10,11... | collective-permute-start | bytes 1572872 | tf_op jit(solution)/shard_map/ppermute | solution.py:509
  132.9 25.6 %copy-start.1 = (bf16[1,1,256,1024]{3,2,1,0:T(8,128)(2,1)S(1)}, bf16[1,1,256,1024]{3,2,1,0:T(8,128)(2,1)}, u32[]{:S(2)}) copy-start(bf16[1,1,256,1024]{3,2,1,0:T(8,128)(2,1)} %param.7) | copy-start | bytes 1572868
  132.9 25.6 %copy-start.3 = (f32[16,1024]{1,0:T(8,128)S(1)}, f32[16,1024]{1,0:T(8,128)}, u32[]{:S(2)}) copy-start(f32[16,1024]{1,0:T(8,128)} %get-tuple-element.27.mean_ref) | copy-start | bytes 196612
  134.3 24.2 %all-to-all-start.4 = ((bf16[8,32,1280]{2,1,0:T(8,128)(2,1)}), bf16[8,32,1280]{2,1,0:T(8,128)(2,1)S(1)}, u32[]{:S(2)}, u32[]{:S(2)}) async-start(bf16[8,32,1280]{2,1,0:T(8,128)(2,1)} %get-tuple-element.26), calls=%async_computation.4 | async-start | bytes 1310720 | tf_op jit(solution)/shard_map/all_to_all | solution.py:562
Sparse Core Ops, SparseCore 0:
  20.7 84.5 all-gather.1

commit v5 on v4

--- a/solution.py
+++ b/solution.py
@@ -104,7 +104,7 @@
     )(side, *in_hbm(weight))
 
 
-def norm_kernel(code_ref, turn_ref, tokens_ref, gain_ref, _, normed_ref, extra_ref):
+def norm_kernel(code_ref, turn_ref, tokens_ref, gain_ref, normed_ref, extra_ref):
     xf = tokens_ref[...].astype(F32)
     scale = lax.rsqrt(jnp.mean(xf * xf, axis=-1, keepdims=True) + EPS)
     normed = xf * scale * gain_ref[...].astype(F32)
@@ -538,7 +538,6 @@
             SMEM,
             SMEM,
             *[pl.BlockSpec(memory_space=pltpu.VMEM)] * 2,
-            pl.BlockSpec(memory_space=pl.ANY),
         ],
         out_shape=(
             pltpu.HBM((PATCHES, D), BF),
@@ -547,7 +546,7 @@
         compiler_params=params(8),
         cost_estimate=cost(1_000),
         name="norm",
-    )(codes.reshape(1), turn, tokens, gain, near)
+    )(codes.reshape(1), turn, tokens, gain)
     same = lax.all_to_all(normed.reshape(8, 32, D), "tm_0", 0, 0, tiled=True)
     cross = shifted(same, "tm_1", 1)
     qkv, prob, partial = forward(touched(10_000_000_000, first, second), touched(10_000_000_000, after[0], before[1]), side, same, cross, own_w, extra)

time: 169 us -> 175 us (1.036)
  waiting for transfers between devices: 68.4 us -> 75.7 us
    ppermute x8, waiting for transfers between devices: 1.13 us -> 11.9 us  [shifted(): lax.ppermute(value, axis, [(i, (i + by) % count) for i in range(count)])]
    ppermute x8, starting transfers between devices: 27.2 us -> 22.7 us  [shifted(): lax.ppermute(value, axis, [(i, (i + by) % count) for i in range(count)])]
    all_to_all x1, waiting for transfers between devices: 8.73 us -> 5.46 us  [local(): same = lax.all_to_all(normed.reshape(8, 32, D), 'tm_0', 0, 0, tiled=True)]
    all_to_all x1, starting transfers between devices: 10.2 us -> 12.6 us  [local(): same = lax.all_to_all(normed.reshape(8, 32, D), 'tm_0', 0, 0, tiled=True)]
    all_to_all x1, starting transfers between devices: 3.72 us -> 5.79 us  [local(): arrived = lax.all_to_all(partial, TM, 0, 0, tiled=True)]
    all_to_all x1, waiting for transfers between devices: 20.3 us -> 18.4 us  [local(): lax.all_to_all(share(side.reshape(1), w_qkv, far), 'dp_0', 0, 0, tiled=True)]
  transfers between devices with their start and end apart: 14 -> 14, of which waited for: 6 -> 7; matrix products, arithmetic and copies ran while one was open for 0% -> 0% of each run, Pallas kernels for 10% -> 9%
where the time goes in v5:
time: 175 us; the launch traced here: 174 us
  waiting for transfers between devices  75.7 us (43%)
  starting transfers between devices  57.2 us (33%)
  Pallas kernels  25.7 us (15%)
  between operations  14.9 us (9%)
    ppermute x8, starting transfers between devices, shifted(): lax.ppermute(value, axis, [(i, (i + by) % count) for i in range(count)])  22.7 us
    all_to_all x1, waiting for transfers between devices, local(): back = lax.all_to_all(outgoing, 'tm_0', 0, 0, tiled=True)  20.7 us
    all_to_all x1, waiting for transfers between devices, local(): lax.all_to_all(share(side.reshape(1), w_qkv, far), 'dp_0', 0, 0, tiled=True)  18.4 us
    all_to_all x1, waiting for transfers between devices, local(): arrived = lax.all_to_all(partial, TM, 0, 0, tiled=True)  14.6 us
    all_to_all x1, starting transfers between devices, local(): same = lax.all_to_all(normed.reshape(8, 32, D), 'tm_0', 0, 0, tiled=True)  12.6 us
    ppermute x8, waiting for transfers between devices, shifted(): lax.ppermute(value, axis, [(i, (i + by) % count) for i in range(count)])  11.9 us
    all_to_all x1, starting transfers between devices, local(): lax.all_to_all(share(side.reshape(1), w_qkv, far), 'dp_0', 0, 0, tiled=True)  7.66 us
    pallas_call x1, Pallas kernels, backward(): pl.pallas_call(backward_kernel, grid=(2,), in_specs=[SMEM, whole((FRAMES,...  6.93 us
  transfers between devices with their start and end apart: 14, of which 7 were waited for; matrix products, arithmetic and copies ran while one was open for 0% of the time, Pallas kernels for 9%

profile of v5, /device:TPU:1, one launch (start us, length us, event | category | flops | bytes accessed | tf_op | source)
XLA Modules:
  0.0 174.3 jit_solution(5230637062134995135)
XLA Ops:
  7.2 0.0 copy-start.5
  7.2 0.0 copy-start
  7.2 1.8 %share.1 = bf16[8,32,1536]{2,1,0:T(8,128)(2,1)} custom-call(s32[1]{0:T(128)} %bitcast.3.side_ref, bf16[32,3072]{1,0:T(8,128)(2,1)} %weight_ref.1), custom_call_target="tpu_custom_call" | custom-call | tf_op jit(solution)/shard_map/share/pallas_call | solution.py:93
  9.0 7.7 %all-to-all-start = ((bf16[8,32,1536]{2,1,0:T(8,128)(2,1)}), bf16[8,32,1536]{2,1,0:T(8,128)(2,1)S(1)}, u32[]{:S(2)}, u32[]{:S(2)}) async-start(bf16[8,32,1536]{2,1,0:T(8,128)(2,1)} %share.1), calls=%async_computation | async-start | bytes 1572864 | tf_op jit(solution)/shard_map/all_to_all | solution.py:521
  16.7 0.0 all-gather.2.cloned.1.call-start
  16.7 0.7 all-gather.2.cloned.1.call-update
  17.4 0.0 copy-done.5
  18.1 0.0 copy-done
  18.1 1.2 norm.1
  19.3 18.4 %all-to-all-done.refs_0_.refs_7_.refs_14_.refs_2_.refs_9_.refs_16_ = bf16[8,32,1536]{2,1,0:T(8,128)(2,1)S(1)} async-done(((bf16[8,32,1536]{2,1,0:T(8,128)(2,1)}), bf16[8,32,1536]{2,1,0:T(8,128)(2,1)S(1)}, u32[]{:S(2)}, u32[]{:S(2)}) %all-to-all-start) | async-done | bytes 786464 | tf_op jit(solution)/shard_map/all_to_all | solution.py:521
  37.7 12.6 %all-to-all-start.1 = ((bf16[8,32,1024]{2,1,0:T(8,128)(2,1)}), bf16[8,32,1024]{2,1,0:T(8,128)(2,1)}, u32[]{:S(2)}, u32[]{:S(2)}) async-start(bf16[8,32,1024]{2,1,0:T(8,128)(2,1)} %bitcast.13), calls=%async_computation.1 | async-start | bytes 1048576 | tf_op jit(solution)/shard_map/all_to_all | solution.py:550
  50.3 0.8 fusion
  51.1 3.1 %collective-permute-start = (bf16[4,32,1536]{2,1,0:T(8,128)(2,1)}, bf16[4,32,1536]{2,1,0:T(8,128)(2,1)S(1)}, u32[]{:S(2)}, u32[]{:S(2)}) collective-permute-start(bf16[4,32,1536]{2,1,0:T(8,128)(2,1)} %get-tuple-element.32), channel_id=1, source_target_pairs={{0,16},{16,32},{32,48},{48,0},{1,17},{17,33},{33,49},{49,1},{2,18}... | collective-permute-start | bytes 1179656 | tf_op jit(solution)/shard_map/ppermute | solution.py:509
  54.2 3.4 %collective-permute-start.2 = (bf16[4,32,1536]{2,1,0:T(8,128)(2,1)S(1)}, bf16[4,32,1536]{2,1,0:T(8,128)(2,1)S(1)}, u32[]{:S(2)}, u32[]{:S(2)}) collective-permute-start(bf16[4,32,1536]{2,1,0:T(8,128)(2,1)S(1)} %get-tuple-element.31), channel_id=1, source_target_pairs={{0,48},{16,0},{32,16},{48,32},{1,49},{17,1},{33,17},{49,33},{2,50}... | collective-permute-start | bytes 1179656 | tf_op jit(solution)/shard_map/ppermute | solution.py:509
  57.6 3.2 %collective-permute-start.4 = (bf16[4,32,1536]{2,1,0:T(8,128)(2,1)}, bf16[4,32,1536]{2,1,0:T(8,128)(2,1)S(1)}, u32[]{:S(2)}, u32[]{:S(2)}) collective-permute-start(bf16[4,32,1536]{2,1,0:T(8,128)(2,1)} %get-tuple-element.32), channel_id=1, source_target_pairs={{0,48},{16,0},{32,16},{48,32},{1,49},{17,1},{33,17},{49,33},{2,50}... | collective-permute-start | bytes 1179656 | tf_op jit(solution)/shard_map/ppermute | solution.py:509
  60.8 2.1 %collective-permute-start.5 = (bf16[4,32,1536]{2,1,0:T(8,128)(2,1)S(1)}, bf16[4,32,1536]{2,1,0:T(8,128)(2,1)S(1)}, u32[]{:S(2)}, u32[]{:S(2)}) collective-permute-start(bf16[4,32,1536]{2,1,0:T(8,128)(2,1)S(1)} %get-tuple-element.31), channel_id=1, source_target_pairs={{0,16},{16,32},{32,48},{48,0},{1,17},{17,33},{33,49},{49,1},{2,18}... | collective-permute-start | bytes 1179656 | tf_op jit(solution)/shard_map/ppermute | solution.py:509
  62.9 5.5 %all-to-all-done.1.same_ref = bf16[8,32,1024]{2,1,0:T(8,128)(2,1)} async-done(((bf16[8,32,1024]{2,1,0:T(8,128)(2,1)}), bf16[8,32,1024]{2,1,0:T(8,128)(2,1)}, u32[]{:S(2)}, u32[]{:S(2)}) %all-to-all-start.1) | async-done | bytes 524320 | tf_op jit(solution)/shard_map/all_to_all | solution.py:550
  68.4 2.4 %collective-permute-start.6 = (bf16[8,32,1024]{2,1,0:T(8,128)(2,1)}, bf16[8,32,1024]{2,1,0:T(8,128)(2,1)S(1)}, u32[]{:S(2)}, u32[]{:S(2)}) collective-permute-start(bf16[8,32,1024]{2,1,0:T(8,128)(2,1)} %all-to-all-done.1.same_ref), channel_id=1, source_target_pairs={{0,1},{1,0},{2,3},{3,2},{4,5},{5,4},{6,7},{7,6},{8,9},{9,8},{10,11... | collective-permute-start | bytes 1572872 | tf_op jit(solution)/shard_map/ppermute | solution.py:509
  70.8 0.0 collective-permute-done.refs_5_.refs_12_.refs_19_.refs_7_.refs_14_.refs_21_
  70.8 3.1 %collective-permute-start.1 = (bf16[4,32,1536]{2,1,0:T(8,128)(2,1)S(1)}, bf16[4,32,1536]{2,1,0:T(8,128)(2,1)S(1)}, u32[]{:S(2)}, u32[]{:S(2)}) collective-permute-start(bf16[4,32,1536]{2,1,0:T(8,128)(2,1)S(1)} %collective-permute-done.refs_5_.refs_12_.refs_19_.refs_7_.refs_14_.refs_21_), channel_id=1, source_target_pairs={{0,16},{16,32},{32,48},{48,0},{1,17},{17,33},{33,49},{49,1},{2,18}... | collective-permute-start | bytes 1179656 | tf_op jit(solution)/shard_map/ppermute | solution.py:509
  73.9 0.0 collective-permute-done.2.refs_2_.refs_9_.refs_16_.refs_4_.refs_11_.refs_18_
  73.9 3.4 %collective-permute-start.3 = (bf16[4,32,1536]{2,1,0:T(8,128)(2,1)S(1)}, bf16[4,32,1536]{2,1,0:T(8,128)(2,1)S(1)}, u32[]{:S(2)}, u32[]{:S(2)}) collective-permute-start(bf16[4,32,1536]{2,1,0:T(8,128)(2,1)S(1)} %collective-permute-done.2.refs_2_.refs_9_.refs_16_.refs_4_.refs_11_.refs_18_), channel_id=1, source_target_pairs={{0,48},{16,0},{32,16},{48,32},{1,49},{17,1},{33,17},{49,33},{2,50}... | collective-permute-start | bytes 1179656 | tf_op jit(solution)/shard_map/ppermute | solution.py:509
  77.3 0.0 collective-permute-done.4.refs_0_.refs_1_.refs_8_.refs_15_.refs_3_.refs_10_.refs_17_
  77.3 0.0 collective-permute-done.5.refs_1_.refs_6_.refs_13_.refs_20_.refs_8_.refs_15_.refs_22_
  77.3 0.6 touch.4.__
  77.9 7.5 %collective-permute-done.1.refs_0_.refs_3_.refs_10_.refs_17_.refs_5_.refs_12_.refs_19_ = bf16[4,32,1536]{2,1,0:T(8,128)(2,1)S(1)} collective-permute-done((bf16[4,32,1536]{2,1,0:T(8,128)(2,1)S(1)}, bf16[4,32,1536]{2,1,0:T(8,128)(2,1)S(1)}, u32[]{:S(2)}, u32[]{:S(2)}) %collective-permute-start.1) | collective-permute-done | bytes 393248 | tf_op jit(solution)/shard_map/ppermute | solution.py:509
  85.4 4.4 %collective-permute-done.3.refs_1_.refs_4_.refs_11_.refs_18_.refs_6_.refs_13_.refs_20_ = bf16[4,32,1536]{2,1,0:T(8,128)(2,1)S(1)} collective-permute-done((bf16[4,32,1536]{2,1,0:T(8,128)(2,1)S(1)}, bf16[4,32,1536]{2,1,0:T(8,128)(2,1)S(1)}, u32[]{:S(2)}, u32[]{:S(2)}) %collective-permute-start.3) | collective-permute-done | bytes 393248 | tf_op jit(solution)/shard_map/ppermute | solution.py:509
  89.8 0.6 touch.3._
  90.4 0.0 collective-permute-done.6.cross_ref
  90.4 0.0 copy-start.4
  90.4 6.2 %forward.1 = (bf16[3,512,512]{2,1,0:T(8,128)(2,1)}, f32[32,128,128]{2,1,0:T(8,128)}, bf16[16,16,768]{2,1,0:T(8,128)(2,1)}) custom-call(f32[8,128]{1,0:T(8,128)} %touch.3._, f32[8,128]{1,0:T(8,128)} %touch.4.__, s32[1]{0:T(128)} %bitcast.3.side_ref, bf16[8,32,1024]{2,1,0:T(8,128)(2,1)} %all-to-all-done.1.same_ref, ...), custom_call_target="tpu_custom_call" | custom-call | flops 1000 | tf_op jit(solution)/shard_map/forward/pallas_call | solution.py:239
  96.6 5.8 %all-to-all-start.2 = ((bf16[16,16,768]{2,1,0:T(8,128)(2,1)}), bf16[16,16,768]{2,1,0:T(8,128)(2,1)S(1)}, u32[]{:S(2)}, u32[]{:S(2)}) async-start(bf16[16,16,768]{2,1,0:T(8,128)(2,1)} %get-tuple-element.19), calls=%async_computation.2 | async-start | bytes 786432 | tf_op jit(solution)/shard_map/all_to_all | solution.py:553
  102.4 14.6 %all-to-all-done.2.got_ref = bf16[16,16,768]{2,1,0:T(8,128)(2,1)S(1)} async-done(((bf16[16,16,768]{2,1,0:T(8,128)(2,1)}), bf16[16,16,768]{2,1,0:T(8,128)(2,1)S(1)}, u32[]{:S(2)}, u32[]{:S(2)}) %all-to-all-start.2) | async-done | bytes 393248 | tf_op jit(solution)/shard_map/all_to_all | solution.py:553
  117.0 0.0 copy-done.4
  117.0 4.2 %head.1 = (bf16[16,1024]{1,0:T(8,128)(2,1)}, f32[16,1024]{1,0:T(8,128)}, bf16[32,16,256]{2,1,0:T(8,128)(2,1)}) custom-call(s32[1]{0:T(128)} %bitcast.2.at_ref, bf16[16,16,768]{2,1,0:T(8,128)(2,1)S(1)} %all-to-all-done.2.got_ref, bf16[1024,1024]{1,0:T(8,128)(2,1)} %all-gather.2.cloned.1.call-done.out_w_hbm, f32[2,32,1024]{2,1,0:T(8,128)} %bitcast.14, ...), custom_call_target="tpu_custom_call" | custom-call | flops 1000 | tf_op jit(solution)/shard_map/head/pallas_call | solution.py:314
  121.2 4.9 %all-to-all-start.3 = ((bf16[32,16,256]{2,1,0:T(8,128)(2,1)}), bf16[32,16,256]{2,1,0:T(8,128)(2,1)S(1)}, u32[]{:S(2)}, u32[]{:S(2)}) async-start(bf16[32,16,256]{2,1,0:T(8,128)(2,1)} %get-tuple-element.20), calls=%async_computation.3 | async-start | bytes 524288 | tf_op jit(solution)/shard_map/all_to_all | solution.py:557
  126.1 6.9 %backward.1 = (f32[8,32,1024]{2,1,0:T(8,128)}, bf16[8,32,1024]{2,1,0:T(8,128)(2,1)}) custom-call(s32[1]{0:T(128)} %bitcast.3.side_ref, bf16[16,1024]{1,0:T(8,128)(2,1)} %get-tuple-element.21.rows_ref, bf16[3,512,512]{2,1,0:T(8,128)(2,1)} %get-tuple-element.22.refs_0_, f32[32,128,128]{2,1,0:T(8,128)} %get-tuple-element.23.refs_1_, ...), custom_call_target="tpu_custom_call" | custom-call | flops 1000 | tf_op jit(solution)/shard_map/backward/pallas_call | solution.py:394
  133.0 2.0 %collective-permute-start.7 = (bf16[8,32,1024]{2,1,0:T(8,128)(2,1)}, bf16[8,32,1024]{2,1,0:T(8,128)(2,1)S(1)}, u32[]{:S(2)}, u32[]{:S(2)}) collective-permute-start(bf16[8,32,1024]{2,1,0:T(8,128)(2,1)} %get-tuple-element.25), channel_id=1, source_target_pairs={{0,1},{1,0},{2,3},{3,2},{4,5},{5,4},{6,7},{7,6},{8,9},{9,8},{10,11... | collective-permute-start | bytes 1572872 | tf_op jit(solution)/shard_map/ppermute | solution.py:509
  135.1 3.9 %all-to-all-done.3.refs_0_.got_ref = bf16[32,16,256]{2,1,0:T(8,128)(2,1)S(1)} async-done(((bf16[32,16,256]{2,1,0:T(8,128)(2,1)}), bf16[32,16,256]{2,1,0:T(8,128)(2,1)S(1)}, u32[]{:S(2)}, u32[]{:S(2)}) %all-to-all-start.3) | async-done | bytes 262176 | tf_op jit(solution)/shard_map/all_to_all | solution.py:557
  139.0 0.6 touch.5._
  139.6 0.0 collective-permute-done.7.cross_ref
  139.6 0.0 copy-done.2
  139.6 1.4 grads.1
  141.1 3.5 %all-to-all-start.4 = ((bf16[8,32,1280]{2,1,0:T(8,128)(2,1)}), bf16[8,32,1280]{2,1,0:T(8,128)(2,1)S(1)}, u32[]{:S(2)}, u32[]{:S(2)}) async-start(bf16[8,32,1280]{2,1,0:T(8,128)(2,1)} %get-tuple-element.26), calls=%async_computation.4 | async-start | bytes 1310720 | tf_op jit(solution)/shard_map/all_to_all | solution.py:561
  144.6 20.7 %all-to-all-done.4.got_ref = bf16[8,32,1280]{2,1,0:T(8,128)(2,1)S(1)} async-done(((bf16[8,32,1280]{2,1,0:T(8,128)(2,1)}), bf16[8,32,1280]{2,1,0:T(8,128)(2,1)S(1)}, u32[]{:S(2)}, u32[]{:S(2)}) %all-to-all-start.4) | async-done | bytes 655392 | tf_op jit(solution)/shard_map/all_to_all | solution.py:561
  165.3 0.0 copy-done.1
  165.3 0.0 copy-done.3
  165.3 2.1 %last.1 = (bf16[256,1024]{1,0:T(8,128)(2,1)}, f32[2,32,1024]{2,1,0:T(8,128)}) custom-call(s32[1]{0:T(128)} %bitcast.at_ref, s32[1]{0:T(128)} %bitcast.1.turn_ref, bf16[8,32,1280]{2,1,0:T(8,128)(2,1)S(1)} %all-to-all-done.4.got_ref, bf16[256,1024]{1,0:T(8,128)(2,1)S(1)} %bitcast.12, bf16[1,1024]{1,0:T(2,128)(2,1)S(1)} %reshape.40.gain_ref, ...), custom_call_target="tpu_custom_call" | custom-call | tf_op jit(solution)/shard_map/last/pallas_call | solution.py:464
  (5 shorter events, 0.0 us)
Async XLA Ops:
  7.2 10.3 %copy-start.5 = (bf16[1024]{0:T(1024)(128)(2,1)S(1)}, bf16[1024]{0:T(1024)(128)(2,1)}, u32[]{:S(2)}) copy-start(bf16[1024]{0:T(1024)(128)(2,1)} %param.8) | copy-start | bytes 6148
  7.2 10.9 %copy-start = (bf16[1,1,256,1024]{3,2,1,0:T(8,128)(2,1)S(1)}, bf16[1,1,256,1024]{3,2,1,0:T(8,128)(2,1)}, u32[]{:S(2)}) copy-start(bf16[1,1,256,1024]{3,2,1,0:T(8,128)(2,1)} %param.7) | copy-start | bytes 1572868
  9.0 28.7 %all-to-all-start = ((bf16[8,32,1536]{2,1,0:T(8,128)(2,1)}), bf16[8,32,1536]{2,1,0:T(8,128)(2,1)S(1)}, u32[]{:S(2)}, u32[]{:S(2)}) async-start(bf16[8,32,1536]{2,1,0:T(8,128)(2,1)} %share.1), calls=%async_computation | async-start | bytes 1572864 | tf_op jit(solution)/shard_map/all_to_all | solution.py:521
  16.7 100.3 %all-gather.2.cloned.1.call-start = ((), (), s32[]{:S(2)}) async-start(), calls=%async_computation.5 | async-start | bytes 2162688 | tf_op jit(solution)/shard_map/all_gather | solution.py:519
  37.7 30.7 %all-to-all-start.1 = ((bf16[8,32,1024]{2,1,0:T(8,128)(2,1)}), bf16[8,32,1024]{2,1,0:T(8,128)(2,1)}, u32[]{:S(2)}, u32[]{:S(2)}) async-start(bf16[8,32,1024]{2,1,0:T(8,128)(2,1)} %bitcast.13), calls=%async_computation.1 | async-start | bytes 1048576 | tf_op jit(solution)/shard_map/all_to_all | solution.py:550
  51.1 19.7 %collective-permute-start = (bf16[4,32,1536]{2,1,0:T(8,128)(2,1)}, bf16[4,32,1536]{2,1,0:T(8,128)(2,1)S(1)}, u32[]{:S(2)}, u32[]{:S(2)}) collective-permute-start(bf16[4,32,1536]{2,1,0:T(8,128)(2,1)} %get-tuple-element.32), channel_id=1, source_target_pairs={{0,16},{16,32},{32,48},{48,0},{1,17},{17,33},{33,49},{49,1},{2,18}... | collective-permute-start | bytes 1179656 | tf_op jit(solution)/shard_map/ppermute | solution.py:509
  54.2 19.7 %collective-permute-start.2 = (bf16[4,32,1536]{2,1,0:T(8,128)(2,1)S(1)}, bf16[4,32,1536]{2,1,0:T(8,128)(2,1)S(1)}, u32[]{:S(2)}, u32[]{:S(2)}) collective-permute-start(bf16[4,32,1536]{2,1,0:T(8,128)(2,1)S(1)} %get-tuple-element.31), channel_id=1, source_target_pairs={{0,48},{16,0},{32,16},{48,32},{1,49},{17,1},{33,17},{49,33},{2,50}... | collective-permute-start | bytes 1179656 | tf_op jit(solution)/shard_map/ppermute | solution.py:509
  57.6 19.7 %collective-permute-start.4 = (bf16[4,32,1536]{2,1,0:T(8,128)(2,1)}, bf16[4,32,1536]{2,1,0:T(8,128)(2,1)S(1)}, u32[]{:S(2)}, u32[]{:S(2)}) collective-permute-start(bf16[4,32,1536]{2,1,0:T(8,128)(2,1)} %get-tuple-element.32), channel_id=1, source_target_pairs={{0,48},{16,0},{32,16},{48,32},{1,49},{17,1},{33,17},{49,33},{2,50}... | collective-permute-start | bytes 1179656 | tf_op jit(solution)/shard_map/ppermute | solution.py:509
  60.8 16.5 %collective-permute-start.5 = (bf16[4,32,1536]{2,1,0:T(8,128)(2,1)S(1)}, bf16[4,32,1536]{2,1,0:T(8,128)(2,1)S(1)}, u32[]{:S(2)}, u32[]{:S(2)}) collective-permute-start(bf16[4,32,1536]{2,1,0:T(8,128)(2,1)S(1)} %get-tuple-element.31), channel_id=1, source_target_pairs={{0,16},{16,32},{32,48},{48,0},{1,17},{17,33},{33,49},{49,1},{2,18}... | collective-permute-start | bytes 1179656 | tf_op jit(solution)/shard_map/ppermute | solution.py:509
  68.4 22.1 %collective-permute-start.6 = (bf16[8,32,1024]{2,1,0:T(8,128)(2,1)}, bf16[8,32,1024]{2,1,0:T(8,128)(2,1)S(1)}, u32[]{:S(2)}, u32[]{:S(2)}) collective-permute-start(bf16[8,32,1024]{2,1,0:T(8,128)(2,1)} %all-to-all-done.1.same_ref), channel_id=1, source_target_pairs={{0,1},{1,0},{2,3},{3,2},{4,5},{5,4},{6,7},{7,6},{8,9},{9,8},{10,11... | collective-permute-start | bytes 1572872 | tf_op jit(solution)/shard_map/ppermute | solution.py:509
  70.8 14.6 %collective-permute-start.1 = (bf16[4,32,1536]{2,1,0:T(8,128)(2,1)S(1)}, bf16[4,32,1536]{2,1,0:T(8,128)(2,1)S(1)}, u32[]{:S(2)}, u32[]{:S(2)}) collective-permute-start(bf16[4,32,1536]{2,1,0:T(8,128)(2,1)S(1)} %collective-permute-done.refs_5_.refs_12_.refs_19_.refs_7_.refs_14_.refs_21_), channel_id=1, source_target_pairs={{0,16},{16,32},{32,48},{48,0},{1,17},{17,33},{33,49},{49,1},{2,18}... | collective-permute-start | bytes 1179656 | tf_op jit(solution)/shard_map/ppermute | solution.py:509
  73.9 15.9 %collective-permute-start.3 = (bf16[4,32,1536]{2,1,0:T(8,128)(2,1)S(1)}, bf16[4,32,1536]{2,1,0:T(8,128)(2,1)S(1)}, u32[]{:S(2)}, u32[]{:S(2)}) collective-permute-start(bf16[4,32,1536]{2,1,0:T(8,128)(2,1)S(1)} %collective-permute-done.2.refs_2_.refs_9_.refs_16_.refs_4_.refs_11_.refs_18_), channel_id=1, source_target_pairs={{0,48},{16,0},{32,16},{48,32},{1,49},{17,1},{33,17},{49,33},{2,50}... | collective-permute-start | bytes 1179656 | tf_op jit(solution)/shard_map/ppermute | solution.py:509
  90.4 26.5 %copy-start.4 = (f32[8,32]{1,0:T(8,128)S(1)}, f32[8,32]{1,0:T(8,128)}, u32[]{:S(2)}) copy-start(f32[8,32]{1,0:T(8,128)} %book_ref.1) | copy-start | bytes 3076
  96.6 20.3 %all-to-all-start.2 = ((bf16[16,16,768]{2,1,0:T(8,128)(2,1)}), bf16[16,16,768]{2,1,0:T(8,128)(2,1)S(1)}, u32[]{:S(2)}, u32[]{:S(2)}) async-start(bf16[16,16,768]{2,1,0:T(8,128)(2,1)} %get-tuple-element.19), calls=%async_computation.2 | async-start | bytes 786432 | tf_op jit(solution)/shard_map/all_to_all | solution.py:553
  121.2 17.9 %all-to-all-start.3 = ((bf16[32,16,256]{2,1,0:T(8,128)(2,1)}), bf16[32,16,256]{2,1,0:T(8,128)(2,1)S(1)}, u32[]{:S(2)}, u32[]{:S(2)}) async-start(bf16[32,16,256]{2,1,0:T(8,128)(2,1)} %get-tuple-element.20), calls=%async_computation.3 | async-start | bytes 524288 | tf_op jit(solution)/shard_map/all_to_all | solution.py:557
  133.0 6.6 %copy-start.2 = (f32[8,32,1024]{2,1,0:T(8,128)S(1)}, f32[8,32,1024]{2,1,0:T(8,128)}, u32[]{:S(2)}) copy-start(f32[8,32,1024]{2,1,0:T(8,128)} %get-tuple-element.24.keep_ref) | copy-start | bytes 3145732
  133.0 6.6 %collective-permute-start.7 = (bf16[8,32,1024]{2,1,0:T(8,128)(2,1)}, bf16[8,32,1024]{2,1,0:T(8,128)(2,1)S(1)}, u32[]{:S(2)}, u32[]{:S(2)}) collective-permute-start(bf16[8,32,1024]{2,1,0:T(8,128)(2,1)} %get-tuple-element.25), channel_id=1, source_target_pairs={{0,1},{1,0},{2,3},{3,2},{4,5},{5,4},{6,7},{7,6},{8,9},{9,8},{10,11... | collective-permute-start | bytes 1572872 | tf_op jit(solution)/shard_map/ppermute | solution.py:509
  139.6 25.7 %copy-start.1 = (bf16[1,1,256,1024]{3,2,1,0:T(8,128)(2,1)S(1)}, bf16[1,1,256,1024]{3,2,1,0:T(8,128)(2,1)}, u32[]{:S(2)}) copy-start(bf16[1,1,256,1024]{3,2,1,0:T(8,128)(2,1)} %param.7) | copy-start | bytes 1572868
  139.6 25.7 %copy-start.3 = (f32[16,1024]{1,0:T(8,128)S(1)}, f32[16,1024]{1,0:T(8,128)}, u32[]{:S(2)}) copy-start(f32[16,1024]{1,0:T(8,128)} %get-tuple-element.27.mean_ref) | copy-start | bytes 196612
  141.1 24.2 %all-to-all-start.4 = ((bf16[8,32,1280]{2,1,0:T(8,128)(2,1)}), bf16[8,32,1280]{2,1,0:T(8,128)(2,1)S(1)}, u32[]{:S(2)}, u32[]{:S(2)}) async-start(bf16[8,32,1280]{2,1,0:T(8,128)(2,1)} %get-tuple-element.26), calls=%async_computation.4 | async-start | bytes 1310720 | tf_op jit(solution)/shard_map/all_to_all | solution.py:561
Sparse Core Ops, SparseCore 0:
  20.7 84.5 all-gather.1
